TPU v7x, 512 devices: a whole 4x8x8 slice. The times are simulated.
512 devices in a mesh: fsdp: 32 (over z, y_hi), tensor: 16 (over x, y_lo, core).
Axes of the slice: x: 4, y: 8 (y_hi: 4, y_lo: 2; y = y_hi * 2 + y_lo), z: 8, core: 2. Of those that a mesh axis runs over, the one named last changes fastest.
Arguments:
- old_codes: bfloat16 [26624, 16384], P(('fsdp', 'tensor')), may hold values from -1 to 1
- old_scales: float32 [208, 128], replicated, may hold values from 0.003 to 0.03
- gate_pre: bfloat16 [2048, 26624], P('fsdp', 'tensor'), may hold values from -6 to 6
- up_pre: bfloat16 [2048, 26624], P('fsdp', 'tensor'), may hold values from -6 to 6
Outputs:
- mixed: bfloat16 [2048, 16384], P('tensor', 'fsdp')
- codes_t: bfloat16 [16384, 26624], P('fsdp', 'tensor')
- scales_t: float32 [128, 208], P('fsdp', 'tensor')
All inputs are finite; a program needn't handle non-finite values. Where the computation divides by a largest or mean magnitude, that divisor is 1e-20 or more.
Results may differ from a plain program's by a relative error of at most 0.024.
Values may be sent and summed in bfloat16 or wider, within the bound.
No kernel may reach another device: no remote copies, remote signals or barrier semaphores. Data moves between devices by JAX's collectives and lax.ppermute only.
A program may use at most 64 MiB of HBM per device.

v0:
```python
import jax
import jax.numpy as jnp
from jax import lax
from jax.sharding import PartitionSpec as P

TILE = 128


epsilon = 1e-06


def regroup(moved, senders, per_owner, block_rows, col_width):
    stacked = moved.reshape(senders, per_owner, block_rows, col_width)
    return jnp.swapaxes(stacked, 0, 1).reshape(senders * per_owner * block_rows, col_width)


def body(old_codes, old_scales, gate_pre, up_pre):
    n_fsdp = lax.axis_size("fsdp")
    n_tensor = lax.axis_size("tensor")
    f_index = lax.axis_index("fsdp")
    t_index = lax.axis_index("tensor")
    block_rows, full_width = old_codes.shape
    col_width = full_width // n_fsdp
    col_tiles = col_width // TILE
    per_owner = n_fsdp // n_tensor
    own_rows = block_rows * n_fsdp
    row_tiles = own_rows // TILE
    hidden = (jax.nn.silu(gate_pre.astype(jnp.float32)) * up_pre.astype(jnp.float32)).astype(
        jnp.bfloat16
    )
    sectioned = lax.all_to_all(old_codes, "fsdp", split_axis=1, concat_axis=0, tiled=True)
    scale_cols = lax.dynamic_slice_in_dim(old_scales, f_index * col_tiles, col_tiles, 1)
    moved = lax.all_to_all(
        sectioned.reshape(n_tensor, per_owner * block_rows, col_width),
        "tensor",
        split_axis=0,
        concat_axis=0,
        tiled=True,
    )
    final_rows = regroup(moved, n_tensor, per_owner, block_rows, col_width)
    scale_block = lax.dynamic_slice_in_dim(scale_cols, t_index * row_tiles, row_tiles, 0)
    tile_values = (
        final_rows.astype(jnp.float32).reshape(row_tiles, TILE, col_tiles, TILE)
        * scale_block[:, None, :, None]
    )
    new_scale = jnp.max(jnp.abs(tile_values), axis=(1, 3)) + epsilon
    new_codes = (tile_values / new_scale[:, None, :, None]).astype(jnp.bfloat16)
    weight = (
        (new_codes.astype(jnp.float32) * new_scale[:, None, :, None])
        .astype(jnp.bfloat16)
        .reshape(own_rows, col_width)
    )
    partial_value = jnp.dot(
        lax.all_gather(hidden, "fsdp", axis=0, tiled=True),
        weight,
        preferred_element_type=jnp.float32,
    )
    codes_t = new_codes.reshape(own_rows, col_width).T
    scales_t = new_scale.T
    mixed = lax.psum_scatter(
        partial_value.astype(jnp.bfloat16), "tensor", scatter_dimension=0, tiled=True
    )
    return (mixed, codes_t, scales_t)


def solution(mesh):
    return jax.shard_map(
        body,
        mesh=mesh,
        in_specs=(P(("fsdp", "tensor"), None), P(), P("fsdp", "tensor"), P("fsdp", "tensor")),
        out_specs=(P("tensor", "fsdp"), P("fsdp", "tensor"), P("fsdp", "tensor")),
        check_vma=False,
    )
```

profile of v0, /device:TPU:1, one launch (start us, length us, event | category | flops | bytes accessed | tf_op | source)
XLA Modules:
  0.0 262.1 jit_solution(17682116257781332109)
XLA Ops:
  7.2 0.0 all-gather.2.cloned.1.call-start
  7.2 1.8 fusion.7
  9.1 0.0 all-gather.2.cloned.1.call-update
  9.1 2.2 copy.20
  11.2 0.2 slice
  11.4 0.9 copy.14
  12.4 76.7 %all_to_all.21 = bf16[52,32,512]{2,0,1:T(8,128)(2,1)S(1)} all-to-all(bf16[52,32,512]{2,0,1:T(8,128)(2,1)S(1)} %copy.14), channel_id=1, replica_groups=mesh['fsdp'=32,'tensor'=16] {'fsdp'}, dimensions={1} | all-to-all | bytes 3407872 | tf_op jit(solution)/shard_map/all_to_all | solution.py:31
  89.1 1.3 reshape.38
  90.4 6.3 %all-to-all-start.1 = ((bf16[16,104,512]{2,1,0:T(8,128)(2,1)}), bf16[16,104,512]{2,1,0:T(8,128)(2,1)S(1)}, u32[]{:S(2)}, u32[]{:S(2)}) async-start(bf16[16,104,512]{2,1,0:T(8,128)(2,1)} %reshape.38), calls=%async_computation.1 | async-start | bytes 3407872 | tf_op jit(solution)/shard_map/all_to_all | solution.py:33
  96.8 0.2 reduce-scatter.2.cloned.1.call-start
  97.0 0.8 dynamic_slice.4
  97.8 36.6 %all-to-all-done.1 = bf16[16,104,512]{2,1,0:T(8,128)(2,1)S(1)} async-done(((bf16[16,104,512]{2,1,0:T(8,128)(2,1)}), bf16[16,104,512]{2,1,0:T(8,128)(2,1)S(1)}, u32[]{:S(2)}, u32[]{:S(2)}) %all-to-all-start.1) | async-done | bytes 1703968 | tf_op jit(solution)/shard_map/all_to_all | solution.py:33
  134.4 0.6 copy.15
  134.9 3.8 %copy.16 = f32[2,16,52,512]{3,2,1,0:T(8,128)} copy(f32[2,16,52,512]{3,1,2,0:T(8,128)S(1)} %bitcast.27) | data formatting | bytes 6815744 | tf_op jit(solution)/shard_map/convert_element_type | solution.py:43
  138.8 5.2 %reshape.40 = f32[13,128,4,128]{3,2,1,0:T(4,128)} reshape(f32[2,16,52,512]{3,2,1,0:T(8,128)} %copy.16) | data formatting | bytes 6815744 | tf_op jit(solution)/shard_map/convert_element_type | solution.py:43
  143.9 2.9 %reshape.39 = f32[1664,512]{1,0:T(8,128)S(1)} reshape(f32[2,16,52,512]{3,2,1,0:T(8,128)} %copy.16) | data formatting | bytes 6815744 | tf_op jit(solution)/shard_map/convert_element_type | solution.py:43
  146.8 3.1 %abs_reduce_fusion = f32[13,4]{1,0:T(8,128)S(1)} fusion(f32[13,128,4,128]{3,2,1,0:T(4,128)} %reshape.40, f32[13,4]{1,0:T(8,128)S(1)} %dynamic_slice.4), kind=kLoop, calls=%fused_computation.5 | loop fusion | flops 2555852 | bytes 3408288 | tf_op jit(solution)/shard_map/reduce_max | solution.py:46
  149.9 0.5 div.17
  150.4 0.0 copy-start
  150.4 0.5 mul.38
  150.9 1.3 copy-done
  152.2 2.5 fusion
  154.7 0.0 copy-start.1
  154.7 26.7 %all-gather.2.cloned.1.call-done = bf16[2048,1664]{1,0:T(8,128)(2,1)} async-done(((bf16[64,1664]{1,0:T(8,128)(2,1)}), bf16[2048,1664]{1,0:T(8,128)(2,1)}) %all-gather.2.cloned.1.call-update) | async-done | bytes 6815760 | tf_op jit(solution)/shard_map/all_gather | solution.py:54
  181.4 9.7 %convolution_convert_fusion = bf16[2048,512]{1,0:T(8,128)(2,1)} fusion(bf16[2048,1664]{1,0:T(8,128)(2,1)} %all-gather.2.cloned.1.call-done, bf16[1664,512]{1,0:T(8,128)(2,1)} %fusion, f32[208,8,4,128]{3,2,1,0:T(4,128)} %bitcast.29), kind=kOutput, calls=%fused_computation.6 | convolution fusion | flops 3493265408 | bytes 14024704 | tf_op jit(solution)/shard_map/dot_general | solution.py:53
  191.2 0.0 reduce-scatter.2.cloned.1.call-update
  191.2 0.0 copy-done.1
  191.2 2.3 copy.18
  193.5 0.7 copy.19
  194.2 61.0 %reduce-scatter.2.cloned.1.call-done = bf16[128,512]{1,0:T(8,128)(2,1)} async-done(((bf16[2048,512]{1,0:T(8,128)(2,1)}), bf16[128,512]{1,0:T(8,128)(2,1)}) %reduce-scatter.2.cloned.1.call-update) | async-done | bytes 131088 | tf_op jit(solution)/shard_map/reduce_scatter | solution.py:60
  (1 shorter events, 0.0 us)
Async XLA Ops:
  7.2 174.3 %all-gather.2.cloned.1.call-start = ((), (), s32[]{:S(2)}) async-start(), calls=%async_computation.3 | async-start | bytes 7028736 | tf_op jit(solution)/shard_map/all_gather | solution.py:54
  90.4 44.0 %all-to-all-start.1 = ((bf16[16,104,512]{2,1,0:T(8,128)(2,1)}), bf16[16,104,512]{2,1,0:T(8,128)(2,1)S(1)}, u32[]{:S(2)}, u32[]{:S(2)}) async-start(bf16[16,104,512]{2,1,0:T(8,128)(2,1)} %reshape.38), calls=%async_computation.1 | async-start | bytes 3407872 | tf_op jit(solution)/shard_map/all_to_all | solution.py:33
  96.8 158.5 %reduce-scatter.2.cloned.1.call-start = ((), (), s32[]{:S(2)}) async-start(), calls=%async_computation.4 | async-start | bytes 2228224 | tf_op jit(solution)/shard_map/reduce_scatter | solution.py:60
  150.4 1.8 copy-start
  154.7 36.4 %copy-start.1 = (bf16[1664,512]{1,0:T(8,128)(2,1)S(1)}, bf16[1664,512]{1,0:T(8,128)(2,1)}, u32[]{:S(2)}) copy-start(bf16[1664,512]{1,0:T(8,128)(2,1)} %fusion) | copy-start | bytes 5111812
Sparse Core Ops, SparseCore 0:
  11.2 170.2 all-gather.1
  191.3 63.8 reduce-scatter.1
where the time goes:
time: 264 us; the launch traced here: 262 us
  waiting for transfers between devices  124 us (47%)
  blocking collectives  76.7 us (29%)
  local copies, waits for them, and re-layouts  23.1 us (9%)
  between operations  14.1 us (5%)
  matrix products  9.71 us (4%)
  other arithmetic  7.45 us (3%)
  starting transfers between devices  6.6 us (2%)
    all_to_all x1, blocking collectives, body(): lax.all_to_all(old_codes, 'fsdp', split_axis=1, concat_axis=0, tiled=True)  76.7 us
    reduce_scatter x1, waiting for transfers between devices, body(): lax.psum_scatter(partial_value.astype(jnp.bfloat16), 'tensor', scatter_di...  61 us
    all_to_all x1, waiting for transfers between devices, body(): lax.all_to_all(sectioned.reshape(n_tensor, per_owner * block_rows, col_wi...  36.6 us
    all_gather x1, waiting for transfers between devices, body(): lax.all_gather(hidden, 'fsdp', axis=0, tiled=True)  26.7 us
    convert_element_type x4, local copies, waits for them, and re-layouts, body(): final_rows.astype(jnp.float32).reshape(row_tiles, TILE, col_tiles, TILE)  12.4 us
    dot_general x1, matrix products, body(): jnp.dot(lax.all_gather(hidden, 'fsdp', axis=0, tiled=True), weight, prefe...  9.71 us
    unnamed x7, local copies, waits for them, and re-layouts  6.44 us
    all_to_all x1, starting transfers between devices, body(): lax.all_to_all(sectioned.reshape(n_tensor, per_owner * block_rows, col_wi...  6.35 us
  transfers between devices with their start and end apart: 3, of which 3 were waited for; matrix products, arithmetic and copies ran while one was open for 10% of the time, Pallas kernels for 0%

commit v1 on v0

v1 whole, which is shorter than its diff:
```python
import jax
import jax.numpy as jnp
from jax import lax
from jax.sharding import Mesh, PartitionSpec as P

TILE = 128
EPSILON = 1e-06
AXES = ("z", "h", "x", "l", "c")
SIZES = (8, 4, 4, 2, 2)
FSDP = ("z", "h")
TENSOR = ("x", "l", "c")


def body(old_codes, old_scales, gate_pre, up_pre):
    n_fsdp = lax.axis_size(FSDP)
    n_tensor = lax.axis_size(TENSOR)
    f_index = lax.axis_index(FSDP)
    t_index = lax.axis_index(TENSOR)
    block_rows, full_width = old_codes.shape
    col_width = full_width // n_fsdp
    col_tiles = col_width // TILE
    per_owner = n_fsdp // n_tensor
    own_rows = block_rows * n_fsdp
    row_tiles = own_rows // TILE
    hidden = (jax.nn.silu(gate_pre.astype(jnp.float32)) * up_pre.astype(jnp.float32)).astype(
        jnp.bfloat16
    )
    near = lax.all_gather(hidden, "h", axis=0, tiled=True)
    every = lax.all_gather(near, "z", axis=0, tiled=True)
    sectioned = lax.all_to_all(old_codes, FSDP, split_axis=1, concat_axis=0, tiled=True)
    moved = lax.all_to_all(
        sectioned.reshape(n_tensor, per_owner * block_rows, col_width),
        TENSOR,
        split_axis=0,
        concat_axis=0,
        tiled=True,
    )
    final_rows = jnp.swapaxes(
        moved.reshape(n_tensor, per_owner, block_rows, col_width), 0, 1
    ).reshape(own_rows, col_width)
    scale_block = lax.dynamic_slice(
        old_scales, (t_index * row_tiles, f_index * col_tiles), (row_tiles, col_tiles)
    )
    tile_values = (
        final_rows.astype(jnp.float32).reshape(row_tiles, TILE, col_tiles, TILE)
        * scale_block[:, None, :, None]
    )
    new_scale = jnp.max(jnp.abs(tile_values), axis=(1, 3)) + EPSILON
    new_codes = (tile_values / new_scale[:, None, :, None]).astype(jnp.bfloat16)
    weight = (
        (new_codes.astype(jnp.float32) * new_scale[:, None, :, None])
        .astype(jnp.bfloat16)
        .reshape(own_rows, col_width)
    )
    partial_value = jnp.dot(every, weight, preferred_element_type=jnp.float32)
    codes_t = new_codes.reshape(own_rows, col_width).T
    scales_t = new_scale.T
    shares = lax.all_to_all(
        partial_value.astype(jnp.bfloat16), TENSOR, split_axis=0, concat_axis=0, tiled=True
    )
    tokens = shares.shape[0] // n_tensor
    mixed = jnp.sum(
        shares.reshape(n_tensor, tokens, col_width).astype(jnp.float32), axis=0
    ).astype(jnp.bfloat16)
    return (mixed, codes_t, scales_t)


def solution(mesh):
    fine = Mesh(mesh.devices.reshape(SIZES), AXES)
    return jax.shard_map(
        body,
        mesh=fine,
        in_specs=(P(FSDP + TENSOR, None), P(), P(FSDP, TENSOR), P(FSDP, TENSOR)),
        out_specs=(P(TENSOR, FSDP), P(FSDP, TENSOR), P(FSDP, TENSOR)),
        check_vma=False,
    )
```

time: 264 us -> 205 us (0.78)
  waiting for transfers between devices: 124 us -> 53.2 us
  starting transfers between devices: 6.6 us -> 15.6 us
  blocking collectives: 76.7 us -> 80.3 us
    reduce_scatter x1 -> x0, waiting for transfers between devices: 61 us -> none  [body(): lax.psum_scatter(partial_value.astype(jnp.bfloat16), 'tensor', scatter_di...]
    all_to_all x0 -> x1, waiting for transfers between devices: none -> 22.8 us  [body(): lax.all_to_all(partial_value.astype(jnp.bfloat16), TENSOR, split_axis=0,...]
    all_gather x0 -> x1, blocking collectives: none -> 21.3 us  [body(): near = lax.all_gather(hidden, 'h', axis=0, tiled=True)]
    all_gather x1, waiting for transfers between devices: 26.7 us -> 8.23 us  [body(): every = lax.all_gather(near, 'z', axis=0, tiled=True)]
    all_to_all x1, blocking collectives: 76.7 us -> 58.9 us  [body(): lax.all_to_all(old_codes, FSDP, split_axis=1, concat_axis=0, tiled=True)]
    all_to_all x1, waiting for transfers between devices: 36.6 us -> 22.1 us  [body(): lax.all_to_all(sectioned.reshape(n_tensor, per_owner * block_rows, col_wi...]
    all_to_all x0 -> x1, starting transfers between devices: none -> 4.88 us  [body(): lax.all_to_all(partial_value.astype(jnp.bfloat16), TENSOR, split_axis=0,...]
    all_to_all x1, starting transfers between devices: 6.35 us -> 10.7 us  [body(): lax.all_to_all(sectioned.reshape(n_tensor, per_owner * block_rows, col_wi...]
  transfers between devices with their start and end apart: 3 -> 3, of which waited for: 3 -> 3; matrix products, arithmetic and copies ran while one was open for 10% -> 13% of each run, Pallas kernels for 0% -> 0%
where the time goes in v1:
time: 205 us; the launch traced here: 204 us
  blocking collectives  80.3 us (39%)
  waiting for transfers between devices  53.2 us (26%)
  local copies, waits for them, and re-layouts  22.9 us (11%)
  starting transfers between devices  15.6 us (8%)
  between operations  14.1 us (7%)
  matrix products  9.72 us (5%)
  other arithmetic  7.97 us (4%)
    all_to_all x1, blocking collectives, body(): lax.all_to_all(old_codes, FSDP, split_axis=1, concat_axis=0, tiled=True)  58.9 us
    all_to_all x1, waiting for transfers between devices, body(): lax.all_to_all(partial_value.astype(jnp.bfloat16), TENSOR, split_axis=0,...  22.8 us
    all_to_all x1, waiting for transfers between devices, body(): lax.all_to_all(sectioned.reshape(n_tensor, per_owner * block_rows, col_wi...  22.1 us
    all_gather x1, blocking collectives, body(): near = lax.all_gather(hidden, 'h', axis=0, tiled=True)  21.3 us
    convert_element_type x4, local copies, waits for them, and re-layouts, body(): final_rows.astype(jnp.float32).reshape(row_tiles, TILE, col_tiles, TILE)  12.4 us
    all_to_all x1, starting transfers between devices, body(): lax.all_to_all(sectioned.reshape(n_tensor, per_owner * block_rows, col_wi...  10.7 us
    dot_general x1, matrix products, body(): partial_value = jnp.dot(every, weight, preferred_element_type=jnp.float32)  9.72 us
    all_gather x1, waiting for transfers between devices, body(): every = lax.all_gather(near, 'z', axis=0, tiled=True)  8.23 us
  transfers between devices with their start and end apart: 3, of which 3 were waited for; matrix products, arithmetic and copies ran while one was open for 13% of the time, Pallas kernels for 0%

profile of v1, /device:TPU:1, one launch (start us, length us, event | category | flops | bytes accessed | tf_op | source)
XLA Modules:
  0.0 203.8 jit_solution(15859848705380097356)
XLA Ops:
  7.2 0.0 copy-start.1
  7.2 0.0 all-gather.2.cloned.1.call-start
  7.2 1.3 fusion.7
  8.5 21.3 %all_gather.6 = bf16[256,1664]{1,0:T(8,128)(2,1)} all-gather(bf16[64,1664]{1,0:T(8,128)(2,1)S(1)} %fusion.7), channel_id=1, replica_groups=mesh['z'=8,'h'=4,'x'=4,'l'=2,'c'=2] {'h'}, dimensions={0}, use_global_device_ids=true | all-gather | bytes 1064960 | tf_op jit(solution)/shard_map/all_gather | solution.py:28
  29.8 0.0 all-gather.2.cloned.1.call-update
  29.9 0.0 copy-done.1
  29.9 0.7 copy.20
  30.5 0.2 slice
  30.7 0.9 copy.14
  31.7 58.9 %all_to_all.30 = bf16[52,32,512]{2,0,1:T(8,128)(2,1)S(1)} all-to-all(bf16[52,32,512]{2,0,1:T(8,128)(2,1)S(1)} %copy.14), channel_id=1, replica_groups=mesh['z'=8,'h'=4,'x'=4,'l'=2,'c'=2] {'z','h'}, dimensions={1} | all-to-all | bytes 3407872 | tf_op jit(solution)/shard_map/all_to_all | solution.py:30
  90.6 1.3 reshape.42
  92.0 10.7 %all-to-all-start.1 = ((bf16[16,104,512]{2,1,0:T(8,128)(2,1)}), bf16[16,104,512]{2,1,0:T(8,128)(2,1)S(1)}, u32[]{:S(2)}, u32[]{:S(2)}) async-start(bf16[16,104,512]{2,1,0:T(8,128)(2,1)} %reshape.42), calls=%async_computation.1 | async-start | bytes 3407872 | tf_op jit(solution)/shard_map/all_to_all | solution.py:31
  102.7 0.8 dynamic_slice.3
  103.5 22.1 %all-to-all-done.1 = bf16[16,104,512]{2,1,0:T(8,128)(2,1)S(1)} async-done(((bf16[16,104,512]{2,1,0:T(8,128)(2,1)}), bf16[16,104,512]{2,1,0:T(8,128)(2,1)S(1)}, u32[]{:S(2)}, u32[]{:S(2)}) %all-to-all-start.1) | async-done | bytes 1703968 | tf_op jit(solution)/shard_map/all_to_all | solution.py:31
  125.6 0.6 copy.15
  126.1 3.8 %copy.16 = f32[2,16,52,512]{3,2,1,0:T(8,128)} copy(f32[2,16,52,512]{3,1,2,0:T(8,128)S(1)} %bitcast.28) | data formatting | bytes 6815744 | tf_op jit(solution)/shard_map/convert_element_type | solution.py:45
  130.0 5.2 %reshape.44 = f32[13,128,4,128]{3,2,1,0:T(4,128)} reshape(f32[2,16,52,512]{3,2,1,0:T(8,128)} %copy.16) | data formatting | bytes 6815744 | tf_op jit(solution)/shard_map/convert_element_type | solution.py:45
  135.1 2.9 %reshape.43 = f32[1664,512]{1,0:T(8,128)S(1)} reshape(f32[2,16,52,512]{3,2,1,0:T(8,128)} %copy.16) | data formatting | bytes 6815744 | tf_op jit(solution)/shard_map/convert_element_type | solution.py:45
  138.0 3.1 %abs_reduce_fusion = f32[13,4]{1,0:T(8,128)S(1)} fusion(f32[13,128,4,128]{3,2,1,0:T(4,128)} %reshape.44, f32[13,4]{1,0:T(8,128)S(1)} %dynamic_slice.3), kind=kLoop, calls=%fused_computation.5 | loop fusion | flops 2555852 | bytes 3408288 | tf_op jit(solution)/shard_map/reduce_max | solution.py:48
  141.1 0.5 div.17
  141.6 0.0 copy-start
  141.6 0.5 mul.50
  142.2 1.3 copy-done
  143.4 2.6 %fusion = bf16[1664,512]{1,0:T(8,128)(2,1)} fusion(f32[1664,512]{1,0:T(8,128)S(1)} %reshape.43, f32[208,8,4,128]{3,2,1,0:T(4,128)S(1)} %bitcast.31, f32[208,8,4,128]{3,2,1,0:T(4,128)S(1)} %bitcast.29), kind=kLoop, calls=%fused_computation.2 | loop fusion | flops 2555904 | bytes 11927552 | tf_op jit(solution)/shard_map/convert_element_type | solution.py:49
  146.0 8.2 %all-gather.2.cloned.1.call-done = bf16[2048,1664]{1,0:T(8,128)(2,1)} async-done(((bf16[256,1664]{1,0:T(8,128)(2,1)}), bf16[2048,1664]{1,0:T(8,128)(2,1)}) %all-gather.2.cloned.1.call-update) | async-done | bytes 6815760 | tf_op jit(solution)/shard_map/all_gather | solution.py:29
  154.3 9.7 %convolution_convert_fusion = bf16[2048,512]{1,0:T(8,128)(2,1)} fusion(bf16[2048,1664]{1,0:T(8,128)(2,1)} %all-gather.2.cloned.1.call-done, bf16[1664,512]{1,0:T(8,128)(2,1)} %fusion, f32[208,8,4,128]{3,2,1,0:T(4,128)} %bitcast.30), kind=kOutput, calls=%fused_computation.6 | convolution fusion | flops 3493265408 | bytes 14024704 | tf_op jit(solution)/shard_map/dot_general | solution.py:55
  164.0 4.9 %all-to-all-start.2 = ((bf16[16,128,512]{2,1,0:T(8,128)(2,1)}), bf16[16,128,512]{2,1,0:T(8,128)(2,1)S(1)}, u32[]{:S(2)}, u32[]{:S(2)}) async-start(bf16[16,128,512]{2,1,0:T(8,128)(2,1)} %bitcast.35), calls=%async_computation.2 | async-start | bytes 4194304 | tf_op jit(solution)/shard_map/all_to_all | solution.py:58
  168.9 3.6 %copy.18 = bf16[512,1664]{1,0:T(8,128)(2,1)} copy(bf16[512,1664]{0,1:T(8,128)(2,1)} %bitcast.34) | data formatting | bytes 3407872
  172.5 0.7 copy.19
  173.1 22.8 %all-to-all-done.2 = bf16[16,128,512]{2,1,0:T(8,128)(2,1)S(1)} async-done(((bf16[16,128,512]{2,1,0:T(8,128)(2,1)}), bf16[16,128,512]{2,1,0:T(8,128)(2,1)S(1)}, u32[]{:S(2)}, u32[]{:S(2)}) %all-to-all-start.2) | async-done | bytes 2097184 | tf_op jit(solution)/shard_map/all_to_all | solution.py:58
  196.0 1.0 reduce_sum.12
  (1 shorter events, 0.0 us)
Async XLA Ops:
  7.2 22.7 %copy-start.1 = (bf16[52,16384]{1,0:T(8,128)(2,1)S(1)}, bf16[52,16384]{1,0:T(8,128)(2,1)}, u32[]{:S(2)}) copy-start(bf16[52,16384]{1,0:T(8,128)(2,1)} %param.4) | copy-start | bytes 5111812
  7.2 147.1 %all-gather.2.cloned.1.call-start = ((), (), s32[]{:S(2)}) async-start(), calls=%async_computation.3 | async-start | bytes 7667712 | tf_op jit(solution)/shard_map/all_gather | solution.py:29
  92.0 33.6 %all-to-all-start.1 = ((bf16[16,104,512]{2,1,0:T(8,128)(2,1)}), bf16[16,104,512]{2,1,0:T(8,128)(2,1)S(1)}, u32[]{:S(2)}, u32[]{:S(2)}) async-start(bf16[16,104,512]{2,1,0:T(8,128)(2,1)} %reshape.42), calls=%async_computation.1 | async-start | bytes 3407872 | tf_op jit(solution)/shard_map/all_to_all | solution.py:31
  141.6 1.8 copy-start
  164.0 32.0 %all-to-all-start.2 = ((bf16[16,128,512]{2,1,0:T(8,128)(2,1)}), bf16[16,128,512]{2,1,0:T(8,128)(2,1)S(1)}, u32[]{:S(2)}, u32[]{:S(2)}) async-start(bf16[16,128,512]{2,1,0:T(8,128)(2,1)} %bitcast.35), calls=%async_computation.2 | async-start | bytes 4194304 | tf_op jit(solution)/shard_map/all_to_all | solution.py:58
Sparse Core Ops, SparseCore 0:
  30.0 124.2 all-gather.1

commit v2 on v1

v2 whole, which is shorter than its diff:
```python
import jax
import jax.numpy as jnp
from jax import lax
from jax.experimental import pallas as pl
from jax.experimental.pallas import tpu as pltpu
from jax.sharding import Mesh, PartitionSpec as P

TILE = 128
EPSILON = 1e-06
AXES = ("z", "h", "x", "l", "c")
SIZES = (8, 4, 4, 2, 2)
FSDP = ("z", "h")
TENSOR = ("x", "l", "c")
PACK_STEPS = 4


def pack_kernel(in_ref, out_ref, scratch):
    rows = in_ref.shape[0]
    sections, _, lanes = out_ref.shape
    tiles = in_ref.shape[1] // (sections * lanes)
    for section in range(sections):
        for tile in range(tiles):
            at = (section * tiles + tile) * lanes
            scratch[pl.ds(tile * rows, rows), :] = in_ref[:, pl.ds(at, lanes)].astype(jnp.float32)
        out_ref[section] = scratch[...].astype(jnp.bfloat16)


def pack(old_codes, n_fsdp):
    rows, width = old_codes.shape
    packed_rows = rows * width // n_fsdp // TILE
    sections = n_fsdp // PACK_STEPS
    return pl.pallas_call(
        pack_kernel,
        out_shape=jax.ShapeDtypeStruct((n_fsdp, packed_rows, TILE), jnp.bfloat16),
        grid=(PACK_STEPS,),
        in_specs=[pl.BlockSpec((rows, width // PACK_STEPS), lambda i: (0, i))],
        out_specs=pl.BlockSpec((sections, packed_rows, TILE), lambda i: (i, 0, 0)),
        scratch_shapes=[pltpu.VMEM((packed_rows, TILE), jnp.float32)],
        compiler_params=pltpu.CompilerParams(vmem_limit_bytes=12 << 20),
        name="pack",
    )(old_codes)


def requantize_kernel(scale_ref, in_ref, codes_ref, weight_ref, new_scale_ref, rows_ref, piece_ref):
    senders, parts, packed_rows, _ = in_ref.shape
    total_rows, width = rows_ref.shape
    tiles = width // TILE
    rows = packed_rows // tiles

    for part in range(parts):
        for sender in range(senders):
            slot = sender % 2
            piece_ref[slot] = in_ref[sender, part].astype(jnp.float32)
            base = (part * senders + sender) * rows
            for tile in range(tiles):
                rows_ref[pl.ds(base, rows), tile * TILE : (tile + 1) * TILE] = piece_ref[
                    slot, pl.ds(tile * rows, rows), :
                ]
    lane = lax.broadcasted_iota(jnp.int32, (1, TILE), 1)

    def one_row(row, carry):
        at = pl.ds(pl.multiple_of(row * TILE, TILE), TILE)
        line = jnp.zeros((1, TILE), jnp.float32)
        for tile in range(tiles):
            cols = slice(tile * TILE, (tile + 1) * TILE)
            codes = rows_ref[at, cols]
            scale = scale_ref[row, tile]
            top = jnp.max(jnp.abs(codes), axis=0, keepdims=True)
            new_scale = jnp.max(top, axis=1, keepdims=True) * scale + EPSILON
            line = jnp.where(lane == tile, new_scale, line)
            new_codes = (codes * scale / new_scale).astype(jnp.bfloat16)
            codes_ref[at, cols] = new_codes
            weight_ref[at, cols] = (new_codes.astype(jnp.float32) * new_scale).astype(jnp.bfloat16)
        new_scale_ref[pl.ds(row, 1), :] = line
        return carry

    lax.fori_loop(0, total_rows // TILE, one_row, 0)


def requantize(moved, scale_block, width):
    senders, parts, packed_rows, _ = moved.shape
    total_rows = senders * parts * packed_rows * TILE // width
    vmem = pl.BlockSpec(memory_space=pltpu.VMEM)
    return pl.pallas_call(
        requantize_kernel,
        out_shape=(
            jax.ShapeDtypeStruct((total_rows, width), jnp.bfloat16),
            jax.ShapeDtypeStruct((total_rows, width), jnp.bfloat16),
            jax.ShapeDtypeStruct((total_rows // TILE, TILE), jnp.float32),
        ),
        in_specs=[pl.BlockSpec(memory_space=pltpu.SMEM), vmem],
        out_specs=(vmem, vmem, vmem),
        scratch_shapes=[
            pltpu.VMEM((total_rows, width), jnp.float32),
            pltpu.VMEM((2, packed_rows, TILE), jnp.float32),
        ],
        compiler_params=pltpu.CompilerParams(vmem_limit_bytes=20 << 20),
        name="requantize",
    )(scale_block, moved)


def body(old_codes, old_scales, gate_pre, up_pre):
    n_fsdp = lax.axis_size(FSDP)
    n_tensor = lax.axis_size(TENSOR)
    f_index = lax.axis_index(FSDP)
    t_index = lax.axis_index(TENSOR)
    block_rows, full_width = old_codes.shape
    col_width = full_width // n_fsdp
    col_tiles = col_width // TILE
    per_owner = n_fsdp // n_tensor
    own_rows = block_rows * n_fsdp
    row_tiles = own_rows // TILE
    hidden = (jax.nn.silu(gate_pre.astype(jnp.float32)) * up_pre.astype(jnp.float32)).astype(
        jnp.bfloat16
    )
    half = hidden.shape[0] // 2
    first = lax.all_gather(hidden[:half], FSDP, axis=0, tiled=True)
    packed = pack(old_codes, n_fsdp)
    packed_rows = packed.shape[1]
    near = lax.all_gather(hidden[half:], "h", axis=0, tiled=True)
    second = lax.all_gather(near, "z", axis=0, tiled=True)

    sectioned = lax.all_to_all(packed, FSDP, split_axis=0, concat_axis=0, tiled=True)
    moved = lax.all_to_all(
        sectioned.reshape(n_tensor, per_owner * packed_rows, TILE),
        TENSOR,
        split_axis=0,
        concat_axis=0,
        tiled=True,
    )
    scale_block = lax.dynamic_slice(
        old_scales, (t_index * row_tiles, f_index * col_tiles), (row_tiles, col_tiles)
    )
    new_codes, weight, new_scale = requantize(
        moved.reshape(n_tensor, per_owner, packed_rows, TILE), scale_block, col_width
    )
    codes_t = new_codes.T
    scales_t = new_scale[:, :col_tiles].T

    pieces = []
    for tokens in (first, second):
        share = jnp.dot(tokens, weight, preferred_element_type=jnp.float32).astype(jnp.bfloat16)
        shares = lax.all_to_all(share, TENSOR, split_axis=0, concat_axis=0, tiled=True)
        total = jnp.sum(
            shares.reshape(n_tensor, per_owner, half, col_width).astype(jnp.float32), axis=0
        )
        pieces.append(total.astype(jnp.bfloat16))
    mixed = jnp.stack(pieces, axis=1).reshape(per_owner * 2 * half, col_width)
    return (mixed, codes_t, scales_t)


def solution(mesh):
    fine = Mesh(mesh.devices.reshape(SIZES), AXES)
    return jax.shard_map(
        body,
        mesh=fine,
        in_specs=(P(FSDP + TENSOR, None), P(), P(FSDP, TENSOR), P(FSDP, TENSOR)),
        out_specs=(P(TENSOR, FSDP), P(FSDP, TENSOR), P(FSDP, TENSOR)),
        check_vma=False,
    )
```

time: 205 us -> 251 us (1.22)
  waiting for transfers between devices: 53.2 us -> 160 us
  blocking collectives: 80.3 us -> 17 us
  starting transfers between devices: 15.6 us -> 34.5 us
  local copies, waits for them, and re-layouts: 22.9 us -> 5.64 us
  Pallas kernels: 0 us -> 5.23 us
  other arithmetic: 7.97 us -> 3.48 us
    all_gather x1 -> x2, waiting for transfers between devices: 8.23 us -> 79.9 us  [the longest x1 79.9 us: body(): first = lax.all_gather(hidden[:half], FSDP, axis=0, tiled=True)]
    all_to_all x1 -> x0, blocking collectives: 58.9 us -> none  [body(): lax.all_to_all(old_codes, FSDP, split_axis=1, concat_axis=0, tiled=True)]
    all_to_all x2 -> x4, waiting for transfers between devices: 45 us -> 79.5 us  [the longest x1 45.9 us: body(): lax.all_to_all(packed, FSDP, split_axis=0, concat_axis=0, tiled=True)]
    all_to_all x2 -> x4, starting transfers between devices: 15.6 us -> 34.4 us  [the longest x1 12.5 us: body(): lax.all_to_all(packed, FSDP, split_axis=0, concat_axis=0, tiled=True)]
    convert_element_type x4 -> x0, local copies, waits for them, and re-layouts: 12.4 us -> none  [body(): final_rows.astype(jnp.float32).reshape(row_tiles, TILE, col_tiles, TILE)]
    pallas_call x0 -> x2, Pallas kernels: none -> 5.23 us  [the longest x1 3.28 us: requantize(): pl.pallas_call(requantize_kernel, out_shape=(jax.ShapeDtypeStruct((total_...]
    all_gather x1, blocking collectives: 21.3 us -> 17 us  [body(): near = lax.all_gather(hidden[half:], 'h', axis=0, tiled=True)]
    reduce_max x1 -> x0, other arithmetic: 3.1 us -> none  [body(): new_scale = jnp.max(jnp.abs(tile_values), axis=(1, 3)) + EPSILON]
  transfers between devices with their start and end apart: 3 -> 6, of which waited for: 3 -> 4; matrix products, arithmetic and copies ran while one was open for 13% -> 6% of each run, Pallas kernels for 0% -> 2%
where the time goes in v2:
time: 251 us
  waiting for transfers between devices  160 us (64%)
  starting transfers between devices  34.5 us (14%)
  blocking collectives  17 us (7%)
  between operations  14.1 us (6%)
  matrix products  10.5 us (4%)
  local copies, waits for them, and re-layouts  5.64 us (2%)
  Pallas kernels  5.23 us (2%)
  other arithmetic  3.48 us (1%)
    all_gather x1, waiting for transfers between devices, body(): first = lax.all_gather(hidden[:half], FSDP, axis=0, tiled=True)  79.9 us
    all_to_all x1, waiting for transfers between devices, body(): lax.all_to_all(packed, FSDP, split_axis=0, concat_axis=0, tiled=True)  45.9 us
    all_to_all x1, waiting for transfers between devices, body(): lax.all_to_all(sectioned.reshape(n_tensor, per_owner * packed_rows, TILE)...  22.1 us
    all_gather x1, blocking collectives, body(): near = lax.all_gather(hidden[half:], 'h', axis=0, tiled=True)  17 us
    all_to_all x1, starting transfers between devices, body(): lax.all_to_all(packed, FSDP, split_axis=0, concat_axis=0, tiled=True)  12.5 us
    all_to_all x2, starting transfers between devices, body(): lax.all_to_all(share, TENSOR, split_axis=0, concat_axis=0, tiled=True)  12.1 us
    all_to_all x2, waiting for transfers between devices, body(): lax.all_to_all(share, TENSOR, split_axis=0, concat_axis=0, tiled=True)  11.4 us
    dot_general x2, matrix products, body(): jnp.dot(tokens, weight, preferred_element_type=jnp.float32)  10.5 us
  transfers between devices with their start and end apart: 6, of which 4 were waited for; matrix products, arithmetic and copies ran while one was open for 6% of the time, Pallas kernels for 2%

profile of v2, /device:TPU:1, one launch (start us, length us, event | category | flops | bytes accessed | tf_op | source)
XLA Modules:
  0.0 250.6 jit_solution(12109247267392620832)
XLA Ops:
  7.2 0.0 copy-start
  7.2 0.0 all-gather.5.cloned.1.call-start
  7.2 1.3 fusion.4
  8.5 0.7 fusion.5
  9.2 17.0 %all_gather.10 = bf16[128,1664]{1,0:T(8,128)(2,1)} all-gather(bf16[32,1664]{1,0:T(8,128)(2,1)S(1)} %get-tuple-element.13), channel_id=1, replica_groups=mesh['z'=8,'h'=4,'x'=4,'l'=2,'c'=2] {'h'}, dimensions={0}, use_global_device_ids=true | all-gather | bytes 532480 | tf_op jit(solution)/shard_map/all_gather | solution.py:120
  26.2 0.0 all-gather.5.cloned.1.call-update
  26.2 0.0 copy-done
  26.2 1.9 pack.1
  28.2 12.5 %all-to-all-start = ((bf16[32,208,128]{2,1,0:T(8,128)(2,1)}), bf16[32,208,128]{2,1,0:T(8,128)(2,1)}, u32[]{:S(2)}, u32[]{:S(2)}) async-start(bf16[32,208,128]{2,1,0:T(8,128)(2,1)} %pack.1), calls=%async_computation | async-start | bytes 3407872 | tf_op jit(solution)/shard_map/all_to_all | solution.py:123
  40.7 0.0 all-gather.3.cloned.1.call-start
  40.8 0.7 all-gather.3.cloned.1.call-update
  41.5 45.9 %all-to-all-done = bf16[32,208,128]{2,1,0:T(8,128)(2,1)} async-done(((bf16[32,208,128]{2,1,0:T(8,128)(2,1)}), bf16[32,208,128]{2,1,0:T(8,128)(2,1)}, u32[]{:S(2)}, u32[]{:S(2)}) %all-to-all-start) | async-done | bytes 1703968 | tf_op jit(solution)/shard_map/all_to_all | solution.py:123
  87.4 9.8 %all-to-all-start.1 = ((bf16[16,416,128]{2,1,0:T(8,128)(2,1)}), bf16[16,416,128]{2,1,0:T(8,128)(2,1)S(1)}, u32[]{:S(2)}, u32[]{:S(2)}) async-start(bf16[16,416,128]{2,1,0:T(8,128)(2,1)} %bitcast), calls=%async_computation.1 | async-start | bytes 3407872 | tf_op jit(solution)/shard_map/all_to_all | solution.py:124
  97.2 0.8 dynamic_slice.3.scale_ref
  98.0 22.1 %all-to-all-done.1 = bf16[16,416,128]{2,1,0:T(8,128)(2,1)S(1)} async-done(((bf16[16,416,128]{2,1,0:T(8,128)(2,1)}), bf16[16,416,128]{2,1,0:T(8,128)(2,1)S(1)}, u32[]{:S(2)}, u32[]{:S(2)}) %all-to-all-start.1) | async-done | bytes 1703968 | tf_op jit(solution)/shard_map/all_to_all | solution.py:124
  120.1 3.3 %requantize.1 = (bf16[1664,512]{1,0:T(8,128)(2,1)S(1)}, bf16[1664,512]{1,0:T(8,128)(2,1)S(1)}, f32[13,128]{1,0:T(8,128)S(1)}) custom-call(f32[13,4]{1,0:T(8,128)S(1)} %dynamic_slice.3.scale_ref, bf16[16,2,208,128]{3,2,1,0:T(8,128)(2,1)S(1)} %bitcast.14), custom_call_target="tpu_custom_call" | custom-call | tf_op jit(solution)/shard_map/requantize/pallas_call | solution.py:84
  123.4 0.0 copy-start.1
  123.4 1.2 copy-done.1
  124.6 0.0 all-gather.5.cloned.1.call-done
  124.6 5.5 %convolution_convert_fusion = bf16[1024,512]{1,0:T(8,128)(2,1)} fusion(bf16[1024,1664]{1,0:T(8,128)(2,1)} %all-gather.5.cloned.1.call-done, bf16[1664,512]{1,0:T(8,128)(2,1)} %copy-done.1), kind=kOutput, calls=%fused_computation | convolution fusion | flops 1745354752 | bytes 6160384 | tf_op jit(solution)/shard_map/dot_general | solution.py:142
  130.1 5.1 %all-to-all-start.3 = ((bf16[16,64,512]{2,1,0:T(8,128)(2,1)}), bf16[16,64,512]{2,1,0:T(8,128)(2,1)}, u32[]{:S(2)}, u32[]{:S(2)}) async-start(bf16[16,64,512]{2,1,0:T(8,128)(2,1)} %bitcast.17), calls=%async_computation.3 | async-start | bytes 2097152 | tf_op jit(solution)/shard_map/all_to_all | solution.py:143
  135.2 79.9 %all-gather.3.cloned.1.call-done = bf16[1024,1664]{1,0:T(8,128)(2,1)} async-done(((bf16[32,1664]{1,0:T(8,128)(2,1)}), bf16[1024,1664]{1,0:T(8,128)(2,1)}) %all-gather.3.cloned.1.call-update) | async-done | bytes 3407888 | tf_op jit(solution)/shard_map/all_gather | solution.py:117
  215.1 0.0 copy-done.2
  215.1 5.0 %convolution_convert_fusion.1 = bf16[1024,512]{1,0:T(8,128)(2,1)} fusion(bf16[1024,1664]{1,0:T(8,128)(2,1)} %all-gather.3.cloned.1.call-done, bf16[1664,512]{1,0:T(8,128)(2,1)S(1)} %copy-done.2), kind=kOutput, calls=%fused_computation.1 | convolution fusion | flops 1745354752 | bytes 6160384 | tf_op jit(solution)/shard_map/dot_general | solution.py:142
  220.1 0.0 all-to-all-done.3
  220.1 7.0 %all-to-all-start.2 = ((bf16[16,64,512]{2,1,0:T(8,128)(2,1)}), bf16[16,64,512]{2,1,0:T(8,128)(2,1)S(1)}, u32[]{:S(2)}, u32[]{:S(2)}) async-start(bf16[16,64,512]{2,1,0:T(8,128)(2,1)} %bitcast.16), calls=%async_computation.2 | async-start | bytes 2097152 | tf_op jit(solution)/shard_map/all_to_all | solution.py:143
  227.1 2.3 copy.7
  229.5 0.7 copy.8
  230.1 1.4 reduce_sum.25
  231.5 11.4 %all-to-all-done.2 = bf16[16,64,512]{2,1,0:T(8,128)(2,1)S(1)} async-done(((bf16[16,64,512]{2,1,0:T(8,128)(2,1)}), bf16[16,64,512]{2,1,0:T(8,128)(2,1)S(1)}, u32[]{:S(2)}, u32[]{:S(2)}) %all-to-all-start.2) | async-done | bytes 1048608 | tf_op jit(solution)/shard_map/all_to_all | solution.py:143
  242.9 0.1 reduce_sum.24
  243.1 0.7 pad_maximum_fusion
  (2 shorter events, 0.0 us)
Async XLA Ops:
  7.2 19.1 %copy-start = (bf16[52,16384]{1,0:T(8,128)(2,1)S(1)}, bf16[52,16384]{1,0:T(8,128)(2,1)}, u32[]{:S(2)}) copy-start(bf16[52,16384]{1,0:T(8,128)(2,1)} %in_ref.1) | copy-start | bytes 5111812
  7.2 117.4 %all-gather.5.cloned.1.call-start = ((), (), s32[]{:S(2)}) async-start(), calls=%async_computation.5 | async-start | bytes 3833856 | tf_op jit(solution)/shard_map/all_gather | solution.py:121
  28.2 59.2 %all-to-all-start = ((bf16[32,208,128]{2,1,0:T(8,128)(2,1)}), bf16[32,208,128]{2,1,0:T(8,128)(2,1)}, u32[]{:S(2)}, u32[]{:S(2)}) async-start(bf16[32,208,128]{2,1,0:T(8,128)(2,1)} %pack.1), calls=%async_computation | async-start | bytes 3407872 | tf_op jit(solution)/shard_map/all_to_all | solution.py:123
  40.7 174.4 %all-gather.3.cloned.1.call-start = ((), (), s32[]{:S(2)}) async-start(), calls=%async_computation.4 | async-start | bytes 3514368 | tf_op jit(solution)/shard_map/all_gather | solution.py:117
  87.4 32.7 %all-to-all-start.1 = ((bf16[16,416,128]{2,1,0:T(8,128)(2,1)}), bf16[16,416,128]{2,1,0:T(8,128)(2,1)S(1)}, u32[]{:S(2)}, u32[]{:S(2)}) async-start(bf16[16,416,128]{2,1,0:T(8,128)(2,1)} %bitcast), calls=%async_computation.1 | async-start | bytes 3407872 | tf_op jit(solution)/shard_map/all_to_all | solution.py:124
  123.4 1.2 copy-start.1
  130.1 85.0 %copy-start.2 = (bf16[1664,512]{1,0:T(8,128)(2,1)S(1)}, bf16[1664,512]{1,0:T(8,128)(2,1)}, u32[]{:S(2)}) copy-start(bf16[1664,512]{1,0:T(8,128)(2,1)} %copy-done.1) | copy-start | bytes 5111812
  130.1 90.0 %all-to-all-start.3 = ((bf16[16,64,512]{2,1,0:T(8,128)(2,1)}), bf16[16,64,512]{2,1,0:T(8,128)(2,1)}, u32[]{:S(2)}, u32[]{:S(2)}) async-start(bf16[16,64,512]{2,1,0:T(8,128)(2,1)} %bitcast.17), calls=%async_computation.3 | async-start | bytes 2097152 | tf_op jit(solution)/shard_map/all_to_all | solution.py:143
  220.1 22.8 %all-to-all-start.2 = ((bf16[16,64,512]{2,1,0:T(8,128)(2,1)}), bf16[16,64,512]{2,1,0:T(8,128)(2,1)S(1)}, u32[]{:S(2)}, u32[]{:S(2)}) async-start(bf16[16,64,512]{2,1,0:T(8,128)(2,1)} %bitcast.16), calls=%async_computation.2 | async-start | bytes 2097152 | tf_op jit(solution)/shard_map/all_to_all | solution.py:143
Sparse Core Ops, SparseCore 0:
  26.4 88.9 all-gather.4
  119.1 95.9 all-gather.2

commit v3 on v2

--- a/solution.py
+++ b/solution.py
@@ -1,3 +1,5 @@
+import functools
+
 import jax
 import jax.numpy as jnp
 from jax import lax
@@ -94,9 +96,78 @@
             pltpu.VMEM((total_rows, width), jnp.float32),
             pltpu.VMEM((2, packed_rows, TILE), jnp.float32),
         ],
-        compiler_params=pltpu.CompilerParams(vmem_limit_bytes=20 << 20),
+        compiler_params=pltpu.CompilerParams(vmem_limit_bytes=16 << 20),
         name="requantize",
     )(scale_block, moved)
+
+
+def product_kernel(n_z, n_h, rows, places, at_ref, *refs):
+    *block_refs, weight_ref, out_ref, tokens_ref = refs
+    for (shift, first), block_ref in zip(places, block_refs):
+        z_from = lax.rem(at_ref[0] + shift, n_z)
+        for group in range(block_ref.shape[0] // rows):
+            h_from = lax.rem(at_ref[1] + first + group, n_h)
+            place = pl.multiple_of((z_from * n_h + h_from) * rows, rows)
+            tokens_ref[pl.ds(place, rows), :] = block_ref[group * rows : (group + 1) * rows, :]
+    part = 256
+    for at in range(0, tokens_ref.shape[0], part):
+        out_ref[at : at + part, :] = jnp.dot(
+            tokens_ref[at : at + part, :], weight_ref[...], preferred_element_type=jnp.float32
+        ).astype(jnp.bfloat16)
+
+
+def product(at, places, blocks, weight, n_z, n_h):
+    depth, width = weight.shape
+    count = sum(block.shape[0] for block in blocks)
+    vmem = pl.BlockSpec(memory_space=pltpu.VMEM)
+    return pl.pallas_call(
+        functools.partial(product_kernel, n_z, n_h, count // (n_z * n_h), places),
+        out_shape=jax.ShapeDtypeStruct((count, width), jnp.bfloat16),
+        in_specs=[pl.BlockSpec(memory_space=pltpu.SMEM)] + [vmem] * (len(blocks) + 1),
+        out_specs=vmem,
+        scratch_shapes=[pltpu.VMEM((count, depth), jnp.bfloat16)],
+        compiler_params=pltpu.CompilerParams(vmem_limit_bytes=16 << 20),
+        cost_estimate=pl.CostEstimate(
+            flops=2 * count * depth * width,
+            bytes_accessed=2 * (count * depth + depth * width + count * width),
+            transcendentals=0,
+        ),
+        name="product",
+    )(at, *blocks, weight)
+
+
+def rings(leading, trailing, weight, n_z):
+    up = [(i, (i + 1) % n_z) for i in range(n_z)]
+    down = [(i, (i - 1) % n_z) for i in range(n_z)]
+    rows = leading.shape[0] // 2
+    steps = n_z // 2
+
+    def advance(pair, step):
+        below, above = pair
+        if step == steps:
+            below, above = below[:rows], above[rows:]
+        return lax.ppermute(below, "z", up), lax.ppermute(above, "z", down)
+
+    lead, trail = [(leading, leading)], [(trailing, trailing)]
+    for step in range(1, steps + 1):
+        if step > 2:
+            also = (weight,) if step == steps else ()
+            tied = lax.optimization_barrier(lead[-1] + trail[-1] + also)
+            lead[-1], trail[-1] = tied[:2], tied[2:4]
+            weight = tied[4] if also else weight
+        lead.append(advance(lead[-1], step))
+        if step < steps - 1:
+            trail.append(advance(trail[-1], step))
+    trail.append(advance(trail[-1], steps - 1))
+    tied = lax.optimization_barrier(lead[-1] + trail[-1])
+    lead[-1], trail[-1] = tied[:2], tied[2:]
+    trail.append(advance(trail[-1], steps))
+    places = [(0, 0)]
+    for step in range(1, steps + 1):
+        places += [(n_z - step, 0), (step, 2 if step == steps else 0)]
+    leading_blocks = [leading] + [block for pair in lead[1:] for block in pair]
+    trailing_blocks = [trailing] + [block for pair in trail[1:] for block in pair]
+    return tuple(places), leading_blocks, trailing_blocks, weight
 
 
 def body(old_codes, old_scales, gate_pre, up_pre):
@@ -113,12 +184,20 @@
     hidden = (jax.nn.silu(gate_pre.astype(jnp.float32)) * up_pre.astype(jnp.float32)).astype(
         jnp.bfloat16
     )
+    n_z = lax.axis_size("z")
+    n_h = lax.axis_size("h")
+    at = jnp.stack([lax.axis_index("z"), lax.axis_index("h")]).astype(jnp.int32)
     half = hidden.shape[0] // 2
-    first = lax.all_gather(hidden[:half], FSDP, axis=0, tiled=True)
+    beside = [hidden]
+    for step in range(1, n_h):
+        pairs = [(i, (i - step) % n_h) for i in range(n_h)]
+        beside.append(lax.ppermute(hidden, "h", pairs))
+    halves = [
+        jnp.concatenate([block[part * half : (part + 1) * half] for block in beside])
+        for part in range(2)
+    ]
     packed = pack(old_codes, n_fsdp)
     packed_rows = packed.shape[1]
-    near = lax.all_gather(hidden[half:], "h", axis=0, tiled=True)
-    second = lax.all_gather(near, "z", axis=0, tiled=True)
 
     sectioned = lax.all_to_all(packed, FSDP, split_axis=0, concat_axis=0, tiled=True)
     moved = lax.all_to_all(
@@ -137,9 +216,10 @@
     codes_t = new_codes.T
     scales_t = new_scale[:, :col_tiles].T
 
+    places, blocks_one, blocks_two, weight = rings(halves[0], halves[1], weight, n_z)
     pieces = []
-    for tokens in (first, second):
-        share = jnp.dot(tokens, weight, preferred_element_type=jnp.float32).astype(jnp.bfloat16)
+    for blocks in (blocks_one, blocks_two):
+        share = product(at, places, blocks, weight, n_z, n_h)
         shares = lax.all_to_all(share, TENSOR, split_axis=0, concat_axis=0, tiled=True)
         total = jnp.sum(
             shares.reshape(n_tensor, per_owner, half, col_width).astype(jnp.float32), axis=0

time: 251 us -> 220 us (0.88)
  waiting for transfers between devices: 160 us -> 84 us
  starting transfers between devices: 34.5 us -> 101 us
  blocking collectives: 17 us -> 0 us
  between operations: 14.1 us -> 1.06 us
  local copies, waits for them, and re-layouts: 5.64 us -> 16.3 us
  matrix products: 10.5 us -> 0 us
  Pallas kernels: 5.23 us -> 13.7 us
    all_gather x2 -> x0, waiting for transfers between devices: 79.9 us -> none  [the longest x1 79.9 us: body(): first = lax.all_gather(hidden[:half], FSDP, axis=0, tiled=True)]
    ppermute x0 -> x19, starting transfers between devices: none -> 61.4 us  [the longest x16 47 us: advance(): return (lax.ppermute(below, 'z', up), lax.ppermute(above, 'z', down))]
    ppermute x0 -> x19, waiting for transfers between devices: none -> 31.2 us  [the longest x16 31.2 us: advance(): return (lax.ppermute(below, 'z', up), lax.ppermute(above, 'z', down))]
    all_to_all x1, waiting for transfers between devices: 22.1 us -> 0.01 us  [body(): lax.all_to_all(sectioned.reshape(n_tensor, per_owner * packed_rows, TILE)...]
    all_gather x1 -> x0, blocking collectives: 17 us -> none  [body(): near = lax.all_gather(hidden[half:], 'h', axis=0, tiled=True)]
    dot_general x2 -> x0, matrix products: 10.5 us -> none  [body(): jnp.dot(tokens, weight, preferred_element_type=jnp.float32)]
    unnamed x8 -> x48, local copies, waits for them, and re-layouts: 4.2 us -> 13.5 us
    pallas_call x0 -> x2, Pallas kernels: none -> 8.47 us  [product(): pl.pallas_call(functools.partial(product_kernel, n_z, n_h, count // (n_z...]
  transfers between devices with their start and end apart: 6 -> 23, of which waited for: 4 -> 14; matrix products, arithmetic and copies ran while one was open for 6% -> 3% of each run, Pallas kernels for 2% -> 3%
where the time goes in v3:
time: 220 us; the launch traced here: 219 us
  starting transfers between devices  101 us (46%)
  waiting for transfers between devices  84 us (38%)
  local copies, waits for them, and re-layouts  16.3 us (7%)
  Pallas kernels  13.7 us (6%)
  other arithmetic  2.48 us (1%)
    ppermute x16, starting transfers between devices, advance(): return (lax.ppermute(below, 'z', up), lax.ppermute(above, 'z', down))  47 us
    all_to_all x1, waiting for transfers between devices, body(): lax.all_to_all(packed, FSDP, split_axis=0, concat_axis=0, tiled=True)  41.3 us
    ppermute x16, waiting for transfers between devices, advance(): return (lax.ppermute(below, 'z', up), lax.ppermute(above, 'z', down))  31.2 us
    all_to_all x2, starting transfers between devices, body(): lax.all_to_all(share, TENSOR, split_axis=0, concat_axis=0, tiled=True)  18 us
    all_to_all x1, starting transfers between devices, body(): lax.all_to_all(packed, FSDP, split_axis=0, concat_axis=0, tiled=True)  16.8 us
    ppermute x3, starting transfers between devices, body(): beside.append(lax.ppermute(hidden, 'h', pairs))  14.4 us
    unnamed x48, local copies, waits for them, and re-layouts  13.5 us
    all_to_all x2, waiting for transfers between devices, body(): lax.all_to_all(share, TENSOR, split_axis=0, concat_axis=0, tiled=True)  11.4 us
  transfers between devices with their start and end apart: 23, of which 14 were waited for; matrix products, arithmetic and copies ran while one was open for 3% of the time, Pallas kernels for 3%

profile of v3, /device:TPU:1, one launch (start us, length us, event | category | flops | bytes accessed | tf_op | source)
XLA Modules:
  0.0 219.0 jit_solution(13005271401327138780)
XLA Ops:
  4.1 16.8 %all-to-all-start = ((bf16[32,208,128]{2,1,0:T(8,128)(2,1)}), bf16[32,208,128]{2,1,0:T(8,128)(2,1)}, u32[]{:S(2)}, u32[]{:S(2)}) async-start(bf16[32,208,128]{2,1,0:T(8,128)(2,1)} %pack.1), calls=%async_computation | async-start | bytes 3407872 | tf_op jit(solution)/shard_map/all_to_all | solution.py:202
  21.0 4.0 %collective-permute-start.2 = (bf16[64,1664]{1,0:T(8,128)(2,1)S(1)}, bf16[64,1664]{1,0:T(8,128)(2,1)S(1)}, u32[]{:S(2)}, u32[]{:S(2)}) collective-permute-start(bf16[64,1664]{1,0:T(8,128)(2,1)S(1)} %fusion.4), channel_id=1, source_target_pairs={{0,16},{16,32},{32,48},{48,0},{1,17},{17,33},{33,49},{49,1},{2,18}... | collective-permute-start | bytes 638984 | tf_op jit(solution)/shard_map/ppermute | solution.py:194
  25.0 5.2 %collective-permute-start.1 = (bf16[64,1664]{1,0:T(8,128)(2,1)S(1)}, bf16[64,1664]{1,0:T(8,128)(2,1)S(1)}, u32[]{:S(2)}, u32[]{:S(2)}) collective-permute-start(bf16[64,1664]{1,0:T(8,128)(2,1)S(1)} %fusion.4), channel_id=1, source_target_pairs={{0,32},{16,48},{32,0},{48,16},{1,33},{17,49},{33,1},{49,17},{2,34}... | collective-permute-start | bytes 638984 | tf_op jit(solution)/shard_map/ppermute | solution.py:194
  30.2 5.2 %collective-permute-start = (bf16[64,1664]{1,0:T(8,128)(2,1)S(1)}, bf16[64,1664]{1,0:T(8,128)(2,1)S(1)}, u32[]{:S(2)}, u32[]{:S(2)}) collective-permute-start(bf16[64,1664]{1,0:T(8,128)(2,1)S(1)} %fusion.4), channel_id=1, source_target_pairs={{0,48},{16,0},{32,16},{48,32},{1,49},{17,1},{33,17},{49,33},{2,50}... | collective-permute-start | bytes 638984 | tf_op jit(solution)/shard_map/ppermute | solution.py:194
  35.4 41.3 %all-to-all-done = bf16[32,208,128]{2,1,0:T(8,128)(2,1)} async-done(((bf16[32,208,128]{2,1,0:T(8,128)(2,1)}), bf16[32,208,128]{2,1,0:T(8,128)(2,1)}, u32[]{:S(2)}, u32[]{:S(2)}) %all-to-all-start) | async-done | bytes 1703968 | tf_op jit(solution)/shard_map/all_to_all | solution.py:202
  76.7 5.2 %all-to-all-start.1 = ((bf16[16,416,128]{2,1,0:T(8,128)(2,1)}), bf16[16,416,128]{2,1,0:T(8,128)(2,1)S(1)}, u32[]{:S(2)}, u32[]{:S(2)}) async-start(bf16[16,416,128]{2,1,0:T(8,128)(2,1)} %bitcast.2), calls=%async_computation.1 | async-start | bytes 3407872 | tf_op jit(solution)/shard_map/all_to_all | solution.py:203
  82.1 2.9 %collective-permute-start.9 = (bf16[128,1664]{1,0:T(8,128)(2,1)S(1)}, bf16[128,1664]{1,0:T(8,128)(2,1)S(1)}, u32[]{:S(2)}, u32[]{:S(2)}) collective-permute-start(bf16[128,1664]{1,0:T(8,128)(2,1)S(1)} %pad_maximum_fusion.1.refs_0_), channel_id=1, source_target_pairs={{0,448},{64,0},{128,64},{192,128},{256,192},{320,256},{384,320},{4... | collective-permute-start | bytes 1277960 | tf_op jit(solution)/shard_map/ppermute | solution.py:149
  85.0 2.4 %collective-permute-start.7 = (bf16[128,1664]{1,0:T(8,128)(2,1)S(1)}, bf16[128,1664]{1,0:T(8,128)(2,1)S(1)}, u32[]{:S(2)}, u32[]{:S(2)}) collective-permute-start(bf16[128,1664]{1,0:T(8,128)(2,1)S(1)} %pad_maximum_fusion.1.refs_0_), channel_id=1, source_target_pairs={{0,64},{64,128},{128,192},{192,256},{256,320},{320,384},{384,448},... | collective-permute-start | bytes 1277960 | tf_op jit(solution)/shard_map/ppermute | solution.py:149
  88.2 4.1 %collective-permute-start.4 = (bf16[128,1664]{1,0:T(8,128)(2,1)S(1)}, bf16[128,1664]{1,0:T(8,128)(2,1)S(1)}, u32[]{:S(2)}, u32[]{:S(2)}) collective-permute-start(bf16[128,1664]{1,0:T(8,128)(2,1)S(1)} %pad_maximum_fusion.refs_0_), channel_id=1, source_target_pairs={{0,448},{64,0},{128,64},{192,128},{256,192},{320,256},{384,320},{4... | collective-permute-start | bytes 1277960 | tf_op jit(solution)/shard_map/ppermute | solution.py:149
  95.3 4.2 %collective-permute-start.10 = (bf16[128,1664]{1,0:T(8,128)(2,1)S(1)}, bf16[128,1664]{1,0:T(8,128)(2,1)S(1)}, u32[]{:S(2)}, u32[]{:S(2)}) collective-permute-start(bf16[128,1664]{1,0:T(8,128)(2,1)S(1)} %collective-permute-done.9.refs_2_), channel_id=1, source_target_pairs={{0,448},{64,0},{128,64},{192,128},{256,192},{320,256},{384,320},{4... | collective-permute-start | bytes 1277960 | tf_op jit(solution)/shard_map/ppermute | solution.py:149
  104.5 3.1 %collective-permute-start.6 = (bf16[128,1664]{1,0:T(8,128)(2,1)S(1)}, bf16[128,1664]{1,0:T(8,128)(2,1)}, u32[]{:S(2)}, u32[]{:S(2)}) collective-permute-start(bf16[128,1664]{1,0:T(8,128)(2,1)S(1)} %collective-permute-done.4.refs_2_), channel_id=1, source_target_pairs={{0,448},{64,0},{128,64},{192,128},{256,192},{320,256},{384,320},{4... | collective-permute-start | bytes 1277960 | tf_op jit(solution)/shard_map/ppermute | solution.py:149
  108.4 2.1 collective-permute-start.5
  111.3 2.3 %collective-permute-done.10.refs_4_ = bf16[128,1664]{1,0:T(8,128)(2,1)S(1)} collective-permute-done((bf16[128,1664]{1,0:T(8,128)(2,1)S(1)}, bf16[128,1664]{1,0:T(8,128)(2,1)S(1)}, u32[]{:S(2)}, u32[]{:S(2)}) %collective-permute-start.10) | collective-permute-done | bytes 426016 | tf_op jit(solution)/shard_map/ppermute | solution.py:149
  113.6 2.8 %collective-permute-done.8.refs_3_ = bf16[128,1664]{1,0:T(8,128)(2,1)S(1)} collective-permute-done((bf16[128,1664]{1,0:T(8,128)(2,1)S(1)}, bf16[128,1664]{1,0:T(8,128)(2,1)S(1)}, u32[]{:S(2)}, u32[]{:S(2)}) %collective-permute-start.8) | collective-permute-done | bytes 426016 | tf_op jit(solution)/shard_map/ppermute | solution.py:149
  116.5 6.4 %collective-permute-done.6.refs_4_ = bf16[128,1664]{1,0:T(8,128)(2,1)} collective-permute-done((bf16[128,1664]{1,0:T(8,128)(2,1)S(1)}, bf16[128,1664]{1,0:T(8,128)(2,1)}, u32[]{:S(2)}, u32[]{:S(2)}) %collective-permute-start.6) | collective-permute-done | bytes 426016 | tf_op jit(solution)/shard_map/ppermute | solution.py:149
  122.8 2.8 %collective-permute-done.5.refs_3_ = bf16[128,1664]{1,0:T(8,128)(2,1)} collective-permute-done((bf16[128,1664]{1,0:T(8,128)(2,1)S(1)}, bf16[128,1664]{1,0:T(8,128)(2,1)}, u32[]{:S(2)}, u32[]{:S(2)}) %collective-permute-start.5) | collective-permute-done | bytes 426016 | tf_op jit(solution)/shard_map/ppermute | solution.py:149
  127.6 4.6 %collective-permute-start.12 = (bf16[128,1664]{1,0:T(8,128)(2,1)}, bf16[128,1664]{1,0:T(8,128)(2,1)}, u32[]{:S(2)}, u32[]{:S(2)}) collective-permute-start(bf16[128,1664]{1,0:T(8,128)(2,1)} %collective-permute-done.6.refs_4_), channel_id=1, source_target_pairs={{0,448},{64,0},{128,64},{192,128},{256,192},{320,256},{384,320},{4... | collective-permute-start | bytes 1277960 | tf_op jit(solution)/shard_map/ppermute | solution.py:149
  133.0 3.3 %requantize.1 = (bf16[1664,512]{1,0:T(8,128)(2,1)S(1)}, bf16[1664,512]{1,0:T(8,128)(2,1)S(1)}, f32[13,128]{1,0:T(8,128)S(1)}) custom-call(f32[13,4]{1,0:T(8,128)S(1)} %dynamic_slice.3.scale_ref, bf16[16,2,208,128]{3,2,1,0:T(8,128)(2,1)S(1)} %bitcast.12), custom_call_target="tpu_custom_call" | custom-call | tf_op jit(solution)/shard_map/requantize/pallas_call | solution.py:86
  139.2 2.8 %collective-permute-start.15 = (bf16[128,1664]{1,0:T(8,128)(2,1)S(1)}, bf16[128,1664]{1,0:T(8,128)(2,1)S(1)}, u32[]{:S(2)}, u32[]{:S(2)}) collective-permute-start(bf16[128,1664]{1,0:T(8,128)(2,1)S(1)} %copy-done.15), channel_id=1, source_target_pairs={{0,64},{64,128},{128,192},{192,256},{256,320},{320,384},{384,448},... | collective-permute-start | bytes 1277960 | tf_op jit(solution)/shard_map/ppermute | solution.py:149
  142.0 4.4 %collective-permute-start.16 = (bf16[128,1664]{1,0:T(8,128)(2,1)S(1)}, bf16[128,1664]{1,0:T(8,128)(2,1)S(1)}, u32[]{:S(2)}, u32[]{:S(2)}) collective-permute-start(bf16[128,1664]{1,0:T(8,128)(2,1)S(1)} %copy-done.12), channel_id=1, source_target_pairs={{0,448},{64,0},{128,64},{192,128},{256,192},{320,256},{384,320},{4... | collective-permute-start | bytes 1277960 | tf_op jit(solution)/shard_map/ppermute | solution.py:149
  148.3 3.4 %collective-permute-start.14 = (bf16[64,1664]{1,0:T(8,128)(2,1)S(1)}, bf16[64,1664]{1,0:T(8,128)(2,1)S(1)}, u32[]{:S(2)}, u32[]{:S(2)}) collective-permute-start(bf16[64,1664]{1,0:T(8,128)(2,1)S(1)} %slice.48), channel_id=1, source_target_pairs={{0,448},{64,0},{128,64},{192,128},{256,192},{320,256},{384,320},{4... | collective-permute-start | bytes 638984 | tf_op jit(solution)/shard_map/ppermute | solution.py:149
  153.7 3.9 %collective-permute-done.14.refs_8_ = bf16[64,1664]{1,0:T(8,128)(2,1)S(1)} collective-permute-done((bf16[64,1664]{1,0:T(8,128)(2,1)S(1)}, bf16[64,1664]{1,0:T(8,128)(2,1)S(1)}, u32[]{:S(2)}, u32[]{:S(2)}) %collective-permute-start.14) | collective-permute-done | bytes 213024 | tf_op jit(solution)/shard_map/ppermute | solution.py:149
  159.5 4.7 %product.2 = bf16[1024,512]{1,0:T(8,128)(2,1)} custom-call(s32[2]{0:T(128)S(1)} %pad_add_fusion.at_ref, bf16[128,1664]{1,0:T(8,128)(2,1)S(1)} %copy-done.4, bf16[128,1664]{1,0:T(8,128)(2,1)S(1)} %copy-done.20, bf16[128,1664]{1,0:T(8,128)(2,1)S(1)} %copy-done.18, bf16[128,1664]{1,0:T(8,128)(2,1)} %collective-permute-done.5.refs_3_, ...), custom_call_target="tpu_custom_call" | custom-call | flops 1744830464 | bytes 6160384 | tf_op jit(solution)/shard_map/product/pallas_call | solution.py:123
  164.2 11.5 %all-to-all-start.2 = ((bf16[16,64,512]{2,1,0:T(8,128)(2,1)}), bf16[16,64,512]{2,1,0:T(8,128)(2,1)}, u32[]{:S(2)}, u32[]{:S(2)}) async-start(bf16[16,64,512]{2,1,0:T(8,128)(2,1)} %bitcast.4), calls=%async_computation.2 | async-start | bytes 2097152 | tf_op jit(solution)/shard_map/all_to_all | solution.py:223
  175.7 2.1 collective-permute-start.18
  177.9 3.2 %collective-permute-start.17 = (bf16[64,1664]{1,0:T(8,128)(2,1)S(1)}, bf16[64,1664]{1,0:T(8,128)(2,1)S(1)}, u32[]{:S(2)}, u32[]{:S(2)}) collective-permute-start(bf16[64,1664]{1,0:T(8,128)(2,1)S(1)} %slice.49), channel_id=1, source_target_pairs={{0,64},{64,128},{128,192},{192,256},{256,320},{320,384},{384,448},... | collective-permute-start | bytes 638984 | tf_op jit(solution)/shard_map/ppermute | solution.py:149
  181.0 3.4 %collective-permute-done.18.refs_8_ = bf16[64,1664]{1,0:T(8,128)(2,1)S(1)} collective-permute-done((bf16[64,1664]{1,0:T(8,128)(2,1)S(1)}, bf16[64,1664]{1,0:T(8,128)(2,1)S(1)}, u32[]{:S(2)}, u32[]{:S(2)}) %collective-permute-start.18) | collective-permute-done | bytes 213024 | tf_op jit(solution)/shard_map/ppermute | solution.py:149
  184.4 3.0 %collective-permute-done.17.refs_7_ = bf16[64,1664]{1,0:T(8,128)(2,1)S(1)} collective-permute-done((bf16[64,1664]{1,0:T(8,128)(2,1)S(1)}, bf16[64,1664]{1,0:T(8,128)(2,1)S(1)}, u32[]{:S(2)}, u32[]{:S(2)}) %collective-permute-start.17) | collective-permute-done | bytes 213024 | tf_op jit(solution)/shard_map/ppermute | solution.py:149
  192.0 3.8 %product.3 = bf16[1024,512]{1,0:T(8,128)(2,1)} custom-call(s32[2]{0:T(128)S(1)} %pad_add_fusion.at_ref, bf16[128,1664]{1,0:T(8,128)(2,1)S(1)} %copy-done.2, bf16[128,1664]{1,0:T(8,128)(2,1)S(1)} %copy-done.10, bf16[128,1664]{1,0:T(8,128)(2,1)S(1)} %copy-done.8, bf16[128,1664]{1,0:T(8,128)(2,1)S(1)} %copy-done.16, bf16[128,1664]{1,0:T(8,128)(2,1)S(1)} %copy-done.13, ...), custom_call_target="tpu_custom_call" | custom-call | flops 1744830464 | bytes 6160384 | tf_op jit(solution)/shard_map/product/pallas_call | solution.py:123
  195.8 6.5 %all-to-all-start.3 = ((bf16[16,64,512]{2,1,0:T(8,128)(2,1)}), bf16[16,64,512]{2,1,0:T(8,128)(2,1)S(1)}, u32[]{:S(2)}, u32[]{:S(2)}) async-start(bf16[16,64,512]{2,1,0:T(8,128)(2,1)} %bitcast.6), calls=%async_computation.3 | async-start | bytes 2097152 | tf_op jit(solution)/shard_map/all_to_all | solution.py:223
  202.3 2.3 %copy.7 = bf16[512,1664]{1,0:T(8,128)(2,1)} copy(bf16[512,1664]{0,1:T(8,128)(2,1)S(1)} %bitcast.13) | data formatting | bytes 3407872
  206.7 11.4 %all-to-all-done.3 = bf16[16,64,512]{2,1,0:T(8,128)(2,1)S(1)} async-done(((bf16[16,64,512]{2,1,0:T(8,128)(2,1)}), bf16[16,64,512]{2,1,0:T(8,128)(2,1)S(1)}, u32[]{:S(2)}, u32[]{:S(2)}) %all-to-all-start.3) | async-done | bytes 1048608 | tf_op jit(solution)/shard_map/all_to_all | solution.py:223
  (83 shorter events, 32.6 us)
Async XLA Ops:
  4.1 16.8 %copy-start.21 = (bf16[64,1664]{1,0:T(8,128)(2,1)S(1)}, bf16[64,1664]{1,0:T(8,128)(2,1)}, u32[]{:S(2)}) copy-start(bf16[64,1664]{1,0:T(8,128)(2,1)} %param.7) | copy-start | bytes 638980
  4.1 16.8 %copy-start.22 = (bf16[64,1664]{1,0:T(8,128)(2,1)S(1)}, bf16[64,1664]{1,0:T(8,128)(2,1)}, u32[]{:S(2)}) copy-start(bf16[64,1664]{1,0:T(8,128)(2,1)} %param.6) | copy-start | bytes 638980
  4.1 72.6 %all-to-all-start = ((bf16[32,208,128]{2,1,0:T(8,128)(2,1)}), bf16[32,208,128]{2,1,0:T(8,128)(2,1)}, u32[]{:S(2)}, u32[]{:S(2)}) async-start(bf16[32,208,128]{2,1,0:T(8,128)(2,1)} %pack.1), calls=%async_computation | async-start | bytes 3407872 | tf_op jit(solution)/shard_map/all_to_all | solution.py:202
  21.0 60.9 %collective-permute-start.2 = (bf16[64,1664]{1,0:T(8,128)(2,1)S(1)}, bf16[64,1664]{1,0:T(8,128)(2,1)S(1)}, u32[]{:S(2)}, u32[]{:S(2)}) collective-permute-start(bf16[64,1664]{1,0:T(8,128)(2,1)S(1)} %fusion.4), channel_id=1, source_target_pairs={{0,16},{16,32},{32,48},{48,0},{1,17},{17,33},{33,49},{49,1},{2,18}... | collective-permute-start | bytes 638984 | tf_op jit(solution)/shard_map/ppermute | solution.py:194
  25.0 57.0 %collective-permute-start.1 = (bf16[64,1664]{1,0:T(8,128)(2,1)S(1)}, bf16[64,1664]{1,0:T(8,128)(2,1)S(1)}, u32[]{:S(2)}, u32[]{:S(2)}) collective-permute-start(bf16[64,1664]{1,0:T(8,128)(2,1)S(1)} %fusion.4), channel_id=1, source_target_pairs={{0,32},{16,48},{32,0},{48,16},{1,33},{17,49},{33,1},{49,17},{2,34}... | collective-permute-start | bytes 638984 | tf_op jit(solution)/shard_map/ppermute | solution.py:194
  30.2 51.8 %collective-permute-start = (bf16[64,1664]{1,0:T(8,128)(2,1)S(1)}, bf16[64,1664]{1,0:T(8,128)(2,1)S(1)}, u32[]{:S(2)}, u32[]{:S(2)}) collective-permute-start(bf16[64,1664]{1,0:T(8,128)(2,1)S(1)} %fusion.4), channel_id=1, source_target_pairs={{0,48},{16,0},{32,16},{48,32},{1,49},{17,1},{33,17},{49,33},{2,50}... | collective-permute-start | bytes 638984 | tf_op jit(solution)/shard_map/ppermute | solution.py:194
  76.7 56.3 %all-to-all-start.1 = ((bf16[16,416,128]{2,1,0:T(8,128)(2,1)}), bf16[16,416,128]{2,1,0:T(8,128)(2,1)S(1)}, u32[]{:S(2)}, u32[]{:S(2)}) async-start(bf16[16,416,128]{2,1,0:T(8,128)(2,1)} %bitcast.2), calls=%async_computation.1 | async-start | bytes 3407872 | tf_op jit(solution)/shard_map/all_to_all | solution.py:203
  82.1 13.3 %collective-permute-start.9 = (bf16[128,1664]{1,0:T(8,128)(2,1)S(1)}, bf16[128,1664]{1,0:T(8,128)(2,1)S(1)}, u32[]{:S(2)}, u32[]{:S(2)}) collective-permute-start(bf16[128,1664]{1,0:T(8,128)(2,1)S(1)} %pad_maximum_fusion.1.refs_0_), channel_id=1, source_target_pairs={{0,448},{64,0},{128,64},{192,128},{256,192},{320,256},{384,320},{4... | collective-permute-start | bytes 1277960 | tf_op jit(solution)/shard_map/ppermute | solution.py:149
  85.0 15.3 %collective-permute-start.7 = (bf16[128,1664]{1,0:T(8,128)(2,1)S(1)}, bf16[128,1664]{1,0:T(8,128)(2,1)S(1)}, u32[]{:S(2)}, u32[]{:S(2)}) collective-permute-start(bf16[128,1664]{1,0:T(8,128)(2,1)S(1)} %pad_maximum_fusion.1.refs_0_), channel_id=1, source_target_pairs={{0,64},{64,128},{128,192},{192,256},{256,320},{320,384},{384,448},... | collective-permute-start | bytes 1277960 | tf_op jit(solution)/shard_map/ppermute | solution.py:149
  88.2 16.3 %collective-permute-start.4 = (bf16[128,1664]{1,0:T(8,128)(2,1)S(1)}, bf16[128,1664]{1,0:T(8,128)(2,1)S(1)}, u32[]{:S(2)}, u32[]{:S(2)}) collective-permute-start(bf16[128,1664]{1,0:T(8,128)(2,1)S(1)} %pad_maximum_fusion.refs_0_), channel_id=1, source_target_pairs={{0,448},{64,0},{128,64},{192,128},{256,192},{320,256},{384,320},{4... | collective-permute-start | bytes 1277960 | tf_op jit(solution)/shard_map/ppermute | solution.py:149
  92.3 16.1 %collective-permute-start.3 = (bf16[128,1664]{1,0:T(8,128)(2,1)S(1)}, bf16[128,1664]{1,0:T(8,128)(2,1)S(1)}, u32[]{:S(2)}, u32[]{:S(2)}) collective-permute-start(bf16[128,1664]{1,0:T(8,128)(2,1)S(1)} %pad_maximum_fusion.refs_0_), channel_id=1, source_target_pairs={{0,64},{64,128},{128,192},{192,256},{256,320},{320,384},{384,448},... | collective-permute-start | bytes 1277960 | tf_op jit(solution)/shard_map/ppermute | solution.py:149
  95.3 18.3 %collective-permute-start.10 = (bf16[128,1664]{1,0:T(8,128)(2,1)S(1)}, bf16[128,1664]{1,0:T(8,128)(2,1)S(1)}, u32[]{:S(2)}, u32[]{:S(2)}) collective-permute-start(bf16[128,1664]{1,0:T(8,128)(2,1)S(1)} %collective-permute-done.9.refs_2_), channel_id=1, source_target_pairs={{0,448},{64,0},{128,64},{192,128},{256,192},{320,256},{384,320},{4... | collective-permute-start | bytes 1277960 | tf_op jit(solution)/shard_map/ppermute | solution.py:149
  100.4 16.1 %collective-permute-start.8 = (bf16[128,1664]{1,0:T(8,128)(2,1)S(1)}, bf16[128,1664]{1,0:T(8,128)(2,1)S(1)}, u32[]{:S(2)}, u32[]{:S(2)}) collective-permute-start(bf16[128,1664]{1,0:T(8,128)(2,1)S(1)} %collective-permute-done.7.refs_1_), channel_id=1, source_target_pairs={{0,64},{64,128},{128,192},{192,256},{256,320},{320,384},{384,448},... | collective-permute-start | bytes 1277960 | tf_op jit(solution)/shard_map/ppermute | solution.py:149
  104.5 18.4 %collective-permute-start.6 = (bf16[128,1664]{1,0:T(8,128)(2,1)S(1)}, bf16[128,1664]{1,0:T(8,128)(2,1)}, u32[]{:S(2)}, u32[]{:S(2)}) collective-permute-start(bf16[128,1664]{1,0:T(8,128)(2,1)S(1)} %collective-permute-done.4.refs_2_), channel_id=1, source_target_pairs={{0,448},{64,0},{128,64},{192,128},{256,192},{320,256},{384,320},{4... | collective-permute-start | bytes 1277960 | tf_op jit(solution)/shard_map/ppermute | solution.py:149
  108.4 17.3 %collective-permute-start.5 = (bf16[128,1664]{1,0:T(8,128)(2,1)S(1)}, bf16[128,1664]{1,0:T(8,128)(2,1)}, u32[]{:S(2)}, u32[]{:S(2)}) collective-permute-start(bf16[128,1664]{1,0:T(8,128)(2,1)S(1)} %collective-permute-done.3.refs_1_), channel_id=1, source_target_pairs={{0,64},{64,128},{128,192},{192,256},{256,320},{320,384},{384,448},... | collective-permute-start | bytes 1277960 | tf_op jit(solution)/shard_map/ppermute | solution.py:149
  125.7 12.6 %collective-permute-start.11 = (bf16[128,1664]{1,0:T(8,128)(2,1)}, bf16[128,1664]{1,0:T(8,128)(2,1)}, u32[]{:S(2)}, u32[]{:S(2)}) collective-permute-start(bf16[128,1664]{1,0:T(8,128)(2,1)} %collective-permute-done.5.refs_3_), channel_id=1, source_target_pairs={{0,64},{64,128},{128,192},{192,256},{256,320},{320,384},{384,448},... | collective-permute-start | bytes 1277960 | tf_op jit(solution)/shard_map/ppermute | solution.py:149
  127.6 11.5 %collective-permute-start.12 = (bf16[128,1664]{1,0:T(8,128)(2,1)}, bf16[128,1664]{1,0:T(8,128)(2,1)}, u32[]{:S(2)}, u32[]{:S(2)}) collective-permute-start(bf16[128,1664]{1,0:T(8,128)(2,1)} %collective-permute-done.6.refs_4_), channel_id=1, source_target_pairs={{0,448},{64,0},{128,64},{192,128},{256,192},{320,256},{384,320},{4... | collective-permute-start | bytes 1277960 | tf_op jit(solution)/shard_map/ppermute | solution.py:149
  133.0 9.0 %copy-start.12 = (bf16[128,1664]{1,0:T(8,128)(2,1)S(1)}, bf16[128,1664]{1,0:T(8,128)(2,1)}, u32[]{:S(2)}) copy-start(bf16[128,1664]{1,0:T(8,128)(2,1)} %copy-done.11) | copy-start | bytes 1277956
  133.0 26.5 %copy-start.4 = (bf16[128,1664]{1,0:T(8,128)(2,1)S(1)}, bf16[128,1664]{1,0:T(8,128)(2,1)}, u32[]{:S(2)}) copy-start(bf16[128,1664]{1,0:T(8,128)(2,1)} %copy-done.3) | copy-start | bytes 1277956
  133.0 26.5 %copy-start.18 = (bf16[128,1664]{1,0:T(8,128)(2,1)S(1)}, bf16[128,1664]{1,0:T(8,128)(2,1)}, u32[]{:S(2)}) copy-start(bf16[128,1664]{1,0:T(8,128)(2,1)} %copy-done.17) | copy-start | bytes 1277956
  133.0 26.5 %copy-start.20 = (bf16[128,1664]{1,0:T(8,128)(2,1)S(1)}, bf16[128,1664]{1,0:T(8,128)(2,1)}, u32[]{:S(2)}) copy-start(bf16[128,1664]{1,0:T(8,128)(2,1)} %copy-done.19) | copy-start | bytes 1277956
  136.3 27.9 %copy-start.5 = (bf16[1664,512]{1,0:T(8,128)(2,1)}, bf16[1664,512]{1,0:T(8,128)(2,1)S(1)}, u32[]{:S(2)}) copy-start(bf16[1664,512]{1,0:T(8,128)(2,1)S(1)} %get-tuple-element.30.refs_9_) | copy-start | bytes 5111812
  139.2 20.3 %collective-permute-start.15 = (bf16[128,1664]{1,0:T(8,128)(2,1)S(1)}, bf16[128,1664]{1,0:T(8,128)(2,1)S(1)}, u32[]{:S(2)}, u32[]{:S(2)}) collective-permute-start(bf16[128,1664]{1,0:T(8,128)(2,1)S(1)} %copy-done.15), channel_id=1, source_target_pairs={{0,64},{64,128},{128,192},{192,256},{256,320},{320,384},{384,448},... | collective-permute-start | bytes 1277960 | tf_op jit(solution)/shard_map/ppermute | solution.py:149
  142.0 17.5 %collective-permute-start.16 = (bf16[128,1664]{1,0:T(8,128)(2,1)S(1)}, bf16[128,1664]{1,0:T(8,128)(2,1)S(1)}, u32[]{:S(2)}, u32[]{:S(2)}) collective-permute-start(bf16[128,1664]{1,0:T(8,128)(2,1)S(1)} %copy-done.12), channel_id=1, source_target_pairs={{0,448},{64,0},{128,64},{192,128},{256,192},{320,256},{384,320},{4... | collective-permute-start | bytes 1277960 | tf_op jit(solution)/shard_map/ppermute | solution.py:149
  148.3 9.2 %collective-permute-start.14 = (bf16[64,1664]{1,0:T(8,128)(2,1)S(1)}, bf16[64,1664]{1,0:T(8,128)(2,1)S(1)}, u32[]{:S(2)}, u32[]{:S(2)}) collective-permute-start(bf16[64,1664]{1,0:T(8,128)(2,1)S(1)} %slice.48), channel_id=1, source_target_pairs={{0,448},{64,0},{128,64},{192,128},{256,192},{320,256},{384,320},{4... | collective-permute-start | bytes 638984 | tf_op jit(solution)/shard_map/ppermute | solution.py:149
  151.7 7.8 %collective-permute-start.13 = (bf16[64,1664]{1,0:T(8,128)(2,1)S(1)}, bf16[64,1664]{1,0:T(8,128)(2,1)S(1)}, u32[]{:S(2)}, u32[]{:S(2)}) collective-permute-start(bf16[64,1664]{1,0:T(8,128)(2,1)S(1)} %slice.47), channel_id=1, source_target_pairs={{0,64},{64,128},{128,192},{192,256},{256,320},{320,384},{384,448},... | collective-permute-start | bytes 638984 | tf_op jit(solution)/shard_map/ppermute | solution.py:149
  164.2 23.3 %copy-start.2 = (bf16[128,1664]{1,0:T(8,128)(2,1)S(1)}, bf16[128,1664]{1,0:T(8,128)(2,1)}, u32[]{:S(2)}) copy-start(bf16[128,1664]{1,0:T(8,128)(2,1)} %copy-done.1) | copy-start | bytes 1277956
  164.2 23.3 %copy-start.8 = (bf16[128,1664]{1,0:T(8,128)(2,1)S(1)}, bf16[128,1664]{1,0:T(8,128)(2,1)}, u32[]{:S(2)}) copy-start(bf16[128,1664]{1,0:T(8,128)(2,1)} %copy-done.7) | copy-start | bytes 1277956
  164.2 31.6 %all-to-all-start.2 = ((bf16[16,64,512]{2,1,0:T(8,128)(2,1)}), bf16[16,64,512]{2,1,0:T(8,128)(2,1)}, u32[]{:S(2)}, u32[]{:S(2)}) async-start(bf16[16,64,512]{2,1,0:T(8,128)(2,1)} %bitcast.4), calls=%async_computation.2 | async-start | bytes 2097152 | tf_op jit(solution)/shard_map/all_to_all | solution.py:223
  175.7 8.7 %collective-permute-start.18 = (bf16[64,1664]{1,0:T(8,128)(2,1)S(1)}, bf16[64,1664]{1,0:T(8,128)(2,1)S(1)}, u32[]{:S(2)}, u32[]{:S(2)}) collective-permute-start(bf16[64,1664]{1,0:T(8,128)(2,1)S(1)} %slice.50), channel_id=1, source_target_pairs={{0,448},{64,0},{128,64},{192,128},{256,192},{320,256},{384,320},{4... | collective-permute-start | bytes 638984 | tf_op jit(solution)/shard_map/ppermute | solution.py:149
  177.9 9.6 %collective-permute-start.17 = (bf16[64,1664]{1,0:T(8,128)(2,1)S(1)}, bf16[64,1664]{1,0:T(8,128)(2,1)S(1)}, u32[]{:S(2)}, u32[]{:S(2)}) collective-permute-start(bf16[64,1664]{1,0:T(8,128)(2,1)S(1)} %slice.49), channel_id=1, source_target_pairs={{0,64},{64,128},{128,192},{192,256},{256,320},{320,384},{384,448},... | collective-permute-start | bytes 638984 | tf_op jit(solution)/shard_map/ppermute | solution.py:149
  195.8 22.4 %all-to-all-start.3 = ((bf16[16,64,512]{2,1,0:T(8,128)(2,1)}), bf16[16,64,512]{2,1,0:T(8,128)(2,1)S(1)}, u32[]{:S(2)}, u32[]{:S(2)}) async-start(bf16[16,64,512]{2,1,0:T(8,128)(2,1)} %bitcast.6), calls=%async_computation.3 | async-start | bytes 2097152 | tf_op jit(solution)/shard_map/all_to_all | solution.py:223
  (14 other events, 25.9 us)

commit v4 on v2

--- a/solution.py
+++ b/solution.py
@@ -1,3 +1,5 @@
+import functools
+
 import jax
 import jax.numpy as jnp
 from jax import lax
@@ -12,6 +14,8 @@
 FSDP = ("z", "h")
 TENSOR = ("x", "l", "c")
 PACK_STEPS = 4
+OUTER = 16
+INNER = 16
 
 
 def pack_kernel(in_ref, out_ref, scratch):
@@ -99,6 +103,50 @@
     )(scale_block, moved)
 
 
+def product_kernel(n_z, n_h, early_ref, late_ref, first_ref, weight_ref, out_ref):
+    sections = n_z * n_h
+    rows = out_ref.shape[0] // sections
+    outer = early_ref.shape[0] * 2 // sections
+    inner = rows - outer
+    for which, ref in enumerate((early_ref, late_ref)):
+        value = jnp.dot(ref[...], weight_ref[...], preferred_element_type=jnp.float32)
+        value = value.astype(jnp.bfloat16)
+        for h in range(n_h):
+            for z in range(n_z // 2):
+                at = ((which * (n_z // 2) + z) * n_h + h) * rows
+                source = (h * (n_z // 2) + z) * outer
+                out_ref[at : at + outer, :] = value[source : source + outer, :]
+    part = n_z // 2 * n_h * inner
+    for which in range(2):
+        value = jnp.dot(
+            first_ref[which * part : (which + 1) * part, :],
+            weight_ref[...],
+            preferred_element_type=jnp.float32,
+        ).astype(jnp.bfloat16)
+        for section in range(sections // 2):
+            at = (which * (sections // 2) + section) * rows + outer
+            out_ref[at : at + inner, :] = value[section * inner : (section + 1) * inner, :]
+
+
+def product(early, late, first, weight, n_z, n_h):
+    depth, width = weight.shape
+    count = early.shape[0] + late.shape[0] + first.shape[0]
+    vmem = pl.BlockSpec(memory_space=pltpu.VMEM)
+    return pl.pallas_call(
+        functools.partial(product_kernel, n_z, n_h),
+        out_shape=jax.ShapeDtypeStruct((count, width), jnp.bfloat16),
+        in_specs=[vmem] * 4,
+        out_specs=vmem,
+        compiler_params=pltpu.CompilerParams(vmem_limit_bytes=20 << 20),
+        cost_estimate=pl.CostEstimate(
+            flops=2 * count * depth * width,
+            bytes_accessed=2 * (count * depth + depth * width + count * width),
+            transcendentals=0,
+        ),
+        name="product",
+    )(early, late, first, weight)
+
+
 def body(old_codes, old_scales, gate_pre, up_pre):
     n_fsdp = lax.axis_size(FSDP)
     n_tensor = lax.axis_size(TENSOR)
@@ -113,14 +161,22 @@
     hidden = (jax.nn.silu(gate_pre.astype(jnp.float32)) * up_pre.astype(jnp.float32)).astype(
         jnp.bfloat16
     )
-    half = hidden.shape[0] // 2
-    first = lax.all_gather(hidden[:half], FSDP, axis=0, tiled=True)
+    n_z = lax.axis_size("z")
+    n_h = lax.axis_size("h")
     packed = pack(old_codes, n_fsdp)
     packed_rows = packed.shape[1]
-    near = lax.all_gather(hidden[half:], "h", axis=0, tiled=True)
-    second = lax.all_gather(near, "z", axis=0, tiled=True)
-
     sectioned = lax.all_to_all(packed, FSDP, split_axis=0, concat_axis=0, tiled=True)
+    near = lax.all_gather(hidden[OUTER:], "h", axis=0, tiled=True)
+    far = lax.all_gather(hidden[:OUTER], "z", axis=0, tiled=True)
+    parted = near.reshape(n_h, -1, own_rows)
+    one = parted[:, :INNER].reshape(-1, own_rows)
+    two = parted[:, INNER:].reshape(-1, own_rows)
+    one, two, far, sectioned = lax.optimization_barrier((one, two, far, sectioned))
+    first = lax.all_gather(one, "z", axis=0, tiled=True)
+    second = lax.all_gather(two, "z", axis=0, tiled=True)
+    middle = far.shape[0] // 2
+    early = lax.all_gather(far[:middle], "h", axis=0, tiled=True)
+    late = lax.all_gather(far[middle:], "h", axis=0, tiled=True)
     moved = lax.all_to_all(
         sectioned.reshape(n_tensor, per_owner * packed_rows, TILE),
         TENSOR,
@@ -128,6 +184,7 @@
         concat_axis=0,
         tiled=True,
     )
+    moved, early, late = lax.optimization_barrier((moved, early, late))
     scale_block = lax.dynamic_slice(
         old_scales, (t_index * row_tiles, f_index * col_tiles), (row_tiles, col_tiles)
     )
@@ -137,15 +194,14 @@
     codes_t = new_codes.T
     scales_t = new_scale[:, :col_tiles].T
 
-    pieces = []
-    for tokens in (first, second):
-        share = jnp.dot(tokens, weight, preferred_element_type=jnp.float32).astype(jnp.bfloat16)
+    def reduced(share):
         shares = lax.all_to_all(share, TENSOR, split_axis=0, concat_axis=0, tiled=True)
-        total = jnp.sum(
-            shares.reshape(n_tensor, per_owner, half, col_width).astype(jnp.float32), axis=0
-        )
-        pieces.append(total.astype(jnp.bfloat16))
-    mixed = jnp.stack(pieces, axis=1).reshape(per_owner * 2 * half, col_width)
+        total = jnp.sum(shares.reshape(n_tensor, -1, col_width).astype(jnp.float32), axis=0)
+        return total.astype(jnp.bfloat16).reshape(per_owner, -1, col_width)
+
+    lead = reduced(product(early, late, first, weight, n_z, n_h))
+    trail = reduced(jnp.dot(second, weight, preferred_element_type=jnp.float32).astype(jnp.bfloat16))
+    mixed = jnp.concatenate([lead, trail], axis=1).reshape(-1, col_width)
     return (mixed, codes_t, scales_t)
 
 

time: 251 us -> 244 us (0.972)
  waiting for transfers between devices: 160 us -> 23.2 us
  blocking collectives: 17 us -> 132 us
  starting transfers between devices: 34.5 us -> 45.2 us
  local copies, waits for them, and re-layouts: 5.64 us -> 13.3 us
  matrix products: 10.5 us -> 5.01 us
  Pallas kernels: 5.23 us -> 8.31 us
    all_gather x1 -> x4, blocking collectives: 17 us -> 132 us  [the longest x1 52.7 us: body(): near = lax.all_gather(hidden[OUTER:], 'h', axis=0, tiled=True)]
    all_gather x2, waiting for transfers between devices: 79.9 us -> 8.18 us  [the longest x1 8.18 us: body(): second = lax.all_gather(two, 'z', axis=0, tiled=True)]
    all_to_all x1, waiting for transfers between devices: 45.9 us -> 0.01 us  [body(): lax.all_to_all(packed, FSDP, split_axis=0, concat_axis=0, tiled=True)]
    all_to_all x1, waiting for transfers between devices: 22.1 us -> 0.01 us  [body(): lax.all_to_all(sectioned.reshape(n_tensor, per_owner * packed_rows, TILE)...]
    unnamed x8 -> x20, local copies, waits for them, and re-layouts: 4.2 us -> 10.9 us
    dot_general x2 -> x1, matrix products: 10.5 us -> 5.01 us  [body(): jnp.dot(second, weight, preferred_element_type=jnp.float32)]
    all_to_all x1, starting transfers between devices: 12.5 us -> 16.8 us  [body(): lax.all_to_all(packed, FSDP, split_axis=0, concat_axis=0, tiled=True)]
    all_to_all x1, starting transfers between devices: 9.83 us -> 13.5 us  [body(): lax.all_to_all(sectioned.reshape(n_tensor, per_owner * packed_rows, TILE)...]
  transfers between devices with their start and end apart: 6 -> 6, of which waited for: 4 -> 3; matrix products, arithmetic and copies ran while one was open for 6% -> 5% of each run, Pallas kernels for 2% -> 3%
where the time goes in v4:
time: 244 us
  blocking collectives  132 us (54%)
  starting transfers between devices  45.2 us (19%)
  waiting for transfers between devices  23.2 us (10%)
  between operations  14.1 us (6%)
  local copies, waits for them, and re-layouts  13.3 us (5%)
  Pallas kernels  8.31 us (3%)
  matrix products  5.01 us (2%)
    all_gather x1, blocking collectives, body(): near = lax.all_gather(hidden[OUTER:], 'h', axis=0, tiled=True)  52.7 us
    all_gather x1, blocking collectives, body(): early = lax.all_gather(far[:middle], 'h', axis=0, tiled=True)  38.6 us
    all_gather x1, blocking collectives, body(): far = lax.all_gather(hidden[:OUTER], 'z', axis=0, tiled=True)  23.5 us
    all_gather x1, blocking collectives, body(): late = lax.all_gather(far[middle:], 'h', axis=0, tiled=True)  17.3 us
    all_to_all x1, starting transfers between devices, body(): lax.all_to_all(packed, FSDP, split_axis=0, concat_axis=0, tiled=True)  16.8 us
    all_to_all x2, starting transfers between devices, reduced(): lax.all_to_all(share, TENSOR, split_axis=0, concat_axis=0, tiled=True)  14.8 us
    all_to_all x2, waiting for transfers between devices, reduced(): lax.all_to_all(share, TENSOR, split_axis=0, concat_axis=0, tiled=True)  14.3 us
    all_to_all x1, starting transfers between devices, body(): lax.all_to_all(sectioned.reshape(n_tensor, per_owner * packed_rows, TILE)...  13.5 us
  transfers between devices with their start and end apart: 6, of which 3 were waited for; matrix products, arithmetic and copies ran while one was open for 5% of the time, Pallas kernels for 3%

profile of v4, /device:TPU:1, one launch (start us, length us, event | category | flops | bytes accessed | tf_op | source)
XLA Modules:
  0.0 243.6 jit_solution(14007182828205141583)
XLA Ops:
  7.2 1.5 copy-done
  8.7 1.9 pack.1
  10.6 16.8 %all-to-all-start = ((bf16[32,208,128]{2,1,0:T(8,128)(2,1)}), bf16[32,208,128]{2,1,0:T(8,128)(2,1)}, u32[]{:S(2)}, u32[]{:S(2)}) async-start(bf16[32,208,128]{2,1,0:T(8,128)(2,1)} %pack.1), calls=%async_computation | async-start | bytes 3407872 | tf_op jit(solution)/shard_map/all_to_all | solution.py:168
  27.4 0.0 all-gather.3.cloned.1.call-start
  27.4 0.1 fusion.4
  27.6 52.7 %all_gather.18 = bf16[192,1664]{1,0:T(8,128)(2,1)S(1)} all-gather(bf16[48,1664]{1,0:T(8,128)(2,1)S(1)} %slice.28), channel_id=1, replica_groups=mesh['z'=8,'h'=4,'x'=4,'l'=2,'c'=2] {'h'}, dimensions={0}, use_global_device_ids=true | all-gather | bytes 798720 | tf_op jit(solution)/shard_map/all_gather | solution.py:169
  80.3 0.8 slice.30
  81.1 0.7 slice.29
  81.9 23.5 %all_gather.19 = bf16[128,1664]{1,0:T(8,128)(2,1)S(1)} all-gather(bf16[16,1664]{1,0:T(8,128)(2,1)S(1)} %slice.31), channel_id=1, replica_groups=mesh['z'=8,'h'=4,'x'=4,'l'=2,'c'=2] {'z'}, dimensions={0}, use_global_device_ids=true | all-gather | bytes 479232 | tf_op jit(solution)/shard_map/all_gather | solution.py:170
  105.5 0.7 all-gather.5.cloned.1.call-update
  106.2 13.5 %all-to-all-start.1 = ((bf16[16,416,128]{2,1,0:T(8,128)(2,1)}), bf16[16,416,128]{2,1,0:T(8,128)(2,1)S(1)}, u32[]{:S(2)}, u32[]{:S(2)}) async-start(bf16[16,416,128]{2,1,0:T(8,128)(2,1)} %bitcast.3), calls=%async_computation.1 | async-start | bytes 3407872 | tf_op jit(solution)/shard_map/all_to_all | solution.py:180
  119.7 0.8 dynamic_slice.3.scale_ref
  120.5 38.6 %all_gather.20.early_ref = bf16[256,1664]{1,0:T(8,128)(2,1)} all-gather(bf16[64,1664]{1,0:T(8,128)(2,1)S(1)} %get-tuple-element.27), channel_id=1, replica_groups=mesh['z'=8,'h'=4,'x'=4,'l'=2,'c'=2] {'h'}, dimensions={0}, use_global_device_ids=true | all-gather | bytes 1064960 | tf_op jit(solution)/shard_map/all_gather | solution.py:178
  159.1 17.3 %all_gather.21.late_ref = bf16[256,1664]{1,0:T(8,128)(2,1)} all-gather(bf16[64,1664]{1,0:T(8,128)(2,1)S(1)} %get-tuple-element.26), channel_id=1, replica_groups=mesh['z'=8,'h'=4,'x'=4,'l'=2,'c'=2] {'h'}, dimensions={0}, use_global_device_ids=true | all-gather | bytes 1064960 | tf_op jit(solution)/shard_map/all_gather | solution.py:179
  176.4 3.3 %requantize.1 = (bf16[1664,512]{1,0:T(8,128)(2,1)S(1)}, bf16[1664,512]{1,0:T(8,128)(2,1)S(1)}, f32[13,128]{1,0:T(8,128)S(1)}) custom-call(f32[13,4]{1,0:T(8,128)S(1)} %dynamic_slice.3.scale_ref, bf16[16,2,208,128]{3,2,1,0:T(8,128)(2,1)S(1)} %bitcast.15), custom_call_target="tpu_custom_call" | custom-call | tf_op jit(solution)/shard_map/requantize/pallas_call | solution.py:88
  179.7 1.2 copy-done.4
  180.9 1.2 copy-done.1
  182.1 1.2 copy-done.2
  183.2 1.5 copy-done.3
  184.7 1.5 copy-done.5
  186.1 3.1 %product.1 = bf16[1024,512]{1,0:T(8,128)(2,1)} custom-call(bf16[256,1664]{1,0:T(8,128)(2,1)S(1)} %copy-done.1, bf16[256,1664]{1,0:T(8,128)(2,1)S(1)} %copy-done.2, bf16[512,1664]{1,0:T(8,128)(2,1)S(1)} %copy-done.3, bf16[1664,512]{1,0:T(8,128)(2,1)S(1)} %copy-done.5), custom_call_target="tpu_custom_call" | custom-call | flops 1744830464 | bytes 6160384 | tf_op jit(solution)/shard_map/product/pallas_call | solution.py:135
  189.2 10.5 %all-to-all-start.2 = ((bf16[16,64,512]{2,1,0:T(8,128)(2,1)}), bf16[16,64,512]{2,1,0:T(8,128)(2,1)}, u32[]{:S(2)}, u32[]{:S(2)}) async-start(bf16[16,64,512]{2,1,0:T(8,128)(2,1)} %bitcast.5), calls=%async_computation.2 | async-start | bytes 2097152 | tf_op jit(solution)/shard_map/all_to_all | solution.py:198
  199.7 8.2 %all-gather.5.cloned.1.call-done = bf16[1024,1664]{1,0:T(8,128)(2,1)} async-done(((bf16[128,1664]{1,0:T(8,128)(2,1)}), bf16[1024,1664]{1,0:T(8,128)(2,1)}) %all-gather.5.cloned.1.call-update) | async-done | bytes 3407888 | tf_op jit(solution)/shard_map/all_gather | solution.py:176
  207.9 5.0 %convolution_convert_fusion = bf16[1024,512]{1,0:T(8,128)(2,1)} fusion(bf16[1024,1664]{1,0:T(8,128)(2,1)} %all-gather.5.cloned.1.call-done, bf16[1664,512]{1,0:T(8,128)(2,1)S(1)} %copy-done.6), kind=kOutput, calls=%fused_computation | convolution fusion | flops 1745354752 | bytes 6160384 | tf_op jit(solution)/shard_map/dot_general | solution.py:203
  212.9 2.7 %all-to-all-done.2 = bf16[16,64,512]{2,1,0:T(8,128)(2,1)} async-done(((bf16[16,64,512]{2,1,0:T(8,128)(2,1)}), bf16[16,64,512]{2,1,0:T(8,128)(2,1)}, u32[]{:S(2)}, u32[]{:S(2)}) %all-to-all-start.2) | async-done | bytes 1048608 | tf_op jit(solution)/shard_map/all_to_all | solution.py:198
  215.7 4.3 %all-to-all-start.3 = ((bf16[16,64,512]{2,1,0:T(8,128)(2,1)}), bf16[16,64,512]{2,1,0:T(8,128)(2,1)S(1)}, u32[]{:S(2)}, u32[]{:S(2)}) async-start(bf16[16,64,512]{2,1,0:T(8,128)(2,1)} %bitcast.20), calls=%async_computation.3 | async-start | bytes 2097152 | tf_op jit(solution)/shard_map/all_to_all | solution.py:198
  220.0 2.3 copy.7
  222.3 0.7 copy.8
  223.0 1.4 reduce_sum.24
  224.4 11.5 %all-to-all-done.3 = bf16[16,64,512]{2,1,0:T(8,128)(2,1)S(1)} async-done(((bf16[16,64,512]{2,1,0:T(8,128)(2,1)}), bf16[16,64,512]{2,1,0:T(8,128)(2,1)S(1)}, u32[]{:S(2)}, u32[]{:S(2)}) %all-to-all-start.3) | async-done | bytes 1048608 | tf_op jit(solution)/shard_map/all_to_all | solution.py:198
  235.9 0.1 reduce_sum.25
  236.1 0.7 pad_maximum_fusion
  (21 shorter events, 0.1 us)
Async XLA Ops:
  7.2 1.5 copy-start
  10.6 16.8 %copy-start.7 = (bf16[64,1664]{1,0:T(8,128)(2,1)S(1)}, bf16[64,1664]{1,0:T(8,128)(2,1)}, u32[]{:S(2)}) copy-start(bf16[64,1664]{1,0:T(8,128)(2,1)} %param.7) | copy-start | bytes 638980
  10.6 16.8 %copy-start.8 = (bf16[64,1664]{1,0:T(8,128)(2,1)S(1)}, bf16[64,1664]{1,0:T(8,128)(2,1)}, u32[]{:S(2)}) copy-start(bf16[64,1664]{1,0:T(8,128)(2,1)} %param.6) | copy-start | bytes 638980
  10.6 94.8 %all-to-all-start = ((bf16[32,208,128]{2,1,0:T(8,128)(2,1)}), bf16[32,208,128]{2,1,0:T(8,128)(2,1)}, u32[]{:S(2)}, u32[]{:S(2)}) async-start(bf16[32,208,128]{2,1,0:T(8,128)(2,1)} %pack.1), calls=%async_computation | async-start | bytes 3407872 | tf_op jit(solution)/shard_map/all_to_all | solution.py:168
  27.4 153.5 %all-gather.3.cloned.1.call-start = ((), (), s32[]{:S(2)}) async-start(), calls=%async_computation.4 | async-start | bytes 1916928 | tf_op jit(solution)/shard_map/all_gather | solution.py:175
  105.4 102.5 %all-gather.5.cloned.1.call-start = ((), (), s32[]{:S(2)}) async-start(), calls=%async_computation.5 | async-start | bytes 3833856 | tf_op jit(solution)/shard_map/all_gather | solution.py:176
  106.2 70.2 %all-to-all-start.1 = ((bf16[16,416,128]{2,1,0:T(8,128)(2,1)}), bf16[16,416,128]{2,1,0:T(8,128)(2,1)S(1)}, u32[]{:S(2)}, u32[]{:S(2)}) async-start(bf16[16,416,128]{2,1,0:T(8,128)(2,1)} %bitcast.3), calls=%async_computation.1 | async-start | bytes 3407872 | tf_op jit(solution)/shard_map/all_to_all | solution.py:180
  179.7 1.2 copy-start.4
  180.9 1.2 copy-start.1
  182.0 1.2 copy-start.2
  183.2 1.5 copy-start.3
  184.7 1.5 copy-start.5
  189.2 18.7 %copy-start.6 = (bf16[1664,512]{1,0:T(8,128)(2,1)S(1)}, bf16[1664,512]{1,0:T(8,128)(2,1)}, u32[]{:S(2)}) copy-start(bf16[1664,512]{1,0:T(8,128)(2,1)} %copy-done.4) | copy-start | bytes 5111812
  189.2 26.5 %all-to-all-start.2 = ((bf16[16,64,512]{2,1,0:T(8,128)(2,1)}), bf16[16,64,512]{2,1,0:T(8,128)(2,1)}, u32[]{:S(2)}, u32[]{:S(2)}) async-start(bf16[16,64,512]{2,1,0:T(8,128)(2,1)} %bitcast.5), calls=%async_computation.2 | async-start | bytes 2097152 | tf_op jit(solution)/shard_map/all_to_all | solution.py:198
  215.7 20.2 %all-to-all-start.3 = ((bf16[16,64,512]{2,1,0:T(8,128)(2,1)}), bf16[16,64,512]{2,1,0:T(8,128)(2,1)S(1)}, u32[]{:S(2)}, u32[]{:S(2)}) async-start(bf16[16,64,512]{2,1,0:T(8,128)(2,1)} %bitcast.20), calls=%async_computation.3 | async-start | bytes 2097152 | tf_op jit(solution)/shard_map/all_to_all | solution.py:198
Sparse Core Ops, SparseCore 0:
  105.5 47.2 all-gather.2
  154.9 52.9 all-gather.4

commit v5 on v2

--- a/solution.py
+++ b/solution.py
@@ -113,16 +113,23 @@
     hidden = (jax.nn.silu(gate_pre.astype(jnp.float32)) * up_pre.astype(jnp.float32)).astype(
         jnp.bfloat16
     )
-    half = hidden.shape[0] // 2
-    first = lax.all_gather(hidden[:half], FSDP, axis=0, tiled=True)
+    n_z = lax.axis_size("z")
+    n_h = lax.axis_size("h")
+    near = lax.all_gather(hidden, "h", axis=0, tiled=True)
     packed = pack(old_codes, n_fsdp)
     packed_rows = packed.shape[1]
-    near = lax.all_gather(hidden[half:], "h", axis=0, tiled=True)
-    second = lax.all_gather(near, "z", axis=0, tiled=True)
 
-    sectioned = lax.all_to_all(packed, FSDP, split_axis=0, concat_axis=0, tiled=True)
+    def swapped(sections, rows):
+        return jnp.swapaxes(sections.reshape(rows, -1, packed_rows, TILE), 0, 1).reshape(
+            n_fsdp, packed_rows, TILE
+        )
+
+    along_z = lax.all_to_all(packed, "z", split_axis=0, concat_axis=0, tiled=True)
+    near, along_z = lax.optimization_barrier((near, along_z))
+    every = lax.all_gather(near, "z", axis=0, tiled=True)
+    sectioned = lax.all_to_all(swapped(along_z, n_z), "h", split_axis=0, concat_axis=0, tiled=True)
     moved = lax.all_to_all(
-        sectioned.reshape(n_tensor, per_owner * packed_rows, TILE),
+        swapped(sectioned, n_h).reshape(n_tensor, per_owner * packed_rows, TILE),
         TENSOR,
         split_axis=0,
         concat_axis=0,
@@ -137,15 +144,18 @@
     codes_t = new_codes.T
     scales_t = new_scale[:, :col_tiles].T
 
-    pieces = []
-    for tokens in (first, second):
-        share = jnp.dot(tokens, weight, preferred_element_type=jnp.float32).astype(jnp.bfloat16)
-        shares = lax.all_to_all(share, TENSOR, split_axis=0, concat_axis=0, tiled=True)
-        total = jnp.sum(
-            shares.reshape(n_tensor, per_owner, half, col_width).astype(jnp.float32), axis=0
-        )
-        pieces.append(total.astype(jnp.bfloat16))
-    mixed = jnp.stack(pieces, axis=1).reshape(per_owner * 2 * half, col_width)
+    n_c = lax.axis_size("c")
+    core = lax.axis_index("c")
+    share = jnp.dot(every, weight, preferred_element_type=jnp.float32).astype(jnp.bfloat16)
+    by_core = share.reshape(n_tensor // n_c, n_c, -1, col_width)
+    other = lax.dynamic_index_in_dim(by_core, 1 - core, 1, keepdims=False)
+    other = lax.ppermute(other, "c", [(0, 1), (1, 0)])
+    own = lax.dynamic_index_in_dim(by_core, core, 1, keepdims=False)
+    share = (own.astype(jnp.float32) + other.astype(jnp.float32)).astype(jnp.bfloat16)
+    shares = lax.all_to_all(share, ("x", "l"), split_axis=0, concat_axis=0, tiled=True)
+    mixed = jnp.sum(
+        shares.reshape(n_tensor // n_c, -1, col_width).astype(jnp.float32), axis=0
+    ).astype(jnp.bfloat16)
     return (mixed, codes_t, scales_t)
 
 

time: 251 us -> 191 us (0.76)
  waiting for transfers between devices: 160 us -> 60.1 us
  blocking collectives: 17 us -> 67.1 us
  starting transfers between devices: 34.5 us -> 23.7 us
  local copies, waits for them, and re-layouts: 5.64 us -> 9.29 us
  matrix products: 10.5 us -> 7.37 us
    all_gather x2 -> x1, waiting for transfers between devices: 79.9 us -> 0.01 us  [body(): every = lax.all_gather(near, 'z', axis=0, tiled=True)]
    all_to_all x0 -> x1, blocking collectives: none -> 47.2 us  [body(): lax.all_to_all(swapped(along_z, n_z), 'h', split_axis=0, concat_axis=0, t...]
    all_to_all x4 -> x3, waiting for transfers between devices: 79.5 us -> 57.7 us  [the longest x1 23.2 us: body(): lax.all_to_all(packed, 'z', split_axis=0, concat_axis=0, tiled=True)]
    all_to_all x4 -> x3, starting transfers between devices: 34.4 us -> 20.9 us  [the longest x1 11 us: body(): lax.all_to_all(packed, 'z', split_axis=0, concat_axis=0, tiled=True)]
    dot_general x2 -> x1, matrix products: 10.5 us -> 7.37 us  [body(): jnp.dot(every, weight, preferred_element_type=jnp.float32)]
    convert_element_type x0 -> x1, other arithmetic: none -> 2.85 us  [body(): (own.astype(jnp.float32) + other.astype(jnp.float32)).astype(jnp.bfloat16)]
    all_gather x1, blocking collectives: 17 us -> 19.9 us  [body(): near = lax.all_gather(hidden, 'h', axis=0, tiled=True)]
    unnamed x8 -> x12, local copies, waits for them, and re-layouts: 4.2 us -> 7.01 us
  transfers between devices with their start and end apart: 6 -> 5, of which waited for: 4 -> 4; matrix products, arithmetic and copies ran while one was open for 6% -> 3% of each run, Pallas kernels for 2% -> 2%
where the time goes in v5:
time: 191 us
  blocking collectives  67.1 us (35%)
  waiting for transfers between devices  60.1 us (31%)
  starting transfers between devices  23.7 us (12%)
  between operations  14.1 us (7%)
  local copies, waits for them, and re-layouts  9.29 us (5%)
  matrix products  7.37 us (4%)
  Pallas kernels  5.21 us (3%)
  other arithmetic  3.8 us (2%)
    all_to_all x1, blocking collectives, body(): lax.all_to_all(swapped(along_z, n_z), 'h', split_axis=0, concat_axis=0, t...  47.2 us
    all_to_all x1, waiting for transfers between devices, body(): lax.all_to_all(packed, 'z', split_axis=0, concat_axis=0, tiled=True)  23.2 us
    all_to_all x1, waiting for transfers between devices, body(): lax.all_to_all(swapped(sectioned, n_h).reshape(n_tensor, per_owner * pack...  22.1 us
    all_gather x1, blocking collectives, body(): near = lax.all_gather(hidden, 'h', axis=0, tiled=True)  19.9 us
    all_to_all x1, waiting for transfers between devices, body(): lax.all_to_all(share, ('x', 'l'), split_axis=0, concat_axis=0, tiled=True)  12.4 us
    all_to_all x1, starting transfers between devices, body(): lax.all_to_all(packed, 'z', split_axis=0, concat_axis=0, tiled=True)  11 us
    dot_general x1, matrix products, body(): jnp.dot(every, weight, preferred_element_type=jnp.float32)  7.37 us
    unnamed x12, local copies, waits for them, and re-layouts  7.01 us
  transfers between devices with their start and end apart: 5, of which 4 were waited for; matrix products, arithmetic and copies ran while one was open for 3% of the time, Pallas kernels for 2%

profile of v5, /device:TPU:1, one launch (start us, length us, event | category | flops | bytes accessed | tf_op | source)
XLA Modules:
  0.0 190.7 jit_solution(17024319062201200871)
XLA Ops:
  7.2 0.0 copy-start
  7.2 1.5 copy-done
  8.7 1.9 %pack.1 = bf16[32,208,128]{2,1,0:T(8,128)(2,1)} custom-call(bf16[52,16384]{1,0:T(8,128)(2,1)S(1)} %copy-done), custom_call_target="tpu_custom_call" | custom-call | tf_op jit(solution)/shard_map/pack/pallas_call | solution.py:32
  10.6 11.0 %all-to-all-start = ((bf16[32,208,128]{2,1,0:T(8,128)(2,1)}), bf16[32,208,128]{2,1,0:T(8,128)(2,1)S(1)}, u32[]{:S(2)}, u32[]{:S(2)}) async-start(bf16[32,208,128]{2,1,0:T(8,128)(2,1)} %pack.1), calls=%async_computation | async-start | bytes 3407872 | tf_op jit(solution)/shard_map/all_to_all | solution.py:127
  21.6 0.0 all-gather.2.cloned.1.call-start
  21.6 0.0 copy-done.3
  21.7 0.0 copy-done.4
  21.7 0.1 fusion.5
  21.8 19.9 %all_gather.6 = bf16[256,1664]{1,0:T(8,128)(2,1)} all-gather(bf16[64,1664]{1,0:T(8,128)(2,1)S(1)} %fusion.5), channel_id=1, replica_groups=mesh['z'=8,'h'=4,'x'=4,'l'=2,'c'=2] {'h'}, dimensions={0}, use_global_device_ids=true | all-gather | bytes 1064960 | tf_op jit(solution)/shard_map/all_gather | solution.py:118
  41.7 23.2 %all-to-all-done = bf16[32,208,128]{2,1,0:T(8,128)(2,1)S(1)} async-done(((bf16[32,208,128]{2,1,0:T(8,128)(2,1)}), bf16[32,208,128]{2,1,0:T(8,128)(2,1)S(1)}, u32[]{:S(2)}, u32[]{:S(2)}) %all-to-all-start) | async-done | bytes 1703968 | tf_op jit(solution)/shard_map/all_to_all | solution.py:127
  64.8 0.0 all-gather.2.cloned.1.call-update
  64.9 0.1 copy.12
  65.0 47.2 %all_to_all.20 = bf16[32,208,128]{2,1,0:T(8,128)(2,1)S(1)} all-to-all(bf16[32,208,128]{2,1,0:T(8,128)(2,1)S(1)} %bitcast.23), channel_id=1, replica_groups=mesh['z'=8,'h'=4,'x'=4,'l'=2,'c'=2] {'h'}, dimensions={0} | all-to-all | bytes 3407872 | tf_op jit(solution)/shard_map/all_to_all | solution.py:130
  112.2 1.3 copy.13
  113.5 6.3 %all-to-all-start.2 = ((bf16[16,416,128]{2,1,0:T(8,128)(2,1)}), bf16[16,416,128]{2,1,0:T(8,128)(2,1)S(1)}, u32[]{:S(2)}, u32[]{:S(2)}) async-start(bf16[16,416,128]{2,1,0:T(8,128)(2,1)} %bitcast.5), calls=%async_computation.2 | async-start | bytes 3407872 | tf_op jit(solution)/shard_map/all_to_all | solution.py:131
  119.8 0.8 dynamic_slice.10.scale_ref
  120.6 22.1 %all-to-all-done.2 = bf16[16,416,128]{2,1,0:T(8,128)(2,1)S(1)} async-done(((bf16[16,416,128]{2,1,0:T(8,128)(2,1)}), bf16[16,416,128]{2,1,0:T(8,128)(2,1)S(1)}, u32[]{:S(2)}, u32[]{:S(2)}) %all-to-all-start.2) | async-done | bytes 1703968 | tf_op jit(solution)/shard_map/all_to_all | solution.py:131
  142.7 3.3 %requantize.1 = (bf16[1664,512]{1,0:T(8,128)(2,1)S(1)}, bf16[1664,512]{1,0:T(8,128)(2,1)S(1)}, f32[13,128]{1,0:T(8,128)S(1)}) custom-call(f32[13,4]{1,0:T(8,128)S(1)} %dynamic_slice.10.scale_ref, bf16[16,2,208,128]{3,2,1,0:T(8,128)(2,1)S(1)} %bitcast.20), custom_call_target="tpu_custom_call" | custom-call | tf_op jit(solution)/shard_map/requantize/pallas_call | solution.py:84
  146.0 0.0 copy-start.1
  146.0 1.2 copy-done.1
  147.2 7.4 %convolution_convert_fusion = bf16[2048,512]{1,0:T(8,128)(2,1)S(1)} fusion(bf16[2048,1664]{1,0:T(8,128)(2,1)} %all-gather.2.cloned.1.call-done, bf16[1664,512]{1,0:T(8,128)(2,1)} %copy-done.1), kind=kOutput, calls=%fused_computation | convolution fusion | flops 3490709504 | bytes 10616832 | tf_op jit(solution)/shard_map/dot_general | solution.py:149
  154.6 0.0 copy-start.2
  154.6 1.3 copy-done.2
  155.9 0.1 dynamic-slice_bitcast_fusion
  156.0 2.8 %collective-permute-start = (bf16[8,128,512]{2,1,0:T(8,128)(2,1)S(1)}, bf16[8,128,512]{2,1,0:T(8,128)(2,1)}, u32[]{:S(2)}, u32[]{:S(2)}) collective-permute-start(bf16[8,128,512]{2,1,0:T(8,128)(2,1)S(1)} %dynamic-slice_bitcast_fusion), channel_id=1, source_target_pairs={{0,1},{1,0},{2,3},{3,2},{4,5},{5,4},{6,7},{7,6},{8,9},{9,8},{10,11... | collective-permute-start | bytes 3145736 | tf_op jit(solution)/shard_map/ppermute | solution.py:152
  158.8 2.4 %collective-permute-done = bf16[8,128,512]{2,1,0:T(8,128)(2,1)} collective-permute-done((bf16[8,128,512]{2,1,0:T(8,128)(2,1)S(1)}, bf16[8,128,512]{2,1,0:T(8,128)(2,1)}, u32[]{:S(2)}, u32[]{:S(2)}) %collective-permute-start) | collective-permute-done | bytes 1048608 | tf_op jit(solution)/shard_map/ppermute | solution.py:152
  161.2 2.9 %fusion = bf16[8,128,512]{2,1,0:T(8,128)(2,1)} fusion(bf16[8,128,512]{2,1,0:T(8,128)(2,1)} %collective-permute-done, bf16[8,2,128,512]{3,2,1,0:T(8,128)(2,1)} %bitcast.26, s32[]{:T(128)S(6)} %select_n.15), kind=kLoop, calls=%fused_computation.2 | loop fusion | flops 2097152 | bytes 3145732 | tf_op jit(solution)/shard_map/convert_element_type | solution.py:154
  164.0 3.6 %all-to-all-start.3 = ((bf16[8,128,512]{2,1,0:T(8,128)(2,1)}), bf16[8,128,512]{2,1,0:T(8,128)(2,1)S(1)}, u32[]{:S(2)}, u32[]{:S(2)}) async-start(bf16[8,128,512]{2,1,0:T(8,128)(2,1)} %fusion), calls=%async_computation.3 | async-start | bytes 2097152 | tf_op jit(solution)/shard_map/all_to_all | solution.py:155
  167.6 2.3 %copy.14 = bf16[512,1664]{1,0:T(8,128)(2,1)} copy(bf16[512,1664]{0,1:T(8,128)(2,1)S(1)} %bitcast.21) | data formatting | bytes 3407872
  169.9 0.7 copy.15
  170.6 12.4 %all-to-all-done.3 = bf16[8,128,512]{2,1,0:T(8,128)(2,1)S(1)} async-done(((bf16[8,128,512]{2,1,0:T(8,128)(2,1)}), bf16[8,128,512]{2,1,0:T(8,128)(2,1)S(1)}, u32[]{:S(2)}, u32[]{:S(2)}) %all-to-all-start.3) | async-done | bytes 1048608 | tf_op jit(solution)/shard_map/all_to_all | solution.py:155
  183.0 0.8 reduce_sum.12
  (4 shorter events, 0.0 us)
Async XLA Ops:
  7.2 1.5 copy-start
  10.6 11.0 %copy-start.3 = (bf16[64,1664]{1,0:T(8,128)(2,1)S(1)}, bf16[64,1664]{1,0:T(8,128)(2,1)}, u32[]{:S(2)}) copy-start(bf16[64,1664]{1,0:T(8,128)(2,1)} %param.7) | copy-start | bytes 638980
  10.6 11.1 %copy-start.4 = (bf16[64,1664]{1,0:T(8,128)(2,1)S(1)}, bf16[64,1664]{1,0:T(8,128)(2,1)}, u32[]{:S(2)}) copy-start(bf16[64,1664]{1,0:T(8,128)(2,1)} %param.6) | copy-start | bytes 638980
  10.6 54.2 %all-to-all-start = ((bf16[32,208,128]{2,1,0:T(8,128)(2,1)}), bf16[32,208,128]{2,1,0:T(8,128)(2,1)S(1)}, u32[]{:S(2)}, u32[]{:S(2)}) async-start(bf16[32,208,128]{2,1,0:T(8,128)(2,1)} %pack.1), calls=%async_computation | async-start | bytes 3407872 | tf_op jit(solution)/shard_map/all_to_all | solution.py:127
  21.6 125.6 %all-gather.2.cloned.1.call-start = ((), (), s32[]{:S(2)}) async-start(), calls=%async_computation.4 | async-start | bytes 7667712 | tf_op jit(solution)/shard_map/all_gather | solution.py:129
  113.5 29.2 %all-to-all-start.2 = ((bf16[16,416,128]{2,1,0:T(8,128)(2,1)}), bf16[16,416,128]{2,1,0:T(8,128)(2,1)S(1)}, u32[]{:S(2)}, u32[]{:S(2)}) async-start(bf16[16,416,128]{2,1,0:T(8,128)(2,1)} %bitcast.5), calls=%async_computation.2 | async-start | bytes 3407872 | tf_op jit(solution)/shard_map/all_to_all | solution.py:131
  146.0 1.2 copy-start.1
  154.6 1.3 copy-start.2
  156.0 5.2 %collective-permute-start = (bf16[8,128,512]{2,1,0:T(8,128)(2,1)S(1)}, bf16[8,128,512]{2,1,0:T(8,128)(2,1)}, u32[]{:S(2)}, u32[]{:S(2)}) collective-permute-start(bf16[8,128,512]{2,1,0:T(8,128)(2,1)S(1)} %dynamic-slice_bitcast_fusion), channel_id=1, source_target_pairs={{0,1},{1,0},{2,3},{3,2},{4,5},{5,4},{6,7},{7,6},{8,9},{9,8},{10,11... | collective-permute-start | bytes 3145736 | tf_op jit(solution)/shard_map/ppermute | solution.py:152
  164.0 19.0 %all-to-all-start.3 = ((bf16[8,128,512]{2,1,0:T(8,128)(2,1)}), bf16[8,128,512]{2,1,0:T(8,128)(2,1)S(1)}, u32[]{:S(2)}, u32[]{:S(2)}) async-start(bf16[8,128,512]{2,1,0:T(8,128)(2,1)} %fusion), calls=%async_computation.3 | async-start | bytes 2097152 | tf_op jit(solution)/shard_map/all_to_all | solution.py:155
Sparse Core Ops, SparseCore 0:
  65.0 78.8 all-gather.1

commit v6 on v5

--- a/solution.py
+++ b/solution.py
@@ -1,3 +1,6 @@
+import itertools
+import math
+
 import jax
 import jax.numpy as jnp
 from jax import lax
@@ -36,26 +39,24 @@
         in_specs=[pl.BlockSpec((rows, width // PACK_STEPS), lambda i: (0, i))],
         out_specs=pl.BlockSpec((sections, packed_rows, TILE), lambda i: (i, 0, 0)),
         scratch_shapes=[pltpu.VMEM((packed_rows, TILE), jnp.float32)],
-        compiler_params=pltpu.CompilerParams(vmem_limit_bytes=12 << 20),
         name="pack",
     )(old_codes)
 
 
 def requantize_kernel(scale_ref, in_ref, codes_ref, weight_ref, new_scale_ref, rows_ref, piece_ref):
-    senders, parts, packed_rows, _ = in_ref.shape
+    *senders, packed_rows, _ = in_ref.shape
+    n_x, n_c, parts, n_l = senders
     total_rows, width = rows_ref.shape
     tiles = width // TILE
     rows = packed_rows // tiles
 
-    for part in range(parts):
-        for sender in range(senders):
-            slot = sender % 2
-            piece_ref[slot] = in_ref[sender, part].astype(jnp.float32)
-            base = (part * senders + sender) * rows
-            for tile in range(tiles):
-                rows_ref[pl.ds(base, rows), tile * TILE : (tile + 1) * TILE] = piece_ref[
-                    slot, pl.ds(tile * rows, rows), :
-                ]
+    for x, core, part, low in itertools.product(*map(range, senders)):
+        piece_ref[core] = in_ref[x, core, part, low].astype(jnp.float32)
+        base = (((part * n_x + x) * n_l + low) * n_c + core) * rows
+        for tile in range(tiles):
+            rows_ref[pl.ds(base, rows), tile * TILE : (tile + 1) * TILE] = piece_ref[
+                core, pl.ds(tile * rows, rows), :
+            ]
     lane = lax.broadcasted_iota(jnp.int32, (1, TILE), 1)
 
     def one_row(row, carry):
@@ -78,8 +79,8 @@
 
 
 def requantize(moved, scale_block, width):
-    senders, parts, packed_rows, _ = moved.shape
-    total_rows = senders * parts * packed_rows * TILE // width
+    *senders, packed_rows, _ = moved.shape
+    total_rows = math.prod(senders) * packed_rows * TILE // width
     vmem = pl.BlockSpec(memory_space=pltpu.VMEM)
     return pl.pallas_call(
         requantize_kernel,
@@ -97,6 +98,40 @@
         compiler_params=pltpu.CompilerParams(vmem_limit_bytes=20 << 20),
         name="requantize",
     )(scale_block, moved)
+
+
+def half_product_kernel(parity_ref, even_ref, odd_ref, weight_ref, out_ref):
+    tokens = jnp.concatenate([even_ref[...], odd_ref[...]], axis=0)
+    out_ref[...] = jnp.dot(
+        tokens, weight_ref[...], preferred_element_type=jnp.float32
+    ).astype(jnp.bfloat16)
+
+
+def half_product(every, weight, parity, owners):
+    depth, width = weight.shape
+    rows = every.shape[0] // owners
+    count = every.shape[0] // 2
+    return pl.pallas_call(
+        half_product_kernel,
+        out_shape=jax.ShapeDtypeStruct((count, width), jnp.bfloat16),
+        grid_spec=pltpu.PrefetchScalarGridSpec(
+            num_scalar_prefetch=1,
+            grid=(owners // 4,),
+            in_specs=[
+                pl.BlockSpec((rows, depth), lambda i, parity: (4 * i + parity[0], 0)),
+                pl.BlockSpec((rows, depth), lambda i, parity: (4 * i + 2 + parity[0], 0)),
+                pl.BlockSpec((depth, width), lambda i, parity: (0, 0), pipeline_mode=pl.Buffered(1)),
+            ],
+            out_specs=pl.BlockSpec((2 * rows, width), lambda i, parity: (i, 0)),
+        ),
+        compiler_params=pltpu.CompilerParams(vmem_limit_bytes=56 << 20),
+        cost_estimate=pl.CostEstimate(
+            flops=2 * count * depth * width,
+            bytes_accessed=2 * (count * depth + depth * width + count * width),
+            transcendentals=0,
+        ),
+        name="half_product",
+    )(parity, every, every, weight)
 
 
 def body(old_codes, old_scales, gate_pre, up_pre):
@@ -119,38 +154,31 @@
     packed = pack(old_codes, n_fsdp)
     packed_rows = packed.shape[1]
 
-    def swapped(sections, rows):
-        return jnp.swapaxes(sections.reshape(rows, -1, packed_rows, TILE), 0, 1).reshape(
-            n_fsdp, packed_rows, TILE
-        )
+    def reordered(sections, sizes, order):
+        parted = sections.reshape(*sizes, packed_rows, TILE)
+        return parted.transpose(*order, 4, 5).reshape(n_fsdp, packed_rows, TILE)
 
+    n_x, n_l, n_c = (lax.axis_size(name) for name in TENSOR)
     along_z = lax.all_to_all(packed, "z", split_axis=0, concat_axis=0, tiled=True)
     near, along_z = lax.optimization_barrier((near, along_z))
     every = lax.all_gather(near, "z", axis=0, tiled=True)
-    sectioned = lax.all_to_all(swapped(along_z, n_z), "h", split_axis=0, concat_axis=0, tiled=True)
-    moved = lax.all_to_all(
-        swapped(sectioned, n_h).reshape(n_tensor, per_owner * packed_rows, TILE),
-        TENSOR,
-        split_axis=0,
-        concat_axis=0,
-        tiled=True,
-    )
+    by_column = reordered(along_z, (1, n_z // n_l, n_l, n_h), (0, 3, 2, 1))
+    along_y = lax.all_to_all(by_column, ("h", "l"), split_axis=0, concat_axis=0, tiled=True)
+    by_owner = reordered(along_y, (n_c, n_h // n_c, n_l, n_z // n_l), (3, 0, 1, 2))
+    moved = lax.all_to_all(by_owner, ("x", "c"), split_axis=0, concat_axis=0, tiled=True)
     scale_block = lax.dynamic_slice(
         old_scales, (t_index * row_tiles, f_index * col_tiles), (row_tiles, col_tiles)
     )
     new_codes, weight, new_scale = requantize(
-        moved.reshape(n_tensor, per_owner, packed_rows, TILE), scale_block, col_width
+        moved.reshape(n_x, n_c, per_owner, n_l, packed_rows, TILE), scale_block, col_width
     )
     codes_t = new_codes.T
     scales_t = new_scale[:, :col_tiles].T
 
-    n_c = lax.axis_size("c")
-    core = lax.axis_index("c")
-    share = jnp.dot(every, weight, preferred_element_type=jnp.float32).astype(jnp.bfloat16)
-    by_core = share.reshape(n_tensor // n_c, n_c, -1, col_width)
-    other = lax.dynamic_index_in_dim(by_core, 1 - core, 1, keepdims=False)
+    core = lax.axis_index("c").astype(jnp.int32).reshape(1)
+    other = half_product(every, weight, 1 - core, n_tensor)
     other = lax.ppermute(other, "c", [(0, 1), (1, 0)])
-    own = lax.dynamic_index_in_dim(by_core, core, 1, keepdims=False)
+    own = half_product(every, weight, core, n_tensor)
     share = (own.astype(jnp.float32) + other.astype(jnp.float32)).astype(jnp.bfloat16)
     shares = lax.all_to_all(share, ("x", "l"), split_axis=0, concat_axis=0, tiled=True)
     mixed = jnp.sum(

time: 191 us -> 192 us (level)
  Pallas kernels: 5.21 us -> 18.5 us
  matrix products: 7.37 us -> 0 us
  local copies, waits for them, and re-layouts: 9.29 us -> 6.43 us
  waiting for transfers between devices: 60.1 us -> 57.4 us
    pallas_call x0 -> x2, Pallas kernels: none -> 11.4 us  [half_product(): pl.pallas_call(half_product_kernel, out_shape=jax.ShapeDtypeStruct((count...]
    dot_general x1 -> x0, matrix products: 7.37 us -> none  [body(): jnp.dot(every, weight, preferred_element_type=jnp.float32)]
    unnamed x12 -> x8, local copies, waits for them, and re-layouts: 7.01 us -> 4.2 us
    ppermute x1, waiting for transfers between devices: 2.4 us -> 0.01 us  [body(): other = lax.ppermute(other, 'c', [(0, 1), (1, 0)])]
  transfers between devices with their start and end apart: 5 -> 5, of which waited for: 4 -> 3; matrix products, arithmetic and copies ran while one was open for 3% -> 3% of each run, Pallas kernels for 2% -> 5%
where the time goes in v6:
time: 192 us
  blocking collectives  68.1 us (35%)
  waiting for transfers between devices  57.4 us (30%)
  starting transfers between devices  23.8 us (12%)
  Pallas kernels  18.5 us (10%)
  between operations  14.1 us (7%)
  local copies, waits for them, and re-layouts  6.43 us (3%)
  other arithmetic  3.53 us (2%)
    all_to_all x1, blocking collectives, body(): lax.all_to_all(by_column, ('h', 'l'), split_axis=0, concat_axis=0, tiled=...  48.2 us
    all_to_all x1, waiting for transfers between devices, body(): lax.all_to_all(packed, 'z', split_axis=0, concat_axis=0, tiled=True)  23.2 us
    all_to_all x1, waiting for transfers between devices, body(): lax.all_to_all(by_owner, ('x', 'c'), split_axis=0, concat_axis=0, tiled=T...  21.3 us
    all_gather x1, blocking collectives, body(): near = lax.all_gather(hidden, 'h', axis=0, tiled=True)  19.9 us
    all_to_all x1, waiting for transfers between devices, body(): lax.all_to_all(share, ('x', 'l'), split_axis=0, concat_axis=0, tiled=True)  12.8 us
    pallas_call x2, Pallas kernels, half_product(): pl.pallas_call(half_product_kernel, out_shape=jax.ShapeDtypeStruct((count...  11.4 us
    all_to_all x1, starting transfers between devices, body(): lax.all_to_all(packed, 'z', split_axis=0, concat_axis=0, tiled=True)  11 us
    all_to_all x1, starting transfers between devices, body(): lax.all_to_all(by_owner, ('x', 'c'), split_axis=0, concat_axis=0, tiled=T...  6.43 us
  transfers between devices with their start and end apart: 5, of which 3 were waited for; matrix products, arithmetic and copies ran while one was open for 3% of the time, Pallas kernels for 5%

profile of v6, /device:TPU:1, one launch (start us, length us, event | category | flops | bytes accessed | tf_op | source)
XLA Modules:
  0.0 191.8 jit_solution(8617775688491253612)
XLA Ops:
  7.2 3.8 %pack.1 = bf16[32,208,128]{2,1,0:T(8,128)(2,1)} custom-call(bf16[52,16384]{1,0:T(8,128)(2,1)} %in_ref.1), custom_call_target="tpu_custom_call" | custom-call | tf_op jit(solution)/shard_map/pack/pallas_call | solution.py:35
  10.9 0.0 copy-start.1
  10.9 0.0 copy-start.2
  10.9 11.0 %all-to-all-start = ((bf16[32,208,128]{2,1,0:T(8,128)(2,1)}), bf16[32,208,128]{2,1,0:T(8,128)(2,1)S(1)}, u32[]{:S(2)}, u32[]{:S(2)}) async-start(bf16[32,208,128]{2,1,0:T(8,128)(2,1)} %pack.1), calls=%async_computation | async-start | bytes 3407872 | tf_op jit(solution)/shard_map/all_to_all | solution.py:162
  21.9 0.0 all-gather.2.cloned.1.call-start
  22.0 0.0 copy-done.1
  22.0 0.0 copy-done.2
  22.0 0.1 fusion.4
  22.1 19.9 %all_gather.6 = bf16[256,1664]{1,0:T(8,128)(2,1)} all-gather(bf16[64,1664]{1,0:T(8,128)(2,1)S(1)} %fusion.4), channel_id=1, replica_groups=mesh['z'=8,'h'=4,'x'=4,'l'=2,'c'=2] {'h'}, dimensions={0}, use_global_device_ids=true | all-gather | bytes 1064960 | tf_op jit(solution)/shard_map/all_gather | solution.py:153
  42.0 23.2 %all-to-all-done = bf16[32,208,128]{2,1,0:T(8,128)(2,1)S(1)} async-done(((bf16[32,208,128]{2,1,0:T(8,128)(2,1)}), bf16[32,208,128]{2,1,0:T(8,128)(2,1)S(1)}, u32[]{:S(2)}, u32[]{:S(2)}) %all-to-all-start) | async-done | bytes 1703968 | tf_op jit(solution)/shard_map/all_to_all | solution.py:162
  65.2 0.0 all-gather.2.cloned.1.call-update
  65.2 0.1 copy.12
  65.3 48.2 %all_to_all.24 = bf16[32,208,128]{2,1,0:T(8,128)(2,1)S(1)} all-to-all(bf16[32,208,128]{2,1,0:T(8,128)(2,1)S(1)} %bitcast.17), channel_id=1, replica_groups=mesh['z'=8,'h'=4,'x'=4,'l'=2,'c'=2] {'h','l'}, dimensions={0} | all-to-all | bytes 3407872 | tf_op jit(solution)/shard_map/all_to_all | solution.py:166
  113.5 1.3 copy.13
  114.9 6.4 %all-to-all-start.2 = ((bf16[32,208,128]{2,1,0:T(8,128)(2,1)}), bf16[32,208,128]{2,1,0:T(8,128)(2,1)S(1)}, u32[]{:S(2)}, u32[]{:S(2)}) async-start(bf16[32,208,128]{2,1,0:T(8,128)(2,1)} %bitcast.6), calls=%async_computation.2 | async-start | bytes 3407872 | tf_op jit(solution)/shard_map/all_to_all | solution.py:168
  121.3 0.8 dynamic_slice.3.scale_ref
  122.1 21.3 %all-to-all-done.2 = bf16[32,208,128]{2,1,0:T(8,128)(2,1)S(1)} async-done(((bf16[32,208,128]{2,1,0:T(8,128)(2,1)}), bf16[32,208,128]{2,1,0:T(8,128)(2,1)S(1)}, u32[]{:S(2)}, u32[]{:S(2)}) %all-to-all-start.2) | async-done | bytes 1703968 | tf_op jit(solution)/shard_map/all_to_all | solution.py:168
  143.4 3.3 %requantize.1 = (bf16[1664,512]{1,0:T(8,128)(2,1)S(1)}, bf16[1664,512]{1,0:T(8,128)(2,1)S(1)}, f32[13,128]{1,0:T(8,128)S(1)}) custom-call(f32[13,4]{1,0:T(8,128)S(1)} %dynamic_slice.3.scale_ref, bf16[4,2,2,2,208,128]{5,4,3,2,1,0:T(8,128)(2,1)S(1)} %bitcast.14), custom_call_target="tpu_custom_call" | custom-call | tf_op jit(solution)/shard_map/requantize/pallas_call | solution.py:85
  146.7 0.0 copy-start
  146.7 1.2 copy-done
  147.9 0.0 all-gather.2.cloned.1.call-done.even_ref.odd_ref
  147.9 5.7 %half_product.3 = bf16[1024,512]{1,0:T(8,128)(2,1)} custom-call(s32[1]{0:T(128)S(6)} %sub.3.parity_ref, bf16[2048,1664]{1,0:T(8,128)(2,1)} %all-gather.2.cloned.1.call-done.even_ref.odd_ref, bf16[2048,1664]{1,0:T(8,128)(2,1)} %all-gather.2.cloned.1.call-done.even_ref.odd_ref, bf16[1664,512]{1,0:T(8,128)(2,1)} %copy-done), custom_call_target="tpu_custom_call" | custom-call | flops 1744830464 | bytes 6160384 | tf_op jit(solution)/shard_map/half_product/pallas_call | solution.py:114
  153.6 2.8 %collective-permute-start = (bf16[1024,512]{1,0:T(8,128)(2,1)}, bf16[1024,512]{1,0:T(8,128)(2,1)S(1)}, u32[]{:S(2)}, u32[]{:S(2)}) collective-permute-start(bf16[1024,512]{1,0:T(8,128)(2,1)} %half_product.3), channel_id=1, source_target_pairs={{0,1},{1,0},{2,3},{3,2},{4,5},{5,4},{6,7},{7,6},{8,9},{9,8},{10,11... | collective-permute-start | bytes 3145736 | tf_op jit(solution)/shard_map/ppermute | solution.py:180
  156.4 5.8 %half_product.2 = bf16[1024,512]{1,0:T(8,128)(2,1)} custom-call(s32[1]{0:T(128)} %bitcast.parity_ref, bf16[2048,1664]{1,0:T(8,128)(2,1)} %all-gather.2.cloned.1.call-done.even_ref.odd_ref, bf16[2048,1664]{1,0:T(8,128)(2,1)} %all-gather.2.cloned.1.call-done.even_ref.odd_ref, bf16[1664,512]{1,0:T(8,128)(2,1)} %copy-done), custom_call_target="tpu_custom_call" | custom-call | flops 1744830464 | bytes 6160384 | tf_op jit(solution)/shard_map/half_product/pallas_call | solution.py:114
  162.1 0.0 collective-permute-done
  162.1 2.6 %add_convert_fusion = bf16[1024,512]{1,0:T(8,128)(2,1)} fusion(bf16[1024,512]{1,0:T(8,128)(2,1)S(1)} %collective-permute-done, bf16[1024,512]{1,0:T(8,128)(2,1)} %half_product.2), kind=kLoop, calls=%fused_computation | loop fusion | flops 2097152 | bytes 3145728 | tf_op jit(solution)/shard_map/convert_element_type | solution.py:182
  164.7 3.6 %all-to-all-start.3 = ((bf16[8,128,512]{2,1,0:T(8,128)(2,1)}), bf16[8,128,512]{2,1,0:T(8,128)(2,1)S(1)}, u32[]{:S(2)}, u32[]{:S(2)}) async-start(bf16[8,128,512]{2,1,0:T(8,128)(2,1)} %bitcast.8), calls=%async_computation.3 | async-start | bytes 2097152 | tf_op jit(solution)/shard_map/all_to_all | solution.py:183
  168.3 2.3 %copy.14 = bf16[512,1664]{1,0:T(8,128)(2,1)} copy(bf16[512,1664]{0,1:T(8,128)(2,1)S(1)} %bitcast.15) | data formatting | bytes 3407872
  170.6 0.7 copy.15
  171.3 12.8 %all-to-all-done.3 = bf16[8,128,512]{2,1,0:T(8,128)(2,1)S(1)} async-done(((bf16[8,128,512]{2,1,0:T(8,128)(2,1)}), bf16[8,128,512]{2,1,0:T(8,128)(2,1)S(1)}, u32[]{:S(2)}, u32[]{:S(2)}) %all-to-all-start.3) | async-done | bytes 1048608 | tf_op jit(solution)/shard_map/all_to_all | solution.py:183
  184.1 0.8 reduce_sum.12
  (1 shorter events, 0.0 us)
Async XLA Ops:
  10.9 11.0 %copy-start.1 = (bf16[64,1664]{1,0:T(8,128)(2,1)S(1)}, bf16[64,1664]{1,0:T(8,128)(2,1)}, u32[]{:S(2)}) copy-start(bf16[64,1664]{1,0:T(8,128)(2,1)} %param.7) | copy-start | bytes 638980
  10.9 11.1 %copy-start.2 = (bf16[64,1664]{1,0:T(8,128)(2,1)S(1)}, bf16[64,1664]{1,0:T(8,128)(2,1)}, u32[]{:S(2)}) copy-start(bf16[64,1664]{1,0:T(8,128)(2,1)} %param.6) | copy-start | bytes 638980
  10.9 54.2 %all-to-all-start = ((bf16[32,208,128]{2,1,0:T(8,128)(2,1)}), bf16[32,208,128]{2,1,0:T(8,128)(2,1)S(1)}, u32[]{:S(2)}, u32[]{:S(2)}) async-start(bf16[32,208,128]{2,1,0:T(8,128)(2,1)} %pack.1), calls=%async_computation | async-start | bytes 3407872 | tf_op jit(solution)/shard_map/all_to_all | solution.py:162
  21.9 126.0 %all-gather.2.cloned.1.call-start = ((), (), s32[]{:S(2)}) async-start(), calls=%async_computation.4 | async-start | bytes 7667712 | tf_op jit(solution)/shard_map/all_gather | solution.py:164
  114.9 28.6 %all-to-all-start.2 = ((bf16[32,208,128]{2,1,0:T(8,128)(2,1)}), bf16[32,208,128]{2,1,0:T(8,128)(2,1)S(1)}, u32[]{:S(2)}, u32[]{:S(2)}) async-start(bf16[32,208,128]{2,1,0:T(8,128)(2,1)} %bitcast.6), calls=%async_computation.2 | async-start | bytes 3407872 | tf_op jit(solution)/shard_map/all_to_all | solution.py:168
  146.7 1.2 copy-start
  153.6 8.5 %collective-permute-start = (bf16[1024,512]{1,0:T(8,128)(2,1)}, bf16[1024,512]{1,0:T(8,128)(2,1)S(1)}, u32[]{:S(2)}, u32[]{:S(2)}) collective-permute-start(bf16[1024,512]{1,0:T(8,128)(2,1)} %half_product.3), channel_id=1, source_target_pairs={{0,1},{1,0},{2,3},{3,2},{4,5},{5,4},{6,7},{7,6},{8,9},{9,8},{10,11... | collective-permute-start | bytes 3145736 | tf_op jit(solution)/shard_map/ppermute | solution.py:180
  164.7 19.4 %all-to-all-start.3 = ((bf16[8,128,512]{2,1,0:T(8,128)(2,1)}), bf16[8,128,512]{2,1,0:T(8,128)(2,1)S(1)}, u32[]{:S(2)}, u32[]{:S(2)}) async-start(bf16[8,128,512]{2,1,0:T(8,128)(2,1)} %bitcast.8), calls=%async_computation.3 | async-start | bytes 2097152 | tf_op jit(solution)/shard_map/all_to_all | solution.py:183
Sparse Core Ops, SparseCore 0:
  65.3 78.8 all-gather.1

commit v7 on v5

--- a/solution.py
+++ b/solution.py
@@ -14,28 +14,34 @@
 PACK_STEPS = 4
 
 
-def pack_kernel(in_ref, out_ref, scratch):
+def pack_kernel(in_ref, *refs):
+    *out_refs, scratch = refs
     rows = in_ref.shape[0]
-    sections, _, lanes = out_ref.shape
-    tiles = in_ref.shape[1] // (sections * lanes)
+    sections, packed_rows, lanes = out_refs[0].shape
+    tiles = packed_rows // rows
     for section in range(sections):
-        for tile in range(tiles):
-            at = (section * tiles + tile) * lanes
-            scratch[pl.ds(tile * rows, rows), :] = in_ref[:, pl.ds(at, lanes)].astype(jnp.float32)
-        out_ref[section] = scratch[...].astype(jnp.bfloat16)
+        for which, out_ref in enumerate(out_refs):
+            for tile in range(tiles):
+                at = ((section * len(out_refs) + which) * tiles + tile) * lanes
+                scratch[which, pl.ds(tile * rows, rows), :] = in_ref[:, pl.ds(at, lanes)].astype(
+                    jnp.float32
+                )
+            out_ref[section] = scratch[which].astype(jnp.bfloat16)
 
 
-def pack(old_codes, n_fsdp):
+def pack(old_codes, n_fsdp, parts):
     rows, width = old_codes.shape
-    packed_rows = rows * width // n_fsdp // TILE
+    packed_rows = rows * width // n_fsdp // TILE // parts
     sections = n_fsdp // PACK_STEPS
+    shape = jax.ShapeDtypeStruct((n_fsdp, packed_rows, TILE), jnp.bfloat16)
+    block = pl.BlockSpec((sections, packed_rows, TILE), lambda i: (i, 0, 0))
     return pl.pallas_call(
         pack_kernel,
-        out_shape=jax.ShapeDtypeStruct((n_fsdp, packed_rows, TILE), jnp.bfloat16),
+        out_shape=(shape,) * parts,
         grid=(PACK_STEPS,),
         in_specs=[pl.BlockSpec((rows, width // PACK_STEPS), lambda i: (0, i))],
-        out_specs=pl.BlockSpec((sections, packed_rows, TILE), lambda i: (i, 0, 0)),
-        scratch_shapes=[pltpu.VMEM((packed_rows, TILE), jnp.float32)],
+        out_specs=(block,) * parts,
+        scratch_shapes=[pltpu.VMEM((parts, packed_rows, TILE), jnp.float32)],
         compiler_params=pltpu.CompilerParams(vmem_limit_bytes=12 << 20),
         name="pack",
     )(old_codes)
@@ -116,20 +122,24 @@
     n_z = lax.axis_size("z")
     n_h = lax.axis_size("h")
     near = lax.all_gather(hidden, "h", axis=0, tiled=True)
-    packed = pack(old_codes, n_fsdp)
-    packed_rows = packed.shape[1]
+    staged, direct = pack(old_codes, n_fsdp, 2)
+    part_rows = staged.shape[1]
+    packed_rows = 2 * part_rows
 
     def swapped(sections, rows):
-        return jnp.swapaxes(sections.reshape(rows, -1, packed_rows, TILE), 0, 1).reshape(
-            n_fsdp, packed_rows, TILE
+        return jnp.swapaxes(sections.reshape(rows, -1, part_rows, TILE), 0, 1).reshape(
+            n_fsdp, part_rows, TILE
         )
 
-    along_z = lax.all_to_all(packed, "z", split_axis=0, concat_axis=0, tiled=True)
+    along_z = lax.all_to_all(staged, "z", split_axis=0, concat_axis=0, tiled=True)
     near, along_z = lax.optimization_barrier((near, along_z))
     every = lax.all_gather(near, "z", axis=0, tiled=True)
-    sectioned = lax.all_to_all(swapped(along_z, n_z), "h", split_axis=0, concat_axis=0, tiled=True)
+    staged = lax.all_to_all(swapped(along_z, n_z), "h", split_axis=0, concat_axis=0, tiled=True)
+    staged, direct = lax.optimization_barrier((staged, direct))
+    direct = lax.all_to_all(direct, FSDP, split_axis=0, concat_axis=0, tiled=True)
+    sectioned = jnp.concatenate([swapped(staged, n_h), direct], axis=1)
     moved = lax.all_to_all(
-        swapped(sectioned, n_h).reshape(n_tensor, per_owner * packed_rows, TILE),
+        sectioned.reshape(n_tensor, per_owner * packed_rows, TILE),
         TENSOR,
         split_axis=0,
         concat_axis=0,

time: 191 us -> 190 us (level)
  blocking collectives: 67.1 us -> 48.9 us
  waiting for transfers between devices: 60.1 us -> 71.1 us
  starting transfers between devices: 23.7 us -> 29.8 us
    all_to_all x1, blocking collectives: 47.2 us -> 29 us  [body(): lax.all_to_all(swapped(along_z, n_z), 'h', split_axis=0, concat_axis=0, t...]
    all_to_all x2 -> x3, waiting for transfers between devices: 45.3 us -> 52.6 us  [the longest x1 25.6 us: body(): lax.all_to_all(direct, FSDP, split_axis=0, concat_axis=0, tiled=True)]
    all_to_all x2 -> x3, starting transfers between devices: 17.3 us -> 22.3 us  [the longest x1 10.9 us: body(): lax.all_to_all(staged, 'z', split_axis=0, concat_axis=0, tiled=True)]
    all_gather x1, waiting for transfers between devices: 0.01 us -> 3.93 us  [body(): every = lax.all_gather(near, 'z', axis=0, tiled=True)]
  transfers between devices with their start and end apart: 5 -> 6, of which waited for: 4 -> 6; matrix products, arithmetic and copies ran while one was open for 3% -> 3% of each run, Pallas kernels for 2% -> 2%
where the time goes in v7:
time: 190 us
  waiting for transfers between devices  71.1 us (37%)
  blocking collectives  48.9 us (26%)
  starting transfers between devices  29.8 us (16%)
  between operations  14.1 us (7%)
  local copies, waits for them, and re-layouts  7.99 us (4%)
  matrix products  7.36 us (4%)
  Pallas kernels  5.22 us (3%)
  other arithmetic  5.13 us (3%)
    all_to_all x1, blocking collectives, body(): lax.all_to_all(swapped(along_z, n_z), 'h', split_axis=0, concat_axis=0, t...  29 us
    all_to_all x1, waiting for transfers between devices, body(): lax.all_to_all(direct, FSDP, split_axis=0, concat_axis=0, tiled=True)  25.6 us
    all_to_all x1, waiting for transfers between devices, body(): lax.all_to_all(sectioned.reshape(n_tensor, per_owner * packed_rows, TILE)...  22.1 us
    all_gather x1, blocking collectives, body(): near = lax.all_gather(hidden, 'h', axis=0, tiled=True)  19.9 us
    all_to_all x1, waiting for transfers between devices, body(): lax.all_to_all(share, ('x', 'l'), split_axis=0, concat_axis=0, tiled=True)  12.2 us
    all_to_all x1, starting transfers between devices, body(): lax.all_to_all(staged, 'z', split_axis=0, concat_axis=0, tiled=True)  10.9 us
    dot_general x1, matrix products, body(): jnp.dot(every, weight, preferred_element_type=jnp.float32)  7.36 us
    all_to_all x1, starting transfers between devices, body(): lax.all_to_all(sectioned.reshape(n_tensor, per_owner * packed_rows, TILE)...  7.13 us
  transfers between devices with their start and end apart: 6, of which 6 were waited for; matrix products, arithmetic and copies ran while one was open for 3% of the time, Pallas kernels for 2%

profile of v7, /device:TPU:1, one launch (start us, length us, event | category | flops | bytes accessed | tf_op | source)
XLA Modules:
  0.0 189.6 jit_solution(12750863978119814984)
XLA Ops:
  7.2 1.5 copy-done
  8.7 1.9 %pack.1 = (bf16[32,104,128]{2,1,0:T(8,128)(2,1)}, bf16[32,104,128]{2,1,0:T(8,128)(2,1)}) custom-call(bf16[52,16384]{1,0:T(8,128)(2,1)S(1)} %copy-done), custom_call_target="tpu_custom_call" | custom-call | tf_op jit(solution)/shard_map/pack/pallas_call | solution.py:38
  10.6 10.9 %all-to-all-start = ((bf16[32,104,128]{2,1,0:T(8,128)(2,1)}), bf16[32,104,128]{2,1,0:T(8,128)(2,1)S(1)}, u32[]{:S(2)}, u32[]{:S(2)}) async-start(bf16[32,104,128]{2,1,0:T(8,128)(2,1)} %get-tuple-element.12), calls=%async_computation | async-start | bytes 1703936 | tf_op jit(solution)/shard_map/all_to_all | solution.py:134
  21.5 0.0 all-gather.2.cloned.1.call-start
  21.5 0.1 fusion.5
  21.7 19.9 %all_gather.6 = bf16[256,1664]{1,0:T(8,128)(2,1)} all-gather(bf16[64,1664]{1,0:T(8,128)(2,1)S(1)} %fusion.5), channel_id=1, replica_groups=mesh['z'=8,'h'=4,'x'=4,'l'=2,'c'=2] {'h'}, dimensions={0}, use_global_device_ids=true | all-gather | bytes 1064960 | tf_op jit(solution)/shard_map/all_gather | solution.py:124
  41.5 4.9 %all-to-all-done = bf16[32,104,128]{2,1,0:T(8,128)(2,1)S(1)} async-done(((bf16[32,104,128]{2,1,0:T(8,128)(2,1)}), bf16[32,104,128]{2,1,0:T(8,128)(2,1)S(1)}, u32[]{:S(2)}, u32[]{:S(2)}) %all-to-all-start) | async-done | bytes 852000 | tf_op jit(solution)/shard_map/all_to_all | solution.py:134
  46.5 0.0 all-gather.2.cloned.1.call-update
  46.5 0.1 copy.9
  46.6 29.0 %all_to_all.25 = bf16[32,104,128]{2,1,0:T(8,128)(2,1)S(1)} all-to-all(bf16[32,104,128]{2,1,0:T(8,128)(2,1)S(1)} %bitcast.25), channel_id=1, replica_groups=mesh['z'=8,'h'=4,'x'=4,'l'=2,'c'=2] {'h'}, dimensions={0} | all-to-all | bytes 1703936 | tf_op jit(solution)/shard_map/all_to_all | solution.py:137
  75.6 4.3 %all-to-all-start.2 = ((bf16[32,104,128]{2,1,0:T(8,128)(2,1)}), bf16[32,104,128]{2,1,0:T(8,128)(2,1)S(1)}, u32[]{:S(2)}, u32[]{:S(2)}) async-start(bf16[32,104,128]{2,1,0:T(8,128)(2,1)} %get-tuple-element.17), calls=%async_computation.2 | async-start | bytes 1703936 | tf_op jit(solution)/shard_map/all_to_all | solution.py:139
  79.9 0.1 copy.10
  79.9 25.6 %all-to-all-done.2 = bf16[32,104,128]{2,1,0:T(8,128)(2,1)S(1)} async-done(((bf16[32,104,128]{2,1,0:T(8,128)(2,1)}), bf16[32,104,128]{2,1,0:T(8,128)(2,1)S(1)}, u32[]{:S(2)}, u32[]{:S(2)}) %all-to-all-start.2) | async-done | bytes 852000 | tf_op jit(solution)/shard_map/all_to_all | solution.py:139
  105.5 1.3 pad_maximum_fusion
  106.8 7.1 %all-to-all-start.3 = ((bf16[16,416,128]{2,1,0:T(8,128)(2,1)}), bf16[16,416,128]{2,1,0:T(8,128)(2,1)S(1)}, u32[]{:S(2)}, u32[]{:S(2)}) async-start(bf16[16,416,128]{2,1,0:T(8,128)(2,1)} %bitcast.6), calls=%async_computation.3 | async-start | bytes 3407872 | tf_op jit(solution)/shard_map/all_to_all | solution.py:141
  113.9 0.8 dynamic_slice.10.scale_ref
  114.7 22.1 %all-to-all-done.3 = bf16[16,416,128]{2,1,0:T(8,128)(2,1)S(1)} async-done(((bf16[16,416,128]{2,1,0:T(8,128)(2,1)}), bf16[16,416,128]{2,1,0:T(8,128)(2,1)S(1)}, u32[]{:S(2)}, u32[]{:S(2)}) %all-to-all-start.3) | async-done | bytes 1703968 | tf_op jit(solution)/shard_map/all_to_all | solution.py:141
  136.8 3.3 %requantize.1 = (bf16[1664,512]{1,0:T(8,128)(2,1)S(1)}, bf16[1664,512]{1,0:T(8,128)(2,1)S(1)}, f32[13,128]{1,0:T(8,128)S(1)}) custom-call(f32[13,4]{1,0:T(8,128)S(1)} %dynamic_slice.10.scale_ref, bf16[16,2,208,128]{3,2,1,0:T(8,128)(2,1)S(1)} %bitcast.21), custom_call_target="tpu_custom_call" | custom-call | tf_op jit(solution)/shard_map/requantize/pallas_call | solution.py:90
  140.1 0.0 copy-start.1
  140.1 1.2 copy-done.1
  141.3 3.9 %all-gather.2.cloned.1.call-done = bf16[2048,1664]{1,0:T(8,128)(2,1)} async-done(((bf16[256,1664]{1,0:T(8,128)(2,1)}), bf16[2048,1664]{1,0:T(8,128)(2,1)}) %all-gather.2.cloned.1.call-update) | async-done | bytes 6815760 | tf_op jit(solution)/shard_map/all_gather | solution.py:136
  145.2 7.4 %convolution_convert_fusion = bf16[2048,512]{1,0:T(8,128)(2,1)S(1)} fusion(bf16[2048,1664]{1,0:T(8,128)(2,1)} %all-gather.2.cloned.1.call-done, bf16[1664,512]{1,0:T(8,128)(2,1)} %copy-done.1), kind=kOutput, calls=%fused_computation | convolution fusion | flops 3490709504 | bytes 10616832 | tf_op jit(solution)/shard_map/dot_general | solution.py:159
  152.6 1.3 copy-done.2
  153.9 0.1 dynamic-slice_bitcast_fusion
  154.0 2.6 %collective-permute-start = (bf16[8,128,512]{2,1,0:T(8,128)(2,1)S(1)}, bf16[8,128,512]{2,1,0:T(8,128)(2,1)}, u32[]{:S(2)}, u32[]{:S(2)}) collective-permute-start(bf16[8,128,512]{2,1,0:T(8,128)(2,1)S(1)} %dynamic-slice_bitcast_fusion), channel_id=1, source_target_pairs={{0,1},{1,0},{2,3},{3,2},{4,5},{5,4},{6,7},{7,6},{8,9},{9,8},{10,11... | collective-permute-start | bytes 3145736 | tf_op jit(solution)/shard_map/ppermute | solution.py:162
  156.6 2.4 %collective-permute-done = bf16[8,128,512]{2,1,0:T(8,128)(2,1)} collective-permute-done((bf16[8,128,512]{2,1,0:T(8,128)(2,1)S(1)}, bf16[8,128,512]{2,1,0:T(8,128)(2,1)}, u32[]{:S(2)}, u32[]{:S(2)}) %collective-permute-start) | collective-permute-done | bytes 1048608 | tf_op jit(solution)/shard_map/ppermute | solution.py:162
  159.0 2.9 %fusion = bf16[8,128,512]{2,1,0:T(8,128)(2,1)} fusion(bf16[8,128,512]{2,1,0:T(8,128)(2,1)} %collective-permute-done, bf16[8,2,128,512]{3,2,1,0:T(8,128)(2,1)} %bitcast.28, s32[]{:T(128)S(6)} %select_n.15), kind=kLoop, calls=%fused_computation.2 | loop fusion | flops 2097152 | bytes 3145732 | tf_op jit(solution)/shard_map/convert_element_type | solution.py:164
  161.9 4.9 %all-to-all-start.4 = ((bf16[8,128,512]{2,1,0:T(8,128)(2,1)}), bf16[8,128,512]{2,1,0:T(8,128)(2,1)S(1)}, u32[]{:S(2)}, u32[]{:S(2)}) async-start(bf16[8,128,512]{2,1,0:T(8,128)(2,1)} %fusion), calls=%async_computation.4 | async-start | bytes 2097152 | tf_op jit(solution)/shard_map/all_to_all | solution.py:165
  166.8 2.3 %copy.11 = bf16[512,1664]{1,0:T(8,128)(2,1)} copy(bf16[512,1664]{0,1:T(8,128)(2,1)S(1)} %bitcast.22) | data formatting | bytes 3407872
  169.1 0.7 copy.12
  169.8 12.2 %all-to-all-done.4 = bf16[8,128,512]{2,1,0:T(8,128)(2,1)S(1)} async-done(((bf16[8,128,512]{2,1,0:T(8,128)(2,1)}), bf16[8,128,512]{2,1,0:T(8,128)(2,1)S(1)}, u32[]{:S(2)}, u32[]{:S(2)}) %all-to-all-start.4) | async-done | bytes 1048608 | tf_op jit(solution)/shard_map/all_to_all | solution.py:165
  182.0 0.8 reduce_sum.12
  (7 shorter events, 0.0 us)
Async XLA Ops:
  7.2 1.5 copy-start
  8.7 12.9 %copy-start.3 = (bf16[64,1664]{1,0:T(8,128)(2,1)S(1)}, bf16[64,1664]{1,0:T(8,128)(2,1)}, u32[]{:S(2)}) copy-start(bf16[64,1664]{1,0:T(8,128)(2,1)} %param.7) | copy-start | bytes 638980
  8.7 12.9 %copy-start.4 = (bf16[64,1664]{1,0:T(8,128)(2,1)S(1)}, bf16[64,1664]{1,0:T(8,128)(2,1)}, u32[]{:S(2)}) copy-start(bf16[64,1664]{1,0:T(8,128)(2,1)} %param.6) | copy-start | bytes 638980
  10.6 35.8 %all-to-all-start = ((bf16[32,104,128]{2,1,0:T(8,128)(2,1)}), bf16[32,104,128]{2,1,0:T(8,128)(2,1)S(1)}, u32[]{:S(2)}, u32[]{:S(2)}) async-start(bf16[32,104,128]{2,1,0:T(8,128)(2,1)} %get-tuple-element.12), calls=%async_computation | async-start | bytes 1703936 | tf_op jit(solution)/shard_map/all_to_all | solution.py:134
  21.5 123.8 %all-gather.2.cloned.1.call-start = ((), (), s32[]{:S(2)}) async-start(), calls=%async_computation.5 | async-start | bytes 7667712 | tf_op jit(solution)/shard_map/all_gather | solution.py:136
  75.6 29.9 %all-to-all-start.2 = ((bf16[32,104,128]{2,1,0:T(8,128)(2,1)}), bf16[32,104,128]{2,1,0:T(8,128)(2,1)S(1)}, u32[]{:S(2)}, u32[]{:S(2)}) async-start(bf16[32,104,128]{2,1,0:T(8,128)(2,1)} %get-tuple-element.17), calls=%async_computation.2 | async-start | bytes 1703936 | tf_op jit(solution)/shard_map/all_to_all | solution.py:139
  106.8 30.0 %all-to-all-start.3 = ((bf16[16,416,128]{2,1,0:T(8,128)(2,1)}), bf16[16,416,128]{2,1,0:T(8,128)(2,1)S(1)}, u32[]{:S(2)}, u32[]{:S(2)}) async-start(bf16[16,416,128]{2,1,0:T(8,128)(2,1)} %bitcast.6), calls=%async_computation.3 | async-start | bytes 3407872 | tf_op jit(solution)/shard_map/all_to_all | solution.py:141
  140.1 1.2 copy-start.1
  152.6 1.3 copy-start.2
  154.0 5.0 %collective-permute-start = (bf16[8,128,512]{2,1,0:T(8,128)(2,1)S(1)}, bf16[8,128,512]{2,1,0:T(8,128)(2,1)}, u32[]{:S(2)}, u32[]{:S(2)}) collective-permute-start(bf16[8,128,512]{2,1,0:T(8,128)(2,1)S(1)} %dynamic-slice_bitcast_fusion), channel_id=1, source_target_pairs={{0,1},{1,0},{2,3},{3,2},{4,5},{5,4},{6,7},{7,6},{8,9},{9,8},{10,11... | collective-permute-start | bytes 3145736 | tf_op jit(solution)/shard_map/ppermute | solution.py:162
  161.9 20.1 %all-to-all-start.4 = ((bf16[8,128,512]{2,1,0:T(8,128)(2,1)}), bf16[8,128,512]{2,1,0:T(8,128)(2,1)S(1)}, u32[]{:S(2)}, u32[]{:S(2)}) async-start(bf16[8,128,512]{2,1,0:T(8,128)(2,1)} %fusion), calls=%async_computation.4 | async-start | bytes 2097152 | tf_op jit(solution)/shard_map/all_to_all | solution.py:165
Sparse Core Ops, SparseCore 0:
  46.6 98.5 all-gather.1

commit v8 on v7

--- a/solution.py
+++ b/solution.py
@@ -105,6 +105,40 @@
     )(scale_block, moved)
 
 
+def half_product_kernel(parity_ref, even_ref, odd_ref, weight_ref, out_ref):
+    tokens = jnp.concatenate([even_ref[...], odd_ref[...]], axis=0)
+    out_ref[...] = jnp.dot(
+        tokens, weight_ref[...], preferred_element_type=jnp.float32
+    ).astype(jnp.bfloat16)
+
+
+def half_product(every, weight, parity, owners):
+    depth, width = weight.shape
+    rows = every.shape[0] // owners
+    count = every.shape[0] // 2
+    return pl.pallas_call(
+        half_product_kernel,
+        out_shape=jax.ShapeDtypeStruct((count, width), jnp.bfloat16),
+        grid_spec=pltpu.PrefetchScalarGridSpec(
+            num_scalar_prefetch=1,
+            grid=(owners // 4,),
+            in_specs=[
+                pl.BlockSpec((rows, depth), lambda i, parity: (4 * i + parity[0], 0)),
+                pl.BlockSpec((rows, depth), lambda i, parity: (4 * i + 2 + parity[0], 0)),
+                pl.BlockSpec(memory_space=pltpu.VMEM),
+            ],
+            out_specs=pl.BlockSpec((2 * rows, width), lambda i, parity: (i, 0)),
+        ),
+        compiler_params=pltpu.CompilerParams(vmem_limit_bytes=10 << 20),
+        cost_estimate=pl.CostEstimate(
+            flops=2 * count * depth * width,
+            bytes_accessed=2 * (count * depth + depth * width + count * width),
+            transcendentals=0,
+        ),
+        name="half_product",
+    )(parity, every, every, weight)
+
+
 def body(old_codes, old_scales, gate_pre, up_pre):
     n_fsdp = lax.axis_size(FSDP)
     n_tensor = lax.axis_size(TENSOR)
@@ -155,12 +189,11 @@
     scales_t = new_scale[:, :col_tiles].T
 
     n_c = lax.axis_size("c")
-    core = lax.axis_index("c")
-    share = jnp.dot(every, weight, preferred_element_type=jnp.float32).astype(jnp.bfloat16)
-    by_core = share.reshape(n_tensor // n_c, n_c, -1, col_width)
-    other = lax.dynamic_index_in_dim(by_core, 1 - core, 1, keepdims=False)
+    core = lax.axis_index("c").astype(jnp.int32).reshape(1)
+    every = pltpu.with_memory_space_constraint(every, pltpu.HBM)
+    other = half_product(every, weight, 1 - core, n_tensor)
     other = lax.ppermute(other, "c", [(0, 1), (1, 0)])
-    own = lax.dynamic_index_in_dim(by_core, core, 1, keepdims=False)
+    own = half_product(every, weight, core, n_tensor)
     share = (own.astype(jnp.float32) + other.astype(jnp.float32)).astype(jnp.bfloat16)
     shares = lax.all_to_all(share, ("x", "l"), split_axis=0, concat_axis=0, tiled=True)
     mixed = jnp.sum(

time: 190 us -> 187 us (0.984)
  Pallas kernels: 5.22 us -> 13.8 us
  matrix products: 7.36 us -> 0 us
  waiting for transfers between devices: 71.1 us -> 69.1 us
    pallas_call x0 -> x2, Pallas kernels: none -> 8.61 us  [half_product(): pl.pallas_call(half_product_kernel, out_shape=jax.ShapeDtypeStruct((count...]
    dot_general x1 -> x0, matrix products: 7.36 us -> none  [body(): jnp.dot(every, weight, preferred_element_type=jnp.float32)]
    ppermute x1, waiting for transfers between devices: 2.4 us -> 0.01 us  [body(): other = lax.ppermute(other, 'c', [(0, 1), (1, 0)])]
  transfers between devices with their start and end apart: 6 -> 6, of which waited for: 6 -> 5; matrix products, arithmetic and copies ran while one was open for 3% -> 3% of each run, Pallas kernels for 2% -> 4%
where the time goes in v8:
time: 187 us; the launch traced here: 186 us
  waiting for transfers between devices  69.1 us (37%)
  blocking collectives  48.9 us (26%)
  starting transfers between devices  29.9 us (16%)
  between operations  14.1 us (8%)
  Pallas kernels  13.8 us (7%)
  local copies, waits for them, and re-layouts  6.61 us (4%)
  other arithmetic  3.54 us (2%)
    all_to_all x1, blocking collectives, body(): lax.all_to_all(swapped(along_z, n_z), 'h', split_axis=0, concat_axis=0, t...  29 us
    all_to_all x1, waiting for transfers between devices, body(): lax.all_to_all(direct, FSDP, split_axis=0, concat_axis=0, tiled=True)  25.6 us
    all_to_all x1, waiting for transfers between devices, body(): lax.all_to_all(sectioned.reshape(n_tensor, per_owner * packed_rows, TILE)...  22.1 us
    all_gather x1, blocking collectives, body(): near = lax.all_gather(hidden, 'h', axis=0, tiled=True)  19.9 us
    all_to_all x1, waiting for transfers between devices, body(): lax.all_to_all(share, ('x', 'l'), split_axis=0, concat_axis=0, tiled=True)  12.6 us
    all_to_all x1, starting transfers between devices, body(): lax.all_to_all(staged, 'z', split_axis=0, concat_axis=0, tiled=True)  10.9 us
    pallas_call x2, Pallas kernels, half_product(): pl.pallas_call(half_product_kernel, out_shape=jax.ShapeDtypeStruct((count...  8.61 us
    all_to_all x1, starting transfers between devices, body(): lax.all_to_all(sectioned.reshape(n_tensor, per_owner * packed_rows, TILE)...  7.13 us
  transfers between devices with their start and end apart: 6, of which 5 were waited for; matrix products, arithmetic and copies ran while one was open for 3% of the time, Pallas kernels for 4%

profile of v8, /device:TPU:1, one launch (start us, length us, event | category | flops | bytes accessed | tf_op | source)
XLA Modules:
  0.0 186.0 jit_solution(416026551187692877)
XLA Ops:
  7.2 0.0 copy-start
  7.2 1.5 copy-done
  8.7 1.9 %pack.1 = (bf16[32,104,128]{2,1,0:T(8,128)(2,1)}, bf16[32,104,128]{2,1,0:T(8,128)(2,1)}) custom-call(bf16[52,16384]{1,0:T(8,128)(2,1)S(1)} %copy-done), custom_call_target="tpu_custom_call" | custom-call | tf_op jit(solution)/shard_map/pack/pallas_call | solution.py:38
  10.6 10.9 %all-to-all-start = ((bf16[32,104,128]{2,1,0:T(8,128)(2,1)}), bf16[32,104,128]{2,1,0:T(8,128)(2,1)S(1)}, u32[]{:S(2)}, u32[]{:S(2)}) async-start(bf16[32,104,128]{2,1,0:T(8,128)(2,1)} %get-tuple-element.12), calls=%async_computation | async-start | bytes 1703936 | tf_op jit(solution)/shard_map/all_to_all | solution.py:168
  21.5 0.0 all-gather.2.cloned.1.call-start
  21.5 0.1 fusion.4
  21.7 19.9 %all_gather.6 = bf16[256,1664]{1,0:T(8,128)(2,1)} all-gather(bf16[64,1664]{1,0:T(8,128)(2,1)S(1)} %fusion.4), channel_id=1, replica_groups=mesh['z'=8,'h'=4,'x'=4,'l'=2,'c'=2] {'h'}, dimensions={0}, use_global_device_ids=true | all-gather | bytes 1064960 | tf_op jit(solution)/shard_map/all_gather | solution.py:158
  41.5 4.9 %all-to-all-done = bf16[32,104,128]{2,1,0:T(8,128)(2,1)S(1)} async-done(((bf16[32,104,128]{2,1,0:T(8,128)(2,1)}), bf16[32,104,128]{2,1,0:T(8,128)(2,1)S(1)}, u32[]{:S(2)}, u32[]{:S(2)}) %all-to-all-start) | async-done | bytes 852000 | tf_op jit(solution)/shard_map/all_to_all | solution.py:168
  46.5 0.0 all-gather.2.cloned.1.call-update
  46.5 0.1 copy.9
  46.6 29.0 %all_to_all.29 = bf16[32,104,128]{2,1,0:T(8,128)(2,1)S(1)} all-to-all(bf16[32,104,128]{2,1,0:T(8,128)(2,1)S(1)} %bitcast.19), channel_id=1, replica_groups=mesh['z'=8,'h'=4,'x'=4,'l'=2,'c'=2] {'h'}, dimensions={0} | all-to-all | bytes 1703936 | tf_op jit(solution)/shard_map/all_to_all | solution.py:171
  75.6 4.3 %all-to-all-start.2 = ((bf16[32,104,128]{2,1,0:T(8,128)(2,1)}), bf16[32,104,128]{2,1,0:T(8,128)(2,1)S(1)}, u32[]{:S(2)}, u32[]{:S(2)}) async-start(bf16[32,104,128]{2,1,0:T(8,128)(2,1)} %get-tuple-element.17), calls=%async_computation.2 | async-start | bytes 1703936 | tf_op jit(solution)/shard_map/all_to_all | solution.py:173
  79.9 0.1 copy.10
  79.9 25.6 %all-to-all-done.2 = bf16[32,104,128]{2,1,0:T(8,128)(2,1)S(1)} async-done(((bf16[32,104,128]{2,1,0:T(8,128)(2,1)}), bf16[32,104,128]{2,1,0:T(8,128)(2,1)S(1)}, u32[]{:S(2)}, u32[]{:S(2)}) %all-to-all-start.2) | async-done | bytes 852000 | tf_op jit(solution)/shard_map/all_to_all | solution.py:173
  105.5 1.3 pad_maximum_fusion
  106.8 7.1 %all-to-all-start.3 = ((bf16[16,416,128]{2,1,0:T(8,128)(2,1)}), bf16[16,416,128]{2,1,0:T(8,128)(2,1)S(1)}, u32[]{:S(2)}, u32[]{:S(2)}) async-start(bf16[16,416,128]{2,1,0:T(8,128)(2,1)} %bitcast.7), calls=%async_computation.3 | async-start | bytes 3407872 | tf_op jit(solution)/shard_map/all_to_all | solution.py:175
  113.9 0.8 dynamic_slice.3.scale_ref
  114.7 22.1 %all-to-all-done.3 = bf16[16,416,128]{2,1,0:T(8,128)(2,1)S(1)} async-done(((bf16[16,416,128]{2,1,0:T(8,128)(2,1)}), bf16[16,416,128]{2,1,0:T(8,128)(2,1)S(1)}, u32[]{:S(2)}, u32[]{:S(2)}) %all-to-all-start.3) | async-done | bytes 1703968 | tf_op jit(solution)/shard_map/all_to_all | solution.py:175
  136.8 3.3 %requantize.1 = (bf16[1664,512]{1,0:T(8,128)(2,1)S(1)}, bf16[1664,512]{1,0:T(8,128)(2,1)S(1)}, f32[13,128]{1,0:T(8,128)S(1)}) custom-call(f32[13,4]{1,0:T(8,128)S(1)} %dynamic_slice.3.scale_ref, bf16[16,2,208,128]{3,2,1,0:T(8,128)(2,1)S(1)} %bitcast.15), custom_call_target="tpu_custom_call" | custom-call | tf_op jit(solution)/shard_map/requantize/pallas_call | solution.py:90
  140.1 0.0 copy-start.1
  140.1 1.2 copy-done.1
  141.3 3.9 %all-gather.2.cloned.1.call-done.even_ref.odd_ref = bf16[2048,1664]{1,0:T(8,128)(2,1)} async-done(((bf16[256,1664]{1,0:T(8,128)(2,1)}), bf16[2048,1664]{1,0:T(8,128)(2,1)}) %all-gather.2.cloned.1.call-update) | async-done | bytes 6815760 | tf_op jit(solution)/shard_map/all_gather | solution.py:170
  145.2 4.3 %half_product.3 = bf16[1024,512]{1,0:T(8,128)(2,1)S(1)} custom-call(s32[1]{0:T(128)S(6)} %sub.3.parity_ref, bf16[2048,1664]{1,0:T(8,128)(2,1)} %all-gather.2.cloned.1.call-done.even_ref.odd_ref, bf16[2048,1664]{1,0:T(8,128)(2,1)} %all-gather.2.cloned.1.call-done.even_ref.odd_ref, bf16[1664,512]{1,0:T(8,128)(2,1)S(1)} %get-tuple-element.18.weight_ref), custom_call_target="tpu_custom_call" | custom-call | flops 1744830464 | bytes 6160384 | tf_op jit(solution)/shard_map/half_product/pallas_call | solution.py:119
  149.6 2.6 %collective-permute-start = (bf16[1024,512]{1,0:T(8,128)(2,1)S(1)}, bf16[1024,512]{1,0:T(8,128)(2,1)S(1)}, u32[]{:S(2)}, u32[]{:S(2)}) collective-permute-start(bf16[1024,512]{1,0:T(8,128)(2,1)S(1)} %half_product.3), channel_id=1, source_target_pairs={{0,1},{1,0},{2,3},{3,2},{4,5},{5,4},{6,7},{7,6},{8,9},{9,8},{10,11... | collective-permute-start | bytes 3145736 | tf_op jit(solution)/shard_map/ppermute | solution.py:195
  152.1 4.3 %half_product.2 = bf16[1024,512]{1,0:T(8,128)(2,1)S(1)} custom-call(s32[1]{0:T(128)} %bitcast.parity_ref, bf16[2048,1664]{1,0:T(8,128)(2,1)} %all-gather.2.cloned.1.call-done.even_ref.odd_ref, bf16[2048,1664]{1,0:T(8,128)(2,1)} %all-gather.2.cloned.1.call-done.even_ref.odd_ref, bf16[1664,512]{1,0:T(8,128)(2,1)S(1)} %get-tuple-element.18.weight_ref), custom_call_target="tpu_custom_call" | custom-call | flops 1744830464 | bytes 6160384 | tf_op jit(solution)/shard_map/half_product/pallas_call | solution.py:119
  156.5 0.0 collective-permute-done
  156.5 1.3 add_convert_fusion
  157.8 5.0 %all-to-all-start.4 = ((bf16[8,128,512]{2,1,0:T(8,128)(2,1)}), bf16[8,128,512]{2,1,0:T(8,128)(2,1)S(1)}, u32[]{:S(2)}, u32[]{:S(2)}) async-start(bf16[8,128,512]{2,1,0:T(8,128)(2,1)} %bitcast.9), calls=%async_computation.4 | async-start | bytes 2097152 | tf_op jit(solution)/shard_map/all_to_all | solution.py:198
  162.8 2.3 %copy.11 = bf16[512,1664]{1,0:T(8,128)(2,1)} copy(bf16[512,1664]{0,1:T(8,128)(2,1)S(1)} %bitcast.16) | data formatting | bytes 3407872
  165.1 0.7 copy.12
  165.8 12.6 %all-to-all-done.4 = bf16[8,128,512]{2,1,0:T(8,128)(2,1)S(1)} async-done(((bf16[8,128,512]{2,1,0:T(8,128)(2,1)}), bf16[8,128,512]{2,1,0:T(8,128)(2,1)S(1)}, u32[]{:S(2)}, u32[]{:S(2)}) %all-to-all-start.4) | async-done | bytes 1048608 | tf_op jit(solution)/shard_map/all_to_all | solution.py:198
  178.4 0.8 reduce_sum.12
  (7 shorter events, 0.0 us)
Async XLA Ops:
  7.2 1.5 copy-start
  8.7 12.9 %copy-start.3 = (bf16[64,1664]{1,0:T(8,128)(2,1)S(1)}, bf16[64,1664]{1,0:T(8,128)(2,1)}, u32[]{:S(2)}) copy-start(bf16[64,1664]{1,0:T(8,128)(2,1)} %param.7) | copy-start | bytes 638980
  8.7 12.9 %copy-start.4 = (bf16[64,1664]{1,0:T(8,128)(2,1)S(1)}, bf16[64,1664]{1,0:T(8,128)(2,1)}, u32[]{:S(2)}) copy-start(bf16[64,1664]{1,0:T(8,128)(2,1)} %param.6) | copy-start | bytes 638980
  10.6 35.8 %all-to-all-start = ((bf16[32,104,128]{2,1,0:T(8,128)(2,1)}), bf16[32,104,128]{2,1,0:T(8,128)(2,1)S(1)}, u32[]{:S(2)}, u32[]{:S(2)}) async-start(bf16[32,104,128]{2,1,0:T(8,128)(2,1)} %get-tuple-element.12), calls=%async_computation | async-start | bytes 1703936 | tf_op jit(solution)/shard_map/all_to_all | solution.py:168
  21.5 123.8 %all-gather.2.cloned.1.call-start = ((), (), s32[]{:S(2)}) async-start(), calls=%async_computation.5 | async-start | bytes 7667712 | tf_op jit(solution)/shard_map/all_gather | solution.py:170
  75.6 29.9 %all-to-all-start.2 = ((bf16[32,104,128]{2,1,0:T(8,128)(2,1)}), bf16[32,104,128]{2,1,0:T(8,128)(2,1)S(1)}, u32[]{:S(2)}, u32[]{:S(2)}) async-start(bf16[32,104,128]{2,1,0:T(8,128)(2,1)} %get-tuple-element.17), calls=%async_computation.2 | async-start | bytes 1703936 | tf_op jit(solution)/shard_map/all_to_all | solution.py:173
  106.8 30.0 %all-to-all-start.3 = ((bf16[16,416,128]{2,1,0:T(8,128)(2,1)}), bf16[16,416,128]{2,1,0:T(8,128)(2,1)S(1)}, u32[]{:S(2)}, u32[]{:S(2)}) async-start(bf16[16,416,128]{2,1,0:T(8,128)(2,1)} %bitcast.7), calls=%async_computation.3 | async-start | bytes 3407872 | tf_op jit(solution)/shard_map/all_to_all | solution.py:175
  140.1 1.2 copy-start.1
  149.6 6.9 %collective-permute-start = (bf16[1024,512]{1,0:T(8,128)(2,1)S(1)}, bf16[1024,512]{1,0:T(8,128)(2,1)S(1)}, u32[]{:S(2)}, u32[]{:S(2)}) collective-permute-start(bf16[1024,512]{1,0:T(8,128)(2,1)S(1)} %half_product.3), channel_id=1, source_target_pairs={{0,1},{1,0},{2,3},{3,2},{4,5},{5,4},{6,7},{7,6},{8,9},{9,8},{10,11... | collective-permute-start | bytes 3145736 | tf_op jit(solution)/shard_map/ppermute | solution.py:195
  157.8 5.0 %copy-start.2 = (bf16[1664,512]{1,0:T(8,128)(2,1)S(1)}, bf16[1664,512]{1,0:T(8,128)(2,1)}, u32[]{:S(2)}) copy-start(bf16[1664,512]{1,0:T(8,128)(2,1)} %copy-done.1) | copy-start | bytes 5111812
  157.8 20.6 %all-to-all-start.4 = ((bf16[8,128,512]{2,1,0:T(8,128)(2,1)}), bf16[8,128,512]{2,1,0:T(8,128)(2,1)S(1)}, u32[]{:S(2)}, u32[]{:S(2)}) async-start(bf16[8,128,512]{2,1,0:T(8,128)(2,1)} %bitcast.9), calls=%async_computation.4 | async-start | bytes 2097152 | tf_op jit(solution)/shard_map/all_to_all | solution.py:198
Sparse Core Ops, SparseCore 0:
  46.6 98.5 all-gather.1

commit v9 on v8

--- a/solution.py
+++ b/solution.py
@@ -11,7 +11,7 @@
 SIZES = (8, 4, 4, 2, 2)
 FSDP = ("z", "h")
 TENSOR = ("x", "l", "c")
-PACK_STEPS = 4
+PACK_STEPS = 8
 
 
 def pack_kernel(in_ref, *refs):
@@ -42,7 +42,6 @@
         in_specs=[pl.BlockSpec((rows, width // PACK_STEPS), lambda i: (0, i))],
         out_specs=(block,) * parts,
         scratch_shapes=[pltpu.VMEM((parts, packed_rows, TILE), jnp.float32)],
-        compiler_params=pltpu.CompilerParams(vmem_limit_bytes=12 << 20),
         name="pack",
     )(old_codes)
 

time: 187 us -> 189 us (1.011)
  Pallas kernels: 13.8 us -> 17.6 us
    pallas_call x1, Pallas kernels: 1.94 us -> 5.67 us  [pack(): pl.pallas_call(pack_kernel, out_shape=(shape,) * parts, grid=(PACK_STEPS,...]
    unnamed x12 -> x10, local copies, waits for them, and re-layouts: 5.7 us -> 4.2 us
where the time goes in v9:
time: 189 us; the launch traced here: 188 us
  waiting for transfers between devices  69.1 us (37%)
  blocking collectives  48.9 us (26%)
  starting transfers between devices  29.9 us (16%)
  Pallas kernels  17.6 us (9%)
  between operations  14.1 us (7%)
  local copies, waits for them, and re-layouts  5.11 us (3%)
  other arithmetic  3.56 us (2%)
    all_to_all x1, blocking collectives, body(): lax.all_to_all(swapped(along_z, n_z), 'h', split_axis=0, concat_axis=0, t...  29 us
    all_to_all x1, waiting for transfers between devices, body(): lax.all_to_all(direct, FSDP, split_axis=0, concat_axis=0, tiled=True)  25.5 us
    all_to_all x1, waiting for transfers between devices, body(): lax.all_to_all(sectioned.reshape(n_tensor, per_owner * packed_rows, TILE)...  22.1 us
    all_gather x1, blocking collectives, body(): near = lax.all_gather(hidden, 'h', axis=0, tiled=True)  19.9 us
    all_to_all x1, waiting for transfers between devices, body(): lax.all_to_all(share, ('x', 'l'), split_axis=0, concat_axis=0, tiled=True)  12.6 us
    all_to_all x1, starting transfers between devices, body(): lax.all_to_all(staged, 'z', split_axis=0, concat_axis=0, tiled=True)  10.9 us
    pallas_call x2, Pallas kernels, half_product(): pl.pallas_call(half_product_kernel, out_shape=jax.ShapeDtypeStruct((count...  8.62 us
    all_to_all x1, starting transfers between devices, body(): lax.all_to_all(sectioned.reshape(n_tensor, per_owner * packed_rows, TILE)...  7.15 us
  transfers between devices with their start and end apart: 6, of which 5 were waited for; matrix products, arithmetic and copies ran while one was open for 3% of the time, Pallas kernels for 4%

profile of v9, /device:TPU:1, one launch (start us, length us, event | category | flops | bytes accessed | tf_op | source)
XLA Modules:
  0.0 188.3 jit_solution(13070581964850152601)
XLA Ops:
  7.2 0.0 copy-start.2
  7.2 5.7 %pack.1 = (bf16[32,104,128]{2,1,0:T(8,128)(2,1)}, bf16[32,104,128]{2,1,0:T(8,128)(2,1)}) custom-call(bf16[52,16384]{1,0:T(8,128)(2,1)} %in_ref.1), custom_call_target="tpu_custom_call" | custom-call | tf_op jit(solution)/shard_map/pack/pallas_call | solution.py:38
  12.9 10.9 %all-to-all-start = ((bf16[32,104,128]{2,1,0:T(8,128)(2,1)}), bf16[32,104,128]{2,1,0:T(8,128)(2,1)S(1)}, u32[]{:S(2)}, u32[]{:S(2)}) async-start(bf16[32,104,128]{2,1,0:T(8,128)(2,1)} %get-tuple-element.12), calls=%async_computation | async-start | bytes 1703936 | tf_op jit(solution)/shard_map/all_to_all | solution.py:167
  23.7 0.0 all-gather.2.cloned.1.call-start
  23.8 0.1 fusion.4
  23.9 19.9 %all_gather.6 = bf16[256,1664]{1,0:T(8,128)(2,1)} all-gather(bf16[64,1664]{1,0:T(8,128)(2,1)S(1)} %fusion.4), channel_id=1, replica_groups=mesh['z'=8,'h'=4,'x'=4,'l'=2,'c'=2] {'h'}, dimensions={0}, use_global_device_ids=true | all-gather | bytes 1064960 | tf_op jit(solution)/shard_map/all_gather | solution.py:157
  43.8 4.9 %all-to-all-done = bf16[32,104,128]{2,1,0:T(8,128)(2,1)S(1)} async-done(((bf16[32,104,128]{2,1,0:T(8,128)(2,1)}), bf16[32,104,128]{2,1,0:T(8,128)(2,1)S(1)}, u32[]{:S(2)}, u32[]{:S(2)}) %all-to-all-start) | async-done | bytes 852000 | tf_op jit(solution)/shard_map/all_to_all | solution.py:167
  48.7 0.0 all-gather.2.cloned.1.call-update
  48.7 0.1 copy.9
  48.8 29.0 %all_to_all.29 = bf16[32,104,128]{2,1,0:T(8,128)(2,1)S(1)} all-to-all(bf16[32,104,128]{2,1,0:T(8,128)(2,1)S(1)} %bitcast.19), channel_id=1, replica_groups=mesh['z'=8,'h'=4,'x'=4,'l'=2,'c'=2] {'h'}, dimensions={0} | all-to-all | bytes 1703936 | tf_op jit(solution)/shard_map/all_to_all | solution.py:170
  77.8 4.3 %all-to-all-start.2 = ((bf16[32,104,128]{2,1,0:T(8,128)(2,1)}), bf16[32,104,128]{2,1,0:T(8,128)(2,1)S(1)}, u32[]{:S(2)}, u32[]{:S(2)}) async-start(bf16[32,104,128]{2,1,0:T(8,128)(2,1)} %get-tuple-element.17), calls=%async_computation.2 | async-start | bytes 1703936 | tf_op jit(solution)/shard_map/all_to_all | solution.py:172
  82.1 0.1 copy.10
  82.2 25.5 %all-to-all-done.2 = bf16[32,104,128]{2,1,0:T(8,128)(2,1)S(1)} async-done(((bf16[32,104,128]{2,1,0:T(8,128)(2,1)}), bf16[32,104,128]{2,1,0:T(8,128)(2,1)S(1)}, u32[]{:S(2)}, u32[]{:S(2)}) %all-to-all-start.2) | async-done | bytes 852000 | tf_op jit(solution)/shard_map/all_to_all | solution.py:172
  107.7 1.3 pad_maximum_fusion
  109.0 7.2 %all-to-all-start.3 = ((bf16[16,416,128]{2,1,0:T(8,128)(2,1)}), bf16[16,416,128]{2,1,0:T(8,128)(2,1)S(1)}, u32[]{:S(2)}, u32[]{:S(2)}) async-start(bf16[16,416,128]{2,1,0:T(8,128)(2,1)} %bitcast.7), calls=%async_computation.3 | async-start | bytes 3407872 | tf_op jit(solution)/shard_map/all_to_all | solution.py:174
  116.2 0.8 dynamic_slice.3.scale_ref
  117.0 22.1 %all-to-all-done.3 = bf16[16,416,128]{2,1,0:T(8,128)(2,1)S(1)} async-done(((bf16[16,416,128]{2,1,0:T(8,128)(2,1)}), bf16[16,416,128]{2,1,0:T(8,128)(2,1)S(1)}, u32[]{:S(2)}, u32[]{:S(2)}) %all-to-all-start.3) | async-done | bytes 1703968 | tf_op jit(solution)/shard_map/all_to_all | solution.py:174
  139.1 3.3 %requantize.1 = (bf16[1664,512]{1,0:T(8,128)(2,1)S(1)}, bf16[1664,512]{1,0:T(8,128)(2,1)S(1)}, f32[13,128]{1,0:T(8,128)S(1)}) custom-call(f32[13,4]{1,0:T(8,128)S(1)} %dynamic_slice.3.scale_ref, bf16[16,2,208,128]{3,2,1,0:T(8,128)(2,1)S(1)} %bitcast.15), custom_call_target="tpu_custom_call" | custom-call | tf_op jit(solution)/shard_map/requantize/pallas_call | solution.py:89
  142.4 0.0 copy-start
  142.4 1.2 copy-done
  143.6 3.9 %all-gather.2.cloned.1.call-done.even_ref.odd_ref = bf16[2048,1664]{1,0:T(8,128)(2,1)} async-done(((bf16[256,1664]{1,0:T(8,128)(2,1)}), bf16[2048,1664]{1,0:T(8,128)(2,1)}) %all-gather.2.cloned.1.call-update) | async-done | bytes 6815760 | tf_op jit(solution)/shard_map/all_gather | solution.py:169
  147.5 4.3 %half_product.3 = bf16[1024,512]{1,0:T(8,128)(2,1)S(1)} custom-call(s32[1]{0:T(128)S(6)} %sub.3.parity_ref, bf16[2048,1664]{1,0:T(8,128)(2,1)} %all-gather.2.cloned.1.call-done.even_ref.odd_ref, bf16[2048,1664]{1,0:T(8,128)(2,1)} %all-gather.2.cloned.1.call-done.even_ref.odd_ref, bf16[1664,512]{1,0:T(8,128)(2,1)S(1)} %get-tuple-element.18.weight_ref), custom_call_target="tpu_custom_call" | custom-call | flops 1744830464 | bytes 6160384 | tf_op jit(solution)/shard_map/half_product/pallas_call | solution.py:118
  151.8 2.6 %collective-permute-start = (bf16[1024,512]{1,0:T(8,128)(2,1)S(1)}, bf16[1024,512]{1,0:T(8,128)(2,1)S(1)}, u32[]{:S(2)}, u32[]{:S(2)}) collective-permute-start(bf16[1024,512]{1,0:T(8,128)(2,1)S(1)} %half_product.3), channel_id=1, source_target_pairs={{0,1},{1,0},{2,3},{3,2},{4,5},{5,4},{6,7},{7,6},{8,9},{9,8},{10,11... | collective-permute-start | bytes 3145736 | tf_op jit(solution)/shard_map/ppermute | solution.py:194
  154.4 4.3 %half_product.2 = bf16[1024,512]{1,0:T(8,128)(2,1)S(1)} custom-call(s32[1]{0:T(128)} %bitcast.parity_ref, bf16[2048,1664]{1,0:T(8,128)(2,1)} %all-gather.2.cloned.1.call-done.even_ref.odd_ref, bf16[2048,1664]{1,0:T(8,128)(2,1)} %all-gather.2.cloned.1.call-done.even_ref.odd_ref, bf16[1664,512]{1,0:T(8,128)(2,1)S(1)} %get-tuple-element.18.weight_ref), custom_call_target="tpu_custom_call" | custom-call | flops 1744830464 | bytes 6160384 | tf_op jit(solution)/shard_map/half_product/pallas_call | solution.py:118
  158.7 0.0 collective-permute-done
  158.7 1.3 add_convert_fusion
  160.0 5.0 %all-to-all-start.4 = ((bf16[8,128,512]{2,1,0:T(8,128)(2,1)}), bf16[8,128,512]{2,1,0:T(8,128)(2,1)S(1)}, u32[]{:S(2)}, u32[]{:S(2)}) async-start(bf16[8,128,512]{2,1,0:T(8,128)(2,1)} %bitcast.9), calls=%async_computation.4 | async-start | bytes 2097152 | tf_op jit(solution)/shard_map/all_to_all | solution.py:197
  165.1 0.0 copy-done.1
  165.1 2.3 %copy.11 = bf16[512,1664]{1,0:T(8,128)(2,1)} copy(bf16[512,1664]{0,1:T(8,128)(2,1)S(1)} %bitcast.16) | data formatting | bytes 3407872
  167.4 0.7 copy.12
  168.1 12.6 %all-to-all-done.4 = bf16[8,128,512]{2,1,0:T(8,128)(2,1)S(1)} async-done(((bf16[8,128,512]{2,1,0:T(8,128)(2,1)}), bf16[8,128,512]{2,1,0:T(8,128)(2,1)S(1)}, u32[]{:S(2)}, u32[]{:S(2)}) %all-to-all-start.4) | async-done | bytes 1048608 | tf_op jit(solution)/shard_map/all_to_all | solution.py:197
  180.6 0.8 reduce_sum.12
  (5 shorter events, 0.0 us)
Async XLA Ops:
  7.2 16.6 %copy-start.2 = (bf16[64,1664]{1,0:T(8,128)(2,1)S(1)}, bf16[64,1664]{1,0:T(8,128)(2,1)}, u32[]{:S(2)}) copy-start(bf16[64,1664]{1,0:T(8,128)(2,1)} %param.7) | copy-start | bytes 638980
  7.2 16.6 %copy-start.3 = (bf16[64,1664]{1,0:T(8,128)(2,1)S(1)}, bf16[64,1664]{1,0:T(8,128)(2,1)}, u32[]{:S(2)}) copy-start(bf16[64,1664]{1,0:T(8,128)(2,1)} %param.6) | copy-start | bytes 638980
  12.9 35.8 %all-to-all-start = ((bf16[32,104,128]{2,1,0:T(8,128)(2,1)}), bf16[32,104,128]{2,1,0:T(8,128)(2,1)S(1)}, u32[]{:S(2)}, u32[]{:S(2)}) async-start(bf16[32,104,128]{2,1,0:T(8,128)(2,1)} %get-tuple-element.12), calls=%async_computation | async-start | bytes 1703936 | tf_op jit(solution)/shard_map/all_to_all | solution.py:167
  23.7 123.8 %all-gather.2.cloned.1.call-start = ((), (), s32[]{:S(2)}) async-start(), calls=%async_computation.5 | async-start | bytes 7667712 | tf_op jit(solution)/shard_map/all_gather | solution.py:169
  77.8 29.9 %all-to-all-start.2 = ((bf16[32,104,128]{2,1,0:T(8,128)(2,1)}), bf16[32,104,128]{2,1,0:T(8,128)(2,1)S(1)}, u32[]{:S(2)}, u32[]{:S(2)}) async-start(bf16[32,104,128]{2,1,0:T(8,128)(2,1)} %get-tuple-element.17), calls=%async_computation.2 | async-start | bytes 1703936 | tf_op jit(solution)/shard_map/all_to_all | solution.py:172
  109.0 30.1 %all-to-all-start.3 = ((bf16[16,416,128]{2,1,0:T(8,128)(2,1)}), bf16[16,416,128]{2,1,0:T(8,128)(2,1)S(1)}, u32[]{:S(2)}, u32[]{:S(2)}) async-start(bf16[16,416,128]{2,1,0:T(8,128)(2,1)} %bitcast.7), calls=%async_computation.3 | async-start | bytes 3407872 | tf_op jit(solution)/shard_map/all_to_all | solution.py:174
  142.4 1.2 copy-start
  151.8 6.9 %collective-permute-start = (bf16[1024,512]{1,0:T(8,128)(2,1)S(1)}, bf16[1024,512]{1,0:T(8,128)(2,1)S(1)}, u32[]{:S(2)}, u32[]{:S(2)}) collective-permute-start(bf16[1024,512]{1,0:T(8,128)(2,1)S(1)} %half_product.3), channel_id=1, source_target_pairs={{0,1},{1,0},{2,3},{3,2},{4,5},{5,4},{6,7},{7,6},{8,9},{9,8},{10,11... | collective-permute-start | bytes 3145736 | tf_op jit(solution)/shard_map/ppermute | solution.py:194
  160.0 5.0 %copy-start.1 = (bf16[1664,512]{1,0:T(8,128)(2,1)S(1)}, bf16[1664,512]{1,0:T(8,128)(2,1)}, u32[]{:S(2)}) copy-start(bf16[1664,512]{1,0:T(8,128)(2,1)} %copy-done) | copy-start | bytes 5111812
  160.0 20.6 %all-to-all-start.4 = ((bf16[8,128,512]{2,1,0:T(8,128)(2,1)}), bf16[8,128,512]{2,1,0:T(8,128)(2,1)S(1)}, u32[]{:S(2)}, u32[]{:S(2)}) async-start(bf16[8,128,512]{2,1,0:T(8,128)(2,1)} %bitcast.9), calls=%async_computation.4 | async-start | bytes 2097152 | tf_op jit(solution)/shard_map/all_to_all | solution.py:197
Sparse Core Ops, SparseCore 0:
  48.8 98.5 all-gather.1

commit v10 on v9

--- a/solution.py
+++ b/solution.py
@@ -11,7 +11,7 @@
 SIZES = (8, 4, 4, 2, 2)
 FSDP = ("z", "h")
 TENSOR = ("x", "l", "c")
-PACK_STEPS = 8
+PACK_STEPS = 2
 
 
 def pack_kernel(in_ref, *refs):
@@ -42,6 +42,7 @@
         in_specs=[pl.BlockSpec((rows, width // PACK_STEPS), lambda i: (0, i))],
         out_specs=(block,) * parts,
         scratch_shapes=[pltpu.VMEM((parts, packed_rows, TILE), jnp.float32)],
+        compiler_params=pltpu.CompilerParams(vmem_limit_bytes=16 << 20),
         name="pack",
     )(old_codes)
 

time: 189 us -> 186 us (0.984)
  Pallas kernels: 17.6 us -> 13.4 us
    pallas_call x1, Pallas kernels: 5.67 us -> 1.53 us  [pack(): pl.pallas_call(pack_kernel, out_shape=(shape,) * parts, grid=(PACK_STEPS,...]
    unnamed x10 -> x12, local copies, waits for them, and re-layouts: 4.2 us -> 5.7 us
where the time goes in v10:
time: 186 us
  waiting for transfers between devices  69.1 us (37%)
  blocking collectives  48.9 us (26%)
  starting transfers between devices  29.9 us (16%)
  between operations  14.1 us (8%)
  Pallas kernels  13.4 us (7%)
  local copies, waits for them, and re-layouts  6.61 us (4%)
  other arithmetic  3.54 us (2%)
    all_to_all x1, blocking collectives, body(): lax.all_to_all(swapped(along_z, n_z), 'h', split_axis=0, concat_axis=0, t...  29 us
    all_to_all x1, waiting for transfers between devices, body(): lax.all_to_all(direct, FSDP, split_axis=0, concat_axis=0, tiled=True)  25.6 us
    all_to_all x1, waiting for transfers between devices, body(): lax.all_to_all(sectioned.reshape(n_tensor, per_owner * packed_rows, TILE)...  22.1 us
    all_gather x1, blocking collectives, body(): near = lax.all_gather(hidden, 'h', axis=0, tiled=True)  19.9 us
    all_to_all x1, waiting for transfers between devices, body(): lax.all_to_all(share, ('x', 'l'), split_axis=0, concat_axis=0, tiled=True)  12.6 us
    all_to_all x1, starting transfers between devices, body(): lax.all_to_all(staged, 'z', split_axis=0, concat_axis=0, tiled=True)  10.9 us
    pallas_call x2, Pallas kernels, half_product(): pl.pallas_call(half_product_kernel, out_shape=jax.ShapeDtypeStruct((count...  8.61 us
    all_to_all x1, starting transfers between devices, body(): lax.all_to_all(sectioned.reshape(n_tensor, per_owner * packed_rows, TILE)...  7.13 us
  transfers between devices with their start and end apart: 6, of which 5 were waited for; matrix products, arithmetic and copies ran while one was open for 3% of the time, Pallas kernels for 4%

profile of v10, /device:TPU:1, one launch (start us, length us, event | category | flops | bytes accessed | tf_op | source)
XLA Modules:
  0.0 185.6 jit_solution(909555201665187125)
XLA Ops:
  7.2 0.0 copy-start
  7.2 1.5 copy-done
  8.7 1.5 pack.1
  10.2 10.9 %all-to-all-start = ((bf16[32,104,128]{2,1,0:T(8,128)(2,1)}), bf16[32,104,128]{2,1,0:T(8,128)(2,1)S(1)}, u32[]{:S(2)}, u32[]{:S(2)}) async-start(bf16[32,104,128]{2,1,0:T(8,128)(2,1)} %get-tuple-element.12), calls=%async_computation | async-start | bytes 1703936 | tf_op jit(solution)/shard_map/all_to_all | solution.py:168
  21.1 0.0 all-gather.2.cloned.1.call-start
  21.1 0.1 fusion.4
  21.3 19.9 %all_gather.6 = bf16[256,1664]{1,0:T(8,128)(2,1)} all-gather(bf16[64,1664]{1,0:T(8,128)(2,1)S(1)} %fusion.4), channel_id=1, replica_groups=mesh['z'=8,'h'=4,'x'=4,'l'=2,'c'=2] {'h'}, dimensions={0}, use_global_device_ids=true | all-gather | bytes 1064960 | tf_op jit(solution)/shard_map/all_gather | solution.py:158
  41.1 4.9 %all-to-all-done = bf16[32,104,128]{2,1,0:T(8,128)(2,1)S(1)} async-done(((bf16[32,104,128]{2,1,0:T(8,128)(2,1)}), bf16[32,104,128]{2,1,0:T(8,128)(2,1)S(1)}, u32[]{:S(2)}, u32[]{:S(2)}) %all-to-all-start) | async-done | bytes 852000 | tf_op jit(solution)/shard_map/all_to_all | solution.py:168
  46.0 0.0 all-gather.2.cloned.1.call-update
  46.1 0.1 copy.9
  46.1 29.0 %all_to_all.29 = bf16[32,104,128]{2,1,0:T(8,128)(2,1)S(1)} all-to-all(bf16[32,104,128]{2,1,0:T(8,128)(2,1)S(1)} %bitcast.19), channel_id=1, replica_groups=mesh['z'=8,'h'=4,'x'=4,'l'=2,'c'=2] {'h'}, dimensions={0} | all-to-all | bytes 1703936 | tf_op jit(solution)/shard_map/all_to_all | solution.py:171
  75.2 4.3 %all-to-all-start.2 = ((bf16[32,104,128]{2,1,0:T(8,128)(2,1)}), bf16[32,104,128]{2,1,0:T(8,128)(2,1)S(1)}, u32[]{:S(2)}, u32[]{:S(2)}) async-start(bf16[32,104,128]{2,1,0:T(8,128)(2,1)} %get-tuple-element.17), calls=%async_computation.2 | async-start | bytes 1703936 | tf_op jit(solution)/shard_map/all_to_all | solution.py:173
  79.5 0.1 copy.10
  79.5 25.6 %all-to-all-done.2 = bf16[32,104,128]{2,1,0:T(8,128)(2,1)S(1)} async-done(((bf16[32,104,128]{2,1,0:T(8,128)(2,1)}), bf16[32,104,128]{2,1,0:T(8,128)(2,1)S(1)}, u32[]{:S(2)}, u32[]{:S(2)}) %all-to-all-start.2) | async-done | bytes 852000 | tf_op jit(solution)/shard_map/all_to_all | solution.py:173
  105.1 1.3 pad_maximum_fusion
  106.4 7.1 %all-to-all-start.3 = ((bf16[16,416,128]{2,1,0:T(8,128)(2,1)}), bf16[16,416,128]{2,1,0:T(8,128)(2,1)S(1)}, u32[]{:S(2)}, u32[]{:S(2)}) async-start(bf16[16,416,128]{2,1,0:T(8,128)(2,1)} %bitcast.7), calls=%async_computation.3 | async-start | bytes 3407872 | tf_op jit(solution)/shard_map/all_to_all | solution.py:175
  113.5 0.8 dynamic_slice.3.scale_ref
  114.3 22.1 %all-to-all-done.3 = bf16[16,416,128]{2,1,0:T(8,128)(2,1)S(1)} async-done(((bf16[16,416,128]{2,1,0:T(8,128)(2,1)}), bf16[16,416,128]{2,1,0:T(8,128)(2,1)S(1)}, u32[]{:S(2)}, u32[]{:S(2)}) %all-to-all-start.3) | async-done | bytes 1703968 | tf_op jit(solution)/shard_map/all_to_all | solution.py:175
  136.4 3.3 %requantize.1 = (bf16[1664,512]{1,0:T(8,128)(2,1)S(1)}, bf16[1664,512]{1,0:T(8,128)(2,1)S(1)}, f32[13,128]{1,0:T(8,128)S(1)}) custom-call(f32[13,4]{1,0:T(8,128)S(1)} %dynamic_slice.3.scale_ref, bf16[16,2,208,128]{3,2,1,0:T(8,128)(2,1)S(1)} %bitcast.15), custom_call_target="tpu_custom_call" | custom-call | tf_op jit(solution)/shard_map/requantize/pallas_call | solution.py:90
  139.7 0.0 copy-start.1
  139.7 1.2 copy-done.1
  140.9 3.9 %all-gather.2.cloned.1.call-done.even_ref.odd_ref = bf16[2048,1664]{1,0:T(8,128)(2,1)} async-done(((bf16[256,1664]{1,0:T(8,128)(2,1)}), bf16[2048,1664]{1,0:T(8,128)(2,1)}) %all-gather.2.cloned.1.call-update) | async-done | bytes 6815760 | tf_op jit(solution)/shard_map/all_gather | solution.py:170
  144.8 4.3 %half_product.3 = bf16[1024,512]{1,0:T(8,128)(2,1)S(1)} custom-call(s32[1]{0:T(128)S(6)} %sub.3.parity_ref, bf16[2048,1664]{1,0:T(8,128)(2,1)} %all-gather.2.cloned.1.call-done.even_ref.odd_ref, bf16[2048,1664]{1,0:T(8,128)(2,1)} %all-gather.2.cloned.1.call-done.even_ref.odd_ref, bf16[1664,512]{1,0:T(8,128)(2,1)S(1)} %get-tuple-element.18.weight_ref), custom_call_target="tpu_custom_call" | custom-call | flops 1744830464 | bytes 6160384 | tf_op jit(solution)/shard_map/half_product/pallas_call | solution.py:119
  149.1 2.6 %collective-permute-start = (bf16[1024,512]{1,0:T(8,128)(2,1)S(1)}, bf16[1024,512]{1,0:T(8,128)(2,1)S(1)}, u32[]{:S(2)}, u32[]{:S(2)}) collective-permute-start(bf16[1024,512]{1,0:T(8,128)(2,1)S(1)} %half_product.3), channel_id=1, source_target_pairs={{0,1},{1,0},{2,3},{3,2},{4,5},{5,4},{6,7},{7,6},{8,9},{9,8},{10,11... | collective-permute-start | bytes 3145736 | tf_op jit(solution)/shard_map/ppermute | solution.py:195
  151.7 4.3 %half_product.2 = bf16[1024,512]{1,0:T(8,128)(2,1)S(1)} custom-call(s32[1]{0:T(128)} %bitcast.parity_ref, bf16[2048,1664]{1,0:T(8,128)(2,1)} %all-gather.2.cloned.1.call-done.even_ref.odd_ref, bf16[2048,1664]{1,0:T(8,128)(2,1)} %all-gather.2.cloned.1.call-done.even_ref.odd_ref, bf16[1664,512]{1,0:T(8,128)(2,1)S(1)} %get-tuple-element.18.weight_ref), custom_call_target="tpu_custom_call" | custom-call | flops 1744830464 | bytes 6160384 | tf_op jit(solution)/shard_map/half_product/pallas_call | solution.py:119
  156.1 0.0 collective-permute-done
  156.1 1.3 add_convert_fusion
  157.3 5.0 %all-to-all-start.4 = ((bf16[8,128,512]{2,1,0:T(8,128)(2,1)}), bf16[8,128,512]{2,1,0:T(8,128)(2,1)S(1)}, u32[]{:S(2)}, u32[]{:S(2)}) async-start(bf16[8,128,512]{2,1,0:T(8,128)(2,1)} %bitcast.9), calls=%async_computation.4 | async-start | bytes 2097152 | tf_op jit(solution)/shard_map/all_to_all | solution.py:198
  162.4 2.3 %copy.11 = bf16[512,1664]{1,0:T(8,128)(2,1)} copy(bf16[512,1664]{0,1:T(8,128)(2,1)S(1)} %bitcast.16) | data formatting | bytes 3407872
  164.7 0.7 copy.12
  165.4 12.6 %all-to-all-done.4 = bf16[8,128,512]{2,1,0:T(8,128)(2,1)S(1)} async-done(((bf16[8,128,512]{2,1,0:T(8,128)(2,1)}), bf16[8,128,512]{2,1,0:T(8,128)(2,1)S(1)}, u32[]{:S(2)}, u32[]{:S(2)}) %all-to-all-start.4) | async-done | bytes 1048608 | tf_op jit(solution)/shard_map/all_to_all | solution.py:198
  178.0 0.8 reduce_sum.12
  (7 shorter events, 0.0 us)
Async XLA Ops:
  7.2 1.5 copy-start
  8.7 12.4 %copy-start.3 = (bf16[64,1664]{1,0:T(8,128)(2,1)S(1)}, bf16[64,1664]{1,0:T(8,128)(2,1)}, u32[]{:S(2)}) copy-start(bf16[64,1664]{1,0:T(8,128)(2,1)} %param.7) | copy-start | bytes 638980
  8.7 12.5 %copy-start.4 = (bf16[64,1664]{1,0:T(8,128)(2,1)S(1)}, bf16[64,1664]{1,0:T(8,128)(2,1)}, u32[]{:S(2)}) copy-start(bf16[64,1664]{1,0:T(8,128)(2,1)} %param.6) | copy-start | bytes 638980
  10.2 35.8 %all-to-all-start = ((bf16[32,104,128]{2,1,0:T(8,128)(2,1)}), bf16[32,104,128]{2,1,0:T(8,128)(2,1)S(1)}, u32[]{:S(2)}, u32[]{:S(2)}) async-start(bf16[32,104,128]{2,1,0:T(8,128)(2,1)} %get-tuple-element.12), calls=%async_computation | async-start | bytes 1703936 | tf_op jit(solution)/shard_map/all_to_all | solution.py:168
  21.1 123.8 %all-gather.2.cloned.1.call-start = ((), (), s32[]{:S(2)}) async-start(), calls=%async_computation.5 | async-start | bytes 7667712 | tf_op jit(solution)/shard_map/all_gather | solution.py:170
  75.2 29.9 %all-to-all-start.2 = ((bf16[32,104,128]{2,1,0:T(8,128)(2,1)}), bf16[32,104,128]{2,1,0:T(8,128)(2,1)S(1)}, u32[]{:S(2)}, u32[]{:S(2)}) async-start(bf16[32,104,128]{2,1,0:T(8,128)(2,1)} %get-tuple-element.17), calls=%async_computation.2 | async-start | bytes 1703936 | tf_op jit(solution)/shard_map/all_to_all | solution.py:173
  106.4 30.0 %all-to-all-start.3 = ((bf16[16,416,128]{2,1,0:T(8,128)(2,1)}), bf16[16,416,128]{2,1,0:T(8,128)(2,1)S(1)}, u32[]{:S(2)}, u32[]{:S(2)}) async-start(bf16[16,416,128]{2,1,0:T(8,128)(2,1)} %bitcast.7), calls=%async_computation.3 | async-start | bytes 3407872 | tf_op jit(solution)/shard_map/all_to_all | solution.py:175
  139.7 1.2 copy-start.1
  149.1 6.9 %collective-permute-start = (bf16[1024,512]{1,0:T(8,128)(2,1)S(1)}, bf16[1024,512]{1,0:T(8,128)(2,1)S(1)}, u32[]{:S(2)}, u32[]{:S(2)}) collective-permute-start(bf16[1024,512]{1,0:T(8,128)(2,1)S(1)} %half_product.3), channel_id=1, source_target_pairs={{0,1},{1,0},{2,3},{3,2},{4,5},{5,4},{6,7},{7,6},{8,9},{9,8},{10,11... | collective-permute-start | bytes 3145736 | tf_op jit(solution)/shard_map/ppermute | solution.py:195
  157.3 5.0 %copy-start.2 = (bf16[1664,512]{1,0:T(8,128)(2,1)S(1)}, bf16[1664,512]{1,0:T(8,128)(2,1)}, u32[]{:S(2)}) copy-start(bf16[1664,512]{1,0:T(8,128)(2,1)} %copy-done.1) | copy-start | bytes 5111812
  157.3 20.6 %all-to-all-start.4 = ((bf16[8,128,512]{2,1,0:T(8,128)(2,1)}), bf16[8,128,512]{2,1,0:T(8,128)(2,1)S(1)}, u32[]{:S(2)}, u32[]{:S(2)}) async-start(bf16[8,128,512]{2,1,0:T(8,128)(2,1)} %bitcast.9), calls=%async_computation.4 | async-start | bytes 2097152 | tf_op jit(solution)/shard_map/all_to_all | solution.py:198
Sparse Core Ops, SparseCore 0:
  46.2 98.5 all-gather.1

commit v11 on v10

--- a/solution.py
+++ b/solution.py
@@ -1,3 +1,5 @@
+import functools
+
 import jax
 import jax.numpy as jnp
 from jax import lax
@@ -12,6 +14,7 @@
 FSDP = ("z", "h")
 TENSOR = ("x", "l", "c")
 PACK_STEPS = 2
+GROUP = 4
 
 
 def pack_kernel(in_ref, *refs):
@@ -105,11 +108,16 @@
     )(scale_block, moved)
 
 
-def half_product_kernel(parity_ref, even_ref, odd_ref, weight_ref, out_ref):
-    tokens = jnp.concatenate([even_ref[...], odd_ref[...]], axis=0)
+def half_product_kernel(parity_ref, *refs):
+    *token_refs, weight_ref, out_ref = refs
+    tokens = jnp.concatenate([ref[...] for ref in token_refs], axis=0)
     out_ref[...] = jnp.dot(
         tokens, weight_ref[...], preferred_element_type=jnp.float32
     ).astype(jnp.bfloat16)
+
+
+def owner_block(member, step, parity_ref):
+    return 2 * (step * GROUP + member) + parity_ref[0], 0
 
 
 def half_product(every, weight, parity, owners):
@@ -121,22 +129,22 @@
         out_shape=jax.ShapeDtypeStruct((count, width), jnp.bfloat16),
         grid_spec=pltpu.PrefetchScalarGridSpec(
             num_scalar_prefetch=1,
-            grid=(owners // 4,),
+            grid=(owners // (2 * GROUP),),
             in_specs=[
-                pl.BlockSpec((rows, depth), lambda i, parity: (4 * i + parity[0], 0)),
-                pl.BlockSpec((rows, depth), lambda i, parity: (4 * i + 2 + parity[0], 0)),
-                pl.BlockSpec(memory_space=pltpu.VMEM),
-            ],
-            out_specs=pl.BlockSpec((2 * rows, width), lambda i, parity: (i, 0)),
+                pl.BlockSpec((rows, depth), functools.partial(owner_block, member))
+                for member in range(GROUP)
+            ]
+            + [pl.BlockSpec(memory_space=pltpu.VMEM)],
+            out_specs=pl.BlockSpec((GROUP * rows, width), lambda i, parity: (i, 0)),
         ),
-        compiler_params=pltpu.CompilerParams(vmem_limit_bytes=10 << 20),
+        compiler_params=pltpu.CompilerParams(vmem_limit_bytes=14 << 20),
         cost_estimate=pl.CostEstimate(
             flops=2 * count * depth * width,
             bytes_accessed=2 * (count * depth + depth * width + count * width),
             transcendentals=0,
         ),
         name="half_product",
-    )(parity, every, every, weight)
+    )(parity, *(every,) * GROUP, weight)
 
 
 def body(old_codes, old_scales, gate_pre, up_pre):

time: 186 us -> 185 us (level)
  no operation moved by 1% of the time
where the time goes in v11:
time: 185 us; the launch traced here: 184 us
  waiting for transfers between devices  69.1 us (37%)
  blocking collectives  48.9 us (26%)
  starting transfers between devices  29.9 us (16%)
  between operations  14.1 us (8%)
  Pallas kernels  12.2 us (7%)
  local copies, waits for them, and re-layouts  6.61 us (4%)
  other arithmetic  3.55 us (2%)
    all_to_all x1, blocking collectives, body(): lax.all_to_all(swapped(along_z, n_z), 'h', split_axis=0, concat_axis=0, t...  29 us
    all_to_all x1, waiting for transfers between devices, body(): lax.all_to_all(direct, FSDP, split_axis=0, concat_axis=0, tiled=True)  25.6 us
    all_to_all x1, waiting for transfers between devices, body(): lax.all_to_all(sectioned.reshape(n_tensor, per_owner * packed_rows, TILE)...  22.1 us
    all_gather x1, blocking collectives, body(): near = lax.all_gather(hidden, 'h', axis=0, tiled=True)  19.9 us
    all_to_all x1, waiting for transfers between devices, body(): lax.all_to_all(share, ('x', 'l'), split_axis=0, concat_axis=0, tiled=True)  12.6 us
    all_to_all x1, starting transfers between devices, body(): lax.all_to_all(staged, 'z', split_axis=0, concat_axis=0, tiled=True)  10.9 us
    pallas_call x2, Pallas kernels, half_product(): pl.pallas_call(half_product_kernel, out_shape=jax.ShapeDtypeStruct((count...  7.44 us
    all_to_all x1, starting transfers between devices, body(): lax.all_to_all(sectioned.reshape(n_tensor, per_owner * packed_rows, TILE)...  7.13 us
  transfers between devices with their start and end apart: 6, of which 5 were waited for; matrix products, arithmetic and copies ran while one was open for 3% of the time, Pallas kernels for 4%

profile of v11, /device:TPU:1, one launch (start us, length us, event | category | flops | bytes accessed | tf_op | source)
XLA Modules:
  0.0 184.5 jit_solution(14899473911120748057)
XLA Ops:
  7.2 0.0 copy-start
  7.2 1.5 copy-done
  8.7 1.5 pack.1
  10.2 10.9 %all-to-all-start = ((bf16[32,104,128]{2,1,0:T(8,128)(2,1)}), bf16[32,104,128]{2,1,0:T(8,128)(2,1)S(1)}, u32[]{:S(2)}, u32[]{:S(2)}) async-start(bf16[32,104,128]{2,1,0:T(8,128)(2,1)} %get-tuple-element.12), calls=%async_computation | async-start | bytes 1703936 | tf_op jit(solution)/shard_map/all_to_all | solution.py:176
  21.1 0.0 all-gather.2.cloned.1.call-start
  21.1 0.1 fusion.4
  21.3 19.9 %all_gather.6 = bf16[256,1664]{1,0:T(8,128)(2,1)} all-gather(bf16[64,1664]{1,0:T(8,128)(2,1)S(1)} %fusion.4), channel_id=1, replica_groups=mesh['z'=8,'h'=4,'x'=4,'l'=2,'c'=2] {'h'}, dimensions={0}, use_global_device_ids=true | all-gather | bytes 1064960 | tf_op jit(solution)/shard_map/all_gather | solution.py:166
  41.1 4.9 %all-to-all-done = bf16[32,104,128]{2,1,0:T(8,128)(2,1)S(1)} async-done(((bf16[32,104,128]{2,1,0:T(8,128)(2,1)}), bf16[32,104,128]{2,1,0:T(8,128)(2,1)S(1)}, u32[]{:S(2)}, u32[]{:S(2)}) %all-to-all-start) | async-done | bytes 852000 | tf_op jit(solution)/shard_map/all_to_all | solution.py:176
  46.0 0.0 all-gather.2.cloned.1.call-update
  46.1 0.1 copy.9
  46.1 29.0 %all_to_all.29 = bf16[32,104,128]{2,1,0:T(8,128)(2,1)S(1)} all-to-all(bf16[32,104,128]{2,1,0:T(8,128)(2,1)S(1)} %bitcast.19), channel_id=1, replica_groups=mesh['z'=8,'h'=4,'x'=4,'l'=2,'c'=2] {'h'}, dimensions={0} | all-to-all | bytes 1703936 | tf_op jit(solution)/shard_map/all_to_all | solution.py:179
  75.2 4.3 %all-to-all-start.2 = ((bf16[32,104,128]{2,1,0:T(8,128)(2,1)}), bf16[32,104,128]{2,1,0:T(8,128)(2,1)S(1)}, u32[]{:S(2)}, u32[]{:S(2)}) async-start(bf16[32,104,128]{2,1,0:T(8,128)(2,1)} %get-tuple-element.17), calls=%async_computation.2 | async-start | bytes 1703936 | tf_op jit(solution)/shard_map/all_to_all | solution.py:181
  79.5 0.1 copy.10
  79.5 25.6 %all-to-all-done.2 = bf16[32,104,128]{2,1,0:T(8,128)(2,1)S(1)} async-done(((bf16[32,104,128]{2,1,0:T(8,128)(2,1)}), bf16[32,104,128]{2,1,0:T(8,128)(2,1)S(1)}, u32[]{:S(2)}, u32[]{:S(2)}) %all-to-all-start.2) | async-done | bytes 852000 | tf_op jit(solution)/shard_map/all_to_all | solution.py:181
  105.1 1.3 pad_maximum_fusion
  106.4 7.1 %all-to-all-start.3 = ((bf16[16,416,128]{2,1,0:T(8,128)(2,1)}), bf16[16,416,128]{2,1,0:T(8,128)(2,1)S(1)}, u32[]{:S(2)}, u32[]{:S(2)}) async-start(bf16[16,416,128]{2,1,0:T(8,128)(2,1)} %bitcast.7), calls=%async_computation.3 | async-start | bytes 3407872 | tf_op jit(solution)/shard_map/all_to_all | solution.py:183
  113.5 0.8 dynamic_slice.3.scale_ref
  114.3 22.1 %all-to-all-done.3 = bf16[16,416,128]{2,1,0:T(8,128)(2,1)S(1)} async-done(((bf16[16,416,128]{2,1,0:T(8,128)(2,1)}), bf16[16,416,128]{2,1,0:T(8,128)(2,1)S(1)}, u32[]{:S(2)}, u32[]{:S(2)}) %all-to-all-start.3) | async-done | bytes 1703968 | tf_op jit(solution)/shard_map/all_to_all | solution.py:183
  136.4 3.3 %requantize.1 = (bf16[1664,512]{1,0:T(8,128)(2,1)S(1)}, bf16[1664,512]{1,0:T(8,128)(2,1)S(1)}, f32[13,128]{1,0:T(8,128)S(1)}) custom-call(f32[13,4]{1,0:T(8,128)S(1)} %dynamic_slice.3.scale_ref, bf16[16,2,208,128]{3,2,1,0:T(8,128)(2,1)S(1)} %bitcast.15), custom_call_target="tpu_custom_call" | custom-call | tf_op jit(solution)/shard_map/requantize/pallas_call | solution.py:93
  139.7 0.0 copy-start.1
  139.7 1.2 copy-done.1
  140.9 3.9 %all-gather.2.cloned.1.call-done.refs_0_.refs_1_.refs_2_.refs_3_ = bf16[2048,1664]{1,0:T(8,128)(2,1)} async-done(((bf16[256,1664]{1,0:T(8,128)(2,1)}), bf16[2048,1664]{1,0:T(8,128)(2,1)}) %all-gather.2.cloned.1.call-update) | async-done | bytes 6815760 | tf_op jit(solution)/shard_map/all_gather | solution.py:178
  144.8 3.7 %half_product.3 = bf16[1024,512]{1,0:T(8,128)(2,1)S(1)} custom-call(s32[1]{0:T(128)S(6)} %sub.3.parity_ref, bf16[2048,1664]{1,0:T(8,128)(2,1)} %all-gather.2.cloned.1.call-done.refs_0_.refs_1_.refs_2_.refs_3_, bf16[2048,1664]{1,0:T(8,128)(2,1)} %all-gather.2.cloned.1.call-done.refs_0_.refs_1_.refs_2_.refs_3_, ...), custom_call_target="tpu_custom_call" | custom-call | flops 1744830464 | bytes 6160384 | tf_op jit(solution)/shard_map/half_product/pallas_call | solution.py:127
  148.5 2.6 %collective-permute-start = (bf16[1024,512]{1,0:T(8,128)(2,1)S(1)}, bf16[1024,512]{1,0:T(8,128)(2,1)S(1)}, u32[]{:S(2)}, u32[]{:S(2)}) collective-permute-start(bf16[1024,512]{1,0:T(8,128)(2,1)S(1)} %half_product.3), channel_id=1, source_target_pairs={{0,1},{1,0},{2,3},{3,2},{4,5},{5,4},{6,7},{7,6},{8,9},{9,8},{10,11... | collective-permute-start | bytes 3145736 | tf_op jit(solution)/shard_map/ppermute | solution.py:203
  151.1 3.7 %half_product.2 = bf16[1024,512]{1,0:T(8,128)(2,1)S(1)} custom-call(s32[1]{0:T(128)} %bitcast.parity_ref, bf16[2048,1664]{1,0:T(8,128)(2,1)} %all-gather.2.cloned.1.call-done.refs_0_.refs_1_.refs_2_.refs_3_, bf16[2048,1664]{1,0:T(8,128)(2,1)} %all-gather.2.cloned.1.call-done.refs_0_.refs_1_.refs_2_.refs_3_, ...), custom_call_target="tpu_custom_call" | custom-call | flops 1744830464 | bytes 6160384 | tf_op jit(solution)/shard_map/half_product/pallas_call | solution.py:127
  154.9 0.0 collective-permute-done
  154.9 1.3 add_convert_fusion
  156.2 5.0 %all-to-all-start.4 = ((bf16[8,128,512]{2,1,0:T(8,128)(2,1)}), bf16[8,128,512]{2,1,0:T(8,128)(2,1)S(1)}, u32[]{:S(2)}, u32[]{:S(2)}) async-start(bf16[8,128,512]{2,1,0:T(8,128)(2,1)} %bitcast.9), calls=%async_computation.4 | async-start | bytes 2097152 | tf_op jit(solution)/shard_map/all_to_all | solution.py:206
  161.2 2.3 %copy.11 = bf16[512,1664]{1,0:T(8,128)(2,1)} copy(bf16[512,1664]{0,1:T(8,128)(2,1)S(1)} %bitcast.16) | data formatting | bytes 3407872
  163.6 0.7 copy.12
  164.2 12.6 %all-to-all-done.4 = bf16[8,128,512]{2,1,0:T(8,128)(2,1)S(1)} async-done(((bf16[8,128,512]{2,1,0:T(8,128)(2,1)}), bf16[8,128,512]{2,1,0:T(8,128)(2,1)S(1)}, u32[]{:S(2)}, u32[]{:S(2)}) %all-to-all-start.4) | async-done | bytes 1048608 | tf_op jit(solution)/shard_map/all_to_all | solution.py:206
  176.8 0.8 reduce_sum.12
  (7 shorter events, 0.0 us)
Async XLA Ops:
  7.2 1.5 copy-start
  8.7 12.4 %copy-start.3 = (bf16[64,1664]{1,0:T(8,128)(2,1)S(1)}, bf16[64,1664]{1,0:T(8,128)(2,1)}, u32[]{:S(2)}) copy-start(bf16[64,1664]{1,0:T(8,128)(2,1)} %param.7) | copy-start | bytes 638980
  8.7 12.5 %copy-start.4 = (bf16[64,1664]{1,0:T(8,128)(2,1)S(1)}, bf16[64,1664]{1,0:T(8,128)(2,1)}, u32[]{:S(2)}) copy-start(bf16[64,1664]{1,0:T(8,128)(2,1)} %param.6) | copy-start | bytes 638980
  10.2 35.8 %all-to-all-start = ((bf16[32,104,128]{2,1,0:T(8,128)(2,1)}), bf16[32,104,128]{2,1,0:T(8,128)(2,1)S(1)}, u32[]{:S(2)}, u32[]{:S(2)}) async-start(bf16[32,104,128]{2,1,0:T(8,128)(2,1)} %get-tuple-element.12), calls=%async_computation | async-start | bytes 1703936 | tf_op jit(solution)/shard_map/all_to_all | solution.py:176
  21.1 123.8 %all-gather.2.cloned.1.call-start = ((), (), s32[]{:S(2)}) async-start(), calls=%async_computation.5 | async-start | bytes 7667712 | tf_op jit(solution)/shard_map/all_gather | solution.py:178
  75.2 29.9 %all-to-all-start.2 = ((bf16[32,104,128]{2,1,0:T(8,128)(2,1)}), bf16[32,104,128]{2,1,0:T(8,128)(2,1)S(1)}, u32[]{:S(2)}, u32[]{:S(2)}) async-start(bf16[32,104,128]{2,1,0:T(8,128)(2,1)} %get-tuple-element.17), calls=%async_computation.2 | async-start | bytes 1703936 | tf_op jit(solution)/shard_map/all_to_all | solution.py:181
  106.4 30.0 %all-to-all-start.3 = ((bf16[16,416,128]{2,1,0:T(8,128)(2,1)}), bf16[16,416,128]{2,1,0:T(8,128)(2,1)S(1)}, u32[]{:S(2)}, u32[]{:S(2)}) async-start(bf16[16,416,128]{2,1,0:T(8,128)(2,1)} %bitcast.7), calls=%async_computation.3 | async-start | bytes 3407872 | tf_op jit(solution)/shard_map/all_to_all | solution.py:183
  139.7 1.2 copy-start.1
  148.5 6.3 %collective-permute-start = (bf16[1024,512]{1,0:T(8,128)(2,1)S(1)}, bf16[1024,512]{1,0:T(8,128)(2,1)S(1)}, u32[]{:S(2)}, u32[]{:S(2)}) collective-permute-start(bf16[1024,512]{1,0:T(8,128)(2,1)S(1)} %half_product.3), channel_id=1, source_target_pairs={{0,1},{1,0},{2,3},{3,2},{4,5},{5,4},{6,7},{7,6},{8,9},{9,8},{10,11... | collective-permute-start | bytes 3145736 | tf_op jit(solution)/shard_map/ppermute | solution.py:203
  156.2 5.0 %copy-start.2 = (bf16[1664,512]{1,0:T(8,128)(2,1)S(1)}, bf16[1664,512]{1,0:T(8,128)(2,1)}, u32[]{:S(2)}) copy-start(bf16[1664,512]{1,0:T(8,128)(2,1)} %copy-done.1) | copy-start | bytes 5111812
  156.2 20.6 %all-to-all-start.4 = ((bf16[8,128,512]{2,1,0:T(8,128)(2,1)}), bf16[8,128,512]{2,1,0:T(8,128)(2,1)S(1)}, u32[]{:S(2)}, u32[]{:S(2)}) async-start(bf16[8,128,512]{2,1,0:T(8,128)(2,1)} %bitcast.9), calls=%async_computation.4 | async-start | bytes 2097152 | tf_op jit(solution)/shard_map/all_to_all | solution.py:206
Sparse Core Ops, SparseCore 0:
  46.2 98.5 all-gather.1

commit v12 on v11

--- a/solution.py
+++ b/solution.py
@@ -13,7 +13,7 @@
 SIZES = (8, 4, 4, 2, 2)
 FSDP = ("z", "h")
 TENSOR = ("x", "l", "c")
-PACK_STEPS = 2
+PACK_STEPS = 1
 GROUP = 4
 
 

time: 185 us -> 185 us (level)
  no operation moved by 1% of the time
where the time goes in v12:
time: 185 us
  waiting for transfers between devices  69.1 us (37%)
  blocking collectives  48.9 us (26%)
  starting transfers between devices  29.9 us (16%)
  between operations  14.1 us (8%)
  Pallas kernels  12.3 us (7%)
  local copies, waits for them, and re-layouts  6.61 us (4%)
  other arithmetic  3.55 us (2%)
    all_to_all x1, blocking collectives, body(): lax.all_to_all(swapped(along_z, n_z), 'h', split_axis=0, concat_axis=0, t...  29 us
    all_to_all x1, waiting for transfers between devices, body(): lax.all_to_all(direct, FSDP, split_axis=0, concat_axis=0, tiled=True)  25.6 us
    all_to_all x1, waiting for transfers between devices, body(): lax.all_to_all(sectioned.reshape(n_tensor, per_owner * packed_rows, TILE)...  22.1 us
    all_gather x1, blocking collectives, body(): near = lax.all_gather(hidden, 'h', axis=0, tiled=True)  19.9 us
    all_to_all x1, waiting for transfers between devices, body(): lax.all_to_all(share, ('x', 'l'), split_axis=0, concat_axis=0, tiled=True)  12.6 us
    all_to_all x1, starting transfers between devices, body(): lax.all_to_all(staged, 'z', split_axis=0, concat_axis=0, tiled=True)  10.9 us
    pallas_call x2, Pallas kernels, half_product(): pl.pallas_call(half_product_kernel, out_shape=jax.ShapeDtypeStruct((count...  7.44 us
    all_to_all x1, starting transfers between devices, body(): lax.all_to_all(sectioned.reshape(n_tensor, per_owner * packed_rows, TILE)...  7.13 us
  transfers between devices with their start and end apart: 6, of which 5 were waited for; matrix products, arithmetic and copies ran while one was open for 3% of the time, Pallas kernels for 4%

profile of v12, /device:TPU:1, one launch (start us, length us, event | category | flops | bytes accessed | tf_op | source)
XLA Modules:
  0.0 184.5 jit_solution(15481973791076660502)
XLA Ops:
  7.2 0.0 copy-start
  7.2 1.5 copy-done
  8.7 1.6 pack.1
  10.3 10.9 %all-to-all-start = ((bf16[32,104,128]{2,1,0:T(8,128)(2,1)}), bf16[32,104,128]{2,1,0:T(8,128)(2,1)S(1)}, u32[]{:S(2)}, u32[]{:S(2)}) async-start(bf16[32,104,128]{2,1,0:T(8,128)(2,1)} %get-tuple-element.12), calls=%async_computation | async-start | bytes 1703936 | tf_op jit(solution)/shard_map/all_to_all | solution.py:176
  21.1 0.0 all-gather.2.cloned.1.call-start
  21.2 0.1 fusion.4
  21.4 19.9 %all_gather.6 = bf16[256,1664]{1,0:T(8,128)(2,1)} all-gather(bf16[64,1664]{1,0:T(8,128)(2,1)S(1)} %fusion.4), channel_id=1, replica_groups=mesh['z'=8,'h'=4,'x'=4,'l'=2,'c'=2] {'h'}, dimensions={0}, use_global_device_ids=true | all-gather | bytes 1064960 | tf_op jit(solution)/shard_map/all_gather | solution.py:166
  41.2 4.9 %all-to-all-done = bf16[32,104,128]{2,1,0:T(8,128)(2,1)S(1)} async-done(((bf16[32,104,128]{2,1,0:T(8,128)(2,1)}), bf16[32,104,128]{2,1,0:T(8,128)(2,1)S(1)}, u32[]{:S(2)}, u32[]{:S(2)}) %all-to-all-start) | async-done | bytes 852000 | tf_op jit(solution)/shard_map/all_to_all | solution.py:176
  46.1 0.0 all-gather.2.cloned.1.call-update
  46.1 0.1 copy.9
  46.2 29.0 %all_to_all.29 = bf16[32,104,128]{2,1,0:T(8,128)(2,1)S(1)} all-to-all(bf16[32,104,128]{2,1,0:T(8,128)(2,1)S(1)} %bitcast.19), channel_id=1, replica_groups=mesh['z'=8,'h'=4,'x'=4,'l'=2,'c'=2] {'h'}, dimensions={0} | all-to-all | bytes 1703936 | tf_op jit(solution)/shard_map/all_to_all | solution.py:179
  75.2 4.3 %all-to-all-start.2 = ((bf16[32,104,128]{2,1,0:T(8,128)(2,1)}), bf16[32,104,128]{2,1,0:T(8,128)(2,1)S(1)}, u32[]{:S(2)}, u32[]{:S(2)}) async-start(bf16[32,104,128]{2,1,0:T(8,128)(2,1)} %get-tuple-element.17), calls=%async_computation.2 | async-start | bytes 1703936 | tf_op jit(solution)/shard_map/all_to_all | solution.py:181
  79.5 0.1 copy.10
  79.6 25.6 %all-to-all-done.2 = bf16[32,104,128]{2,1,0:T(8,128)(2,1)S(1)} async-done(((bf16[32,104,128]{2,1,0:T(8,128)(2,1)}), bf16[32,104,128]{2,1,0:T(8,128)(2,1)S(1)}, u32[]{:S(2)}, u32[]{:S(2)}) %all-to-all-start.2) | async-done | bytes 852000 | tf_op jit(solution)/shard_map/all_to_all | solution.py:181
  105.2 1.3 pad_maximum_fusion
  106.5 7.1 %all-to-all-start.3 = ((bf16[16,416,128]{2,1,0:T(8,128)(2,1)}), bf16[16,416,128]{2,1,0:T(8,128)(2,1)S(1)}, u32[]{:S(2)}, u32[]{:S(2)}) async-start(bf16[16,416,128]{2,1,0:T(8,128)(2,1)} %bitcast.7), calls=%async_computation.3 | async-start | bytes 3407872 | tf_op jit(solution)/shard_map/all_to_all | solution.py:183
  113.6 0.8 dynamic_slice.3.scale_ref
  114.4 22.1 %all-to-all-done.3 = bf16[16,416,128]{2,1,0:T(8,128)(2,1)S(1)} async-done(((bf16[16,416,128]{2,1,0:T(8,128)(2,1)}), bf16[16,416,128]{2,1,0:T(8,128)(2,1)S(1)}, u32[]{:S(2)}, u32[]{:S(2)}) %all-to-all-start.3) | async-done | bytes 1703968 | tf_op jit(solution)/shard_map/all_to_all | solution.py:183
  136.5 3.3 %requantize.1 = (bf16[1664,512]{1,0:T(8,128)(2,1)S(1)}, bf16[1664,512]{1,0:T(8,128)(2,1)S(1)}, f32[13,128]{1,0:T(8,128)S(1)}) custom-call(f32[13,4]{1,0:T(8,128)S(1)} %dynamic_slice.3.scale_ref, bf16[16,2,208,128]{3,2,1,0:T(8,128)(2,1)S(1)} %bitcast.15), custom_call_target="tpu_custom_call" | custom-call | tf_op jit(solution)/shard_map/requantize/pallas_call | solution.py:93
  139.8 0.0 copy-start.1
  139.8 1.2 copy-done.1
  141.0 3.9 %all-gather.2.cloned.1.call-done.refs_0_.refs_1_.refs_2_.refs_3_ = bf16[2048,1664]{1,0:T(8,128)(2,1)} async-done(((bf16[256,1664]{1,0:T(8,128)(2,1)}), bf16[2048,1664]{1,0:T(8,128)(2,1)}) %all-gather.2.cloned.1.call-update) | async-done | bytes 6815760 | tf_op jit(solution)/shard_map/all_gather | solution.py:178
  144.9 3.7 %half_product.3 = bf16[1024,512]{1,0:T(8,128)(2,1)S(1)} custom-call(s32[1]{0:T(128)S(6)} %sub.3.parity_ref, bf16[2048,1664]{1,0:T(8,128)(2,1)} %all-gather.2.cloned.1.call-done.refs_0_.refs_1_.refs_2_.refs_3_, bf16[2048,1664]{1,0:T(8,128)(2,1)} %all-gather.2.cloned.1.call-done.refs_0_.refs_1_.refs_2_.refs_3_, ...), custom_call_target="tpu_custom_call" | custom-call | flops 1744830464 | bytes 6160384 | tf_op jit(solution)/shard_map/half_product/pallas_call | solution.py:127
  148.6 2.6 %collective-permute-start = (bf16[1024,512]{1,0:T(8,128)(2,1)S(1)}, bf16[1024,512]{1,0:T(8,128)(2,1)S(1)}, u32[]{:S(2)}, u32[]{:S(2)}) collective-permute-start(bf16[1024,512]{1,0:T(8,128)(2,1)S(1)} %half_product.3), channel_id=1, source_target_pairs={{0,1},{1,0},{2,3},{3,2},{4,5},{5,4},{6,7},{7,6},{8,9},{9,8},{10,11... | collective-permute-start | bytes 3145736 | tf_op jit(solution)/shard_map/ppermute | solution.py:203
  151.2 3.7 %half_product.2 = bf16[1024,512]{1,0:T(8,128)(2,1)S(1)} custom-call(s32[1]{0:T(128)} %bitcast.parity_ref, bf16[2048,1664]{1,0:T(8,128)(2,1)} %all-gather.2.cloned.1.call-done.refs_0_.refs_1_.refs_2_.refs_3_, bf16[2048,1664]{1,0:T(8,128)(2,1)} %all-gather.2.cloned.1.call-done.refs_0_.refs_1_.refs_2_.refs_3_, ...), custom_call_target="tpu_custom_call" | custom-call | flops 1744830464 | bytes 6160384 | tf_op jit(solution)/shard_map/half_product/pallas_call | solution.py:127
  155.0 0.0 collective-permute-done
  155.0 1.3 add_convert_fusion
  156.3 5.0 %all-to-all-start.4 = ((bf16[8,128,512]{2,1,0:T(8,128)(2,1)}), bf16[8,128,512]{2,1,0:T(8,128)(2,1)S(1)}, u32[]{:S(2)}, u32[]{:S(2)}) async-start(bf16[8,128,512]{2,1,0:T(8,128)(2,1)} %bitcast.9), calls=%async_computation.4 | async-start | bytes 2097152 | tf_op jit(solution)/shard_map/all_to_all | solution.py:206
  161.3 2.3 %copy.11 = bf16[512,1664]{1,0:T(8,128)(2,1)} copy(bf16[512,1664]{0,1:T(8,128)(2,1)S(1)} %bitcast.16) | data formatting | bytes 3407872
  163.7 0.7 copy.12
  164.3 12.6 %all-to-all-done.4 = bf16[8,128,512]{2,1,0:T(8,128)(2,1)S(1)} async-done(((bf16[8,128,512]{2,1,0:T(8,128)(2,1)}), bf16[8,128,512]{2,1,0:T(8,128)(2,1)S(1)}, u32[]{:S(2)}, u32[]{:S(2)}) %all-to-all-start.4) | async-done | bytes 1048608 | tf_op jit(solution)/shard_map/all_to_all | solution.py:206
  176.9 0.8 reduce_sum.12
  (7 shorter events, 0.0 us)
Async XLA Ops:
  7.2 1.5 copy-start
  8.7 12.5 %copy-start.3 = (bf16[64,1664]{1,0:T(8,128)(2,1)S(1)}, bf16[64,1664]{1,0:T(8,128)(2,1)}, u32[]{:S(2)}) copy-start(bf16[64,1664]{1,0:T(8,128)(2,1)} %param.7) | copy-start | bytes 638980
  8.7 12.5 %copy-start.4 = (bf16[64,1664]{1,0:T(8,128)(2,1)S(1)}, bf16[64,1664]{1,0:T(8,128)(2,1)}, u32[]{:S(2)}) copy-start(bf16[64,1664]{1,0:T(8,128)(2,1)} %param.6) | copy-start | bytes 638980
  10.3 35.8 %all-to-all-start = ((bf16[32,104,128]{2,1,0:T(8,128)(2,1)}), bf16[32,104,128]{2,1,0:T(8,128)(2,1)S(1)}, u32[]{:S(2)}, u32[]{:S(2)}) async-start(bf16[32,104,128]{2,1,0:T(8,128)(2,1)} %get-tuple-element.12), calls=%async_computation | async-start | bytes 1703936 | tf_op jit(solution)/shard_map/all_to_all | solution.py:176
  21.1 123.8 %all-gather.2.cloned.1.call-start = ((), (), s32[]{:S(2)}) async-start(), calls=%async_computation.5 | async-start | bytes 7667712 | tf_op jit(solution)/shard_map/all_gather | solution.py:178
  75.2 29.9 %all-to-all-start.2 = ((bf16[32,104,128]{2,1,0:T(8,128)(2,1)}), bf16[32,104,128]{2,1,0:T(8,128)(2,1)S(1)}, u32[]{:S(2)}, u32[]{:S(2)}) async-start(bf16[32,104,128]{2,1,0:T(8,128)(2,1)} %get-tuple-element.17), calls=%async_computation.2 | async-start | bytes 1703936 | tf_op jit(solution)/shard_map/all_to_all | solution.py:181
  106.5 30.0 %all-to-all-start.3 = ((bf16[16,416,128]{2,1,0:T(8,128)(2,1)}), bf16[16,416,128]{2,1,0:T(8,128)(2,1)S(1)}, u32[]{:S(2)}, u32[]{:S(2)}) async-start(bf16[16,416,128]{2,1,0:T(8,128)(2,1)} %bitcast.7), calls=%async_computation.3 | async-start | bytes 3407872 | tf_op jit(solution)/shard_map/all_to_all | solution.py:183
  139.8 1.2 copy-start.1
  148.6 6.3 %collective-permute-start = (bf16[1024,512]{1,0:T(8,128)(2,1)S(1)}, bf16[1024,512]{1,0:T(8,128)(2,1)S(1)}, u32[]{:S(2)}, u32[]{:S(2)}) collective-permute-start(bf16[1024,512]{1,0:T(8,128)(2,1)S(1)} %half_product.3), channel_id=1, source_target_pairs={{0,1},{1,0},{2,3},{3,2},{4,5},{5,4},{6,7},{7,6},{8,9},{9,8},{10,11... | collective-permute-start | bytes 3145736 | tf_op jit(solution)/shard_map/ppermute | solution.py:203
  156.3 5.0 %copy-start.2 = (bf16[1664,512]{1,0:T(8,128)(2,1)S(1)}, bf16[1664,512]{1,0:T(8,128)(2,1)}, u32[]{:S(2)}) copy-start(bf16[1664,512]{1,0:T(8,128)(2,1)} %copy-done.1) | copy-start | bytes 5111812
  156.3 20.6 %all-to-all-start.4 = ((bf16[8,128,512]{2,1,0:T(8,128)(2,1)}), bf16[8,128,512]{2,1,0:T(8,128)(2,1)S(1)}, u32[]{:S(2)}, u32[]{:S(2)}) async-start(bf16[8,128,512]{2,1,0:T(8,128)(2,1)} %bitcast.9), calls=%async_computation.4 | async-start | bytes 2097152 | tf_op jit(solution)/shard_map/all_to_all | solution.py:206
Sparse Core Ops, SparseCore 0:
  46.3 98.5 all-gather.1
